TPU v7x, 32 devices: a whole 2x2x4 slice. The times are simulated.
32 devices in a mesh: row: 4 (over z), col: 8 (over y, x, core).
Axes of the slice: x: 2, y: 2, z: 4, core: 2. Of those that a mesh axis runs over, the one named last changes fastest.
Arguments:
- tokens: bfloat16 [16384, 2048], P('row', 'col'), may hold values from -8 to 8
- norm_gain: float32 [2048], P('col'), may hold values from 0.5 to 1.5
- norm_bias: float32 [2048], P('col'), may hold values from -3 to 3
- qkv_weight: bfloat16 [2048, 3, 2048], P('row', None, 'col'), may hold values from -0.125 to 0.125
- gate_up_weight: bfloat16 [2048, 2, 5632], P('row', None, 'col'), may hold values from -0.125 to 0.125
- out_weight: bfloat16 [2048, 2048], P('row', 'col'), may hold values from -1 to 1
- down_weight: bfloat16 [2048, 5632], P('row', 'col'), may hold values from -0.078125 to 0.078125
- image_start: int32 [16], P('row'), may hold values from 0 to 768
- doc_ids: int32 [16, 1024], P('row'), may hold values from 0 to 3, never falling along the last dimension, each value on 1 to 512 neighbouring positions
- out_grad: bfloat16 [16384, 2048], P('row', 'col'), may hold values from -8 to 8
Outputs:
- layer_out: bfloat16 [16384, 2048], P('row', 'col')
- input_grad: float32 [16384, 2048], P('row', 'col')
- norm_gain_grad: float32 [2048], P('col')
- norm_bias_grad: float32 [2048], P('col')
- qkv_weight_grad: float32 [2048, 3, 2048], P('row', None, 'col')
- gate_up_weight_grad: float32 [2048, 2, 5632], P('row', None, 'col')
- out_weight_grad: float32 [2048, 2048], P('row', 'col')
- down_weight_grad: float32 [2048, 5632], P('row', 'col')
Inputs may be any that keep to these rules, and one draw needn't show every extreme that they name: `image_start`: the image piece lies inside its sequence. `doc_ids`: never falls along a sequence; a document holds 1 to 512 tokens.
All inputs are finite; a program needn't handle non-finite values.
Results may differ from a plain program's by a relative error of at most 0.012.
Values may be sent and summed in bfloat16 or wider, within the bound.
A program may use at most 256 MiB of HBM per device.

v0:
```python
import jax
import jax.numpy as jnp
from jax import lax
from jax.sharding import PartitionSpec as P

D = 2048
HD = 64
ROT = 16
LEN = 1024
IMG = 256


NORM_EPS = 1e-05
MASKED_SCORE = -1e30
ROPE_BASE = 10000.0


def rotate(values):
    half_rot = ROT // 2
    places = jnp.arange(LEN).astype(jnp.float32)
    inv_freq = ROPE_BASE ** (-2.0 * jnp.arange(half_rot).astype(jnp.float32) / ROT)
    angles = places[:, None] * inv_freq[None, :]
    cosines = jnp.cos(angles)[:, None, :]
    sines = jnp.sin(angles)[:, None, :]
    first_half = values[..., :half_rot]
    second_half = values[..., half_rot:ROT]
    return jnp.concatenate(
        [
            first_half * cosines - second_half * sines,
            second_half * cosines + first_half * sines,
            values[..., ROT:],
        ],
        axis=-1,
    )


def allowed_pairs(doc_row, img_start):
    places = jnp.arange(LEN)
    causal = places[:, None] >= places[None, :]
    inside = (places >= img_start) & (places < img_start + IMG)
    same_doc = doc_row[:, None] == doc_row[None, :]
    return same_doc & (causal | inside[:, None] & inside[None, :])


def contract(left, right, left_dim, right_dim):
    return lax.dot_general(
        left, right, (((left_dim,), (right_dim,)), ((), ())), preferred_element_type=jnp.float32
    )


def masked_scores(queries, key_rows, img_start, doc_row):
    scores = jnp.einsum(
        "qhd,khd->hqk", queries, key_rows, preferred_element_type=jnp.float32
    ) * HD ** (-0.5)
    return jnp.where(allowed_pairs(doc_row, img_start)[None], scores, MASKED_SCORE)


def attend(items):
    queries, key_rows, value_rows, img_start, doc_row = items
    scores = masked_scores(queries, key_rows, img_start, doc_row)
    row_max = jnp.max(scores, axis=-1, keepdims=True)
    expo = jnp.exp(scores - row_max)
    row_total = jnp.sum(expo, axis=-1, keepdims=True)
    probs_low = (expo / row_total).astype(jnp.bfloat16)
    mixed_out = jnp.einsum(
        "hqk,khd->qhd", probs_low, value_rows, preferred_element_type=jnp.float32
    )
    return (mixed_out, (row_max + jnp.log(row_total))[..., 0])


def attend_back(items):
    queries, key_rows, value_rows, img_start, doc_row, log_total, grad_mixed = items
    scores = masked_scores(queries, key_rows, img_start, doc_row)
    attn_probs = jnp.exp(scores - log_total[..., None])
    probs_low = attn_probs.astype(jnp.bfloat16)
    grad_probs = jnp.einsum(
        "qhd,khd->hqk", grad_mixed, value_rows, preferred_element_type=jnp.float32
    )
    grad_values = jnp.einsum(
        "hqk,qhd->khd", probs_low, grad_mixed, preferred_element_type=jnp.float32
    )
    row_delta = jnp.sum(grad_probs * attn_probs, axis=-1, keepdims=True)
    grad_scores = (attn_probs * (grad_probs - row_delta)).astype(jnp.bfloat16)
    grad_queries = jnp.einsum(
        "hqk,khd->qhd", grad_scores, key_rows, preferred_element_type=jnp.float32
    ) * HD ** (-0.5)
    grad_keys = jnp.einsum(
        "hqk,qhd->khd", grad_scores, queries, preferred_element_type=jnp.float32
    ) * HD ** (-0.5)
    return (grad_queries, grad_keys, grad_values)


def local(
    tokens,
    norm_gain,
    norm_bias,
    qkv_weight,
    gate_up_weight,
    out_weight,
    down_weight,
    image_start,
    doc_ids,
    out_grad,
):
    block_rows = tokens.shape[0]
    local_width = tokens.shape[1]
    ffn_local = gate_up_weight.shape[2]
    local_heads = local_width // HD
    count = block_rows // LEN
    head_shape = (count, LEN, local_heads, HD)
    inputs = tokens.astype(jnp.float32)
    full_qkv, full_gate_up, full_out, full_down = (
        lax.all_gather(qkv_weight, "row", axis=0, tiled=True),
        lax.all_gather(gate_up_weight, "row", axis=0, tiled=True),
        lax.all_gather(out_weight, "row", axis=0, tiled=True),
        lax.all_gather(down_weight, "row", axis=0, tiled=True),
    )
    qkv_matrix = full_qkv.reshape(D, 3 * local_width)
    gate_up_matrix = full_gate_up.reshape(D, 2 * ffn_local)
    row_mean = lax.psum(jnp.sum(inputs, axis=1), "col") / D
    centered = inputs - row_mean[:, None]
    row_var = lax.psum(jnp.sum(centered * centered, axis=1), "col") / D
    inv_std = lax.rsqrt(row_var + NORM_EPS)
    unit_rows = centered * inv_std[:, None]
    normed = (unit_rows * norm_gain + norm_bias).astype(jnp.bfloat16)
    normed_full = lax.all_gather(normed, "col", axis=1, tiled=True)
    projected = jnp.dot(normed_full, qkv_matrix, preferred_element_type=jnp.float32)
    query_raw = projected[:, :local_width].reshape(head_shape)
    key_raw = projected[:, local_width : 2 * local_width].reshape(head_shape)
    queries = rotate(query_raw).astype(jnp.bfloat16)
    key_rows = rotate(key_raw).astype(jnp.bfloat16)
    value_rows = projected[:, 2 * local_width :].reshape(head_shape).astype(jnp.bfloat16)
    attended, log_totals = lax.map(attend, (queries, key_rows, value_rows, image_start, doc_ids))
    attended = attended.reshape(block_rows, local_width).astype(jnp.bfloat16)
    gate_up = jnp.dot(normed_full, gate_up_matrix, preferred_element_type=jnp.float32)
    gate_pre = gate_up[:, :ffn_local]
    up_pre = gate_up[:, ffn_local:]
    silu_gate = jax.nn.silu(gate_pre)
    hidden = (silu_gate * up_pre).astype(jnp.bfloat16)
    attn_branch = contract(attended, full_out, 1, 1)
    ffn_branch = contract(hidden, full_down, 1, 1)
    attn_sum = lax.psum_scatter(attn_branch, "col", scatter_dimension=1, tiled=True)
    ffn_sum = lax.psum_scatter(
        ffn_branch.astype(jnp.bfloat16), "col", scatter_dimension=1, tiled=True
    ).astype(jnp.float32)
    outputs = inputs + attn_sum + ffn_sum
    grad_full = lax.all_gather(out_grad, "col", axis=1, tiled=True)
    out_weight_grad = contract(grad_full, attended, 0, 0)
    down_weight_grad = contract(grad_full, hidden, 0, 0)
    grad_attended = jnp.dot(grad_full, full_out, preferred_element_type=jnp.float32).astype(
        jnp.bfloat16
    )
    grad_hidden = jnp.dot(grad_full, full_down, preferred_element_type=jnp.float32)
    sigma = jax.nn.sigmoid(gate_pre)
    grad_gate = (grad_hidden * up_pre * (sigma + gate_pre * sigma * (1.0 - sigma))).astype(
        jnp.bfloat16
    )
    grad_up = (grad_hidden * silu_gate).astype(jnp.bfloat16)
    grad_queries, grad_keys, grad_values = lax.map(
        attend_back,
        (
            queries,
            key_rows,
            value_rows,
            image_start,
            doc_ids,
            log_totals,
            grad_attended.reshape(head_shape),
        ),
    )
    rotate_back = jax.vjp(rotate, query_raw)[1]
    grad_query_raw = rotate_back(grad_queries)[0]
    grad_key_raw = rotate_back(grad_keys)[0]
    grad_projected = jnp.concatenate(
        [
            grad_query_raw.reshape(block_rows, local_width),
            grad_key_raw.reshape(block_rows, local_width),
            grad_values.reshape(block_rows, local_width),
        ],
        axis=1,
    ).astype(jnp.bfloat16)
    grad_gate_up = jnp.concatenate([grad_gate, grad_up], axis=1)
    qkv_grad = contract(normed_full, grad_projected, 0, 0).reshape(D, 3, local_width)
    gate_up_grad = contract(normed_full, grad_gate_up, 0, 0).reshape(D, 2, ffn_local)
    qkv_sum, gate_up_sum, out_sum, down_sum = (
        lax.psum_scatter(
            qkv_grad.astype(jnp.bfloat16), "row", scatter_dimension=0, tiled=True
        ).astype(jnp.float32),
        lax.psum_scatter(
            gate_up_grad.astype(jnp.bfloat16), "row", scatter_dimension=0, tiled=True
        ).astype(jnp.float32),
        lax.psum_scatter(
            out_weight_grad.astype(jnp.bfloat16), "row", scatter_dimension=0, tiled=True
        ).astype(jnp.float32),
        lax.psum_scatter(
            down_weight_grad.astype(jnp.bfloat16), "row", scatter_dimension=0, tiled=True
        ).astype(jnp.float32),
    )
    normed_partial = contract(grad_projected, qkv_matrix, 1, 1) + contract(
        grad_gate_up, gate_up_matrix, 1, 1
    )
    grad_normed = lax.psum_scatter(
        normed_partial.astype(jnp.bfloat16), "col", scatter_dimension=1, tiled=True
    ).astype(jnp.float32)
    scaled_grad = grad_normed * norm_gain
    grad_sum, cross_sum = (
        lax.psum(jnp.sum(scaled_grad, axis=1).astype(jnp.bfloat16), "col").astype(jnp.float32),
        lax.psum(jnp.sum(scaled_grad * unit_rows, axis=1).astype(jnp.bfloat16), "col").astype(
            jnp.float32
        ),
    )
    input_grad = out_grad.astype(jnp.float32) + inv_std[:, None] * (
        scaled_grad - grad_sum[:, None] / D - unit_rows * (cross_sum[:, None] / D)
    )
    gain_grad, bias_grad = lax.psum(
        (jnp.sum(grad_normed * unit_rows, axis=0), jnp.sum(grad_normed, axis=0)), "row"
    )
    return (
        outputs.astype(jnp.bfloat16),
        input_grad,
        gain_grad,
        bias_grad,
        qkv_sum,
        gate_up_sum,
        out_sum,
        down_sum,
    )


def solution(mesh):
    placed = (
        P("row", "col"),
        P("col"),
        P("col"),
        P("row", None, "col"),
        P("row", None, "col"),
        P("row", "col"),
        P("row", "col"),
        P("row"),
        P("row", None),
        P("row", "col"),
    )
    return jax.shard_map(
        local,
        mesh=mesh,
        in_specs=placed,
        out_specs=(
            P("row", "col"),
            P("row", "col"),
            P("col"),
            P("col"),
            P("row", None, "col"),
            P("row", None, "col"),
            P("row", "col"),
            P("row", "col"),
        ),
        check_vma=False,
    )
```

profile of v0, /device:TPU:0, one launch (start us, length us, event | category | flops | bytes accessed | tf_op | source)
XLA Modules:
  0.0 1553.2 jit_solution(7412619552443875088)
XLA Ops:
  12.0 26.3 %psum.42 = f32[4096]{0:T(1024)S(1)} all-reduce(f32[4096]{0:T(1024)S(1)} %convert_reduce_fusion.1), channel_id=1, replica_groups=mesh['row'=4,'col'=8] {'col'}, use_global_device_ids=true, to_apply=%region_1.0 | all-reduce | flops 4096 | bytes 32768 | tf_op jit(solution)/shard_map/psum | solution.py:120
  39.6 23.9 %psum.43 = f32[4096]{0:T(1024)S(1)} all-reduce(f32[4096]{0:T(1024)S(1)} %fusion.64), channel_id=1, replica_groups=mesh['row'=4,'col'=8] {'col'}, use_global_device_ids=true, to_apply=%region_3.0 | all-reduce | flops 4096 | bytes 32768 | tf_op jit(solution)/shard_map/psum | solution.py:122
  76.4 94.3 %all-gather.7.cloned.1.call-done = bf16[4096,2048]{1,0:T(8,128)(2,1)} async-done(((bf16[4096,256]{1,0:T(8,128)(2,1)}), bf16[4096,2048]{1,0:T(8,128)(2,1)}) %all-gather.7.cloned.1.call-update) | async-done | bytes 16777232 | tf_op jit(solution)/shard_map/all_gather | solution.py:126
  170.7 17.9 %fusion.74 = f32[4096,768]{1,0:T(8,128)S(1)} fusion(bf16[4096,2048]{1,0:T(8,128)(2,1)} %all-gather.7.cloned.1.call-done, bf16[2048,768]{0,1:T(8,128)(2,1)} %bitcast.178), kind=kOutput, calls=%fused_computation.133 | convolution fusion | flops 12884901888 | bytes 32505856 | tf_op jit(solution)/shard_map/dot_general | solution.py:127
  200.2 94.4 %all-gather.17.cloned.1.call-done = bf16[4096,2048]{1,0:T(8,128)(2,1)} async-done(((bf16[4096,256]{1,0:T(8,128)(2,1)}), bf16[4096,2048]{1,0:T(8,128)(2,1)}) %all-gather.17.cloned.1.call-update) | async-done | bytes 16777232 | tf_op jit(solution)/shard_map/all_gather | solution.py:147
  294.6 11.9 convolution_convert_fusion.2
  370.4 71.4 %while.26 = (s32[]{:T(128)}, bf16[4,1024,4,64]{1,3,2,0:T(8,128)(2,1)S(1)}, f32[4,4,1024]{2,1,0:T(4,128)S(1)}, bf16[4,1024,4,64]{1,3,2,0:T(8,128)(2,1)}, s32[4,10...) while((s32[]{:T(128)}, ...), condition=%wide.region_7.8_spmd, body=%wide.region_4.7_spmd.sunk | while | flops 1129315328 | bytes 57294996 | solution.py:133
  443.8 318.4 %while.27 = (s32[]{:T(128)}, f32[4,1024,4,64]{1,0,3,2:T(4,128)}, f32[4,1024,4,64]{1,0,3,2:T(4,128)}, bf16[4,1024,4,64]{1,3,2,0:T(8,128)(2,1)}, bf16[4,1024,4,64]...) while((s32[]{:T(128)}, f32[4,1024,4,64]{1,0,3,2:T(4,128)}, ...), condition=%wide.region_12.13_spmd, body=%wide.region_10.12_spmd.sunk | while | flops 2727869440 | bytes 143230144 | solution.py:159
  457.9 9.4 multiply_reduce_fusion.2
  483.6 19.9 %dynamic_update_slice.29 = f32[4,1024,4,64]{1,0,3,2:T(4,128)} dynamic-update-slice(f32[4,1024,4,64]{1,0,3,2:T(4,128)} %get-tuple-element.412, f32[1,1024,4,64]{1,0,3,2:T(1,128)S(1)} %copy.90, s32[]{:T(128)S(6)} %copy.109, s32[]{:T(128)} %constant.68.clone.1..sunk, s32[]{:T(128)} %constant.68.clone.1..sunk, s32[]{:T(128)} %constant.68.clone.1..sunk) | dynamic-update-slice | bytes 2097156 | tf_op jit(solution)/shard_map/while/body/jit(dynamic_update_index_in_dim)/dynamic_update_slice | solution.py:133
  503.6 19.9 %dynamic_update_slice.28 = f32[4,1024,4,64]{1,0,3,2:T(4,128)} dynamic-update-slice(f32[4,1024,4,64]{1,0,3,2:T(4,128)} %get-tuple-element.411, f32[1,1024,4,64]{1,0,3,2:T(1,128)S(1)} %copy.89, s32[]{:T(128)S(6)} %copy.109, s32[]{:T(128)} %constant.68.clone.1..sunk, s32[]{:T(128)} %constant.68.clone.1..sunk, s32[]{:T(128)} %constant.68.clone.1..sunk) | dynamic-update-slice | bytes 2097156 | tf_op jit(solution)/shard_map/while/body/jit(dynamic_update_index_in_dim)/dynamic_update_slice | solution.py:133
  563.2 19.9 %dynamic_update_slice.29 = f32[4,1024,4,64]{1,0,3,2:T(4,128)} dynamic-update-slice(f32[4,1024,4,64]{1,0,3,2:T(4,128)} %get-tuple-element.412, f32[1,1024,4,64]{1,0,3,2:T(1,128)S(1)} %copy.90, s32[]{:T(128)S(6)} %copy.109, s32[]{:T(128)} %constant.68.clone.1..sunk, s32[]{:T(128)} %constant.68.clone.1..sunk, s32[]{:T(128)} %constant.68.clone.1..sunk) | dynamic-update-slice | bytes 2097156 | tf_op jit(solution)/shard_map/while/body/jit(dynamic_update_index_in_dim)/dynamic_update_slice | solution.py:133
  583.1 19.9 %dynamic_update_slice.28 = f32[4,1024,4,64]{1,0,3,2:T(4,128)} dynamic-update-slice(f32[4,1024,4,64]{1,0,3,2:T(4,128)} %get-tuple-element.411, f32[1,1024,4,64]{1,0,3,2:T(1,128)S(1)} %copy.89, s32[]{:T(128)S(6)} %copy.109, s32[]{:T(128)} %constant.68.clone.1..sunk, s32[]{:T(128)} %constant.68.clone.1..sunk, s32[]{:T(128)} %constant.68.clone.1..sunk) | dynamic-update-slice | bytes 2097156 | tf_op jit(solution)/shard_map/while/body/jit(dynamic_update_index_in_dim)/dynamic_update_slice | solution.py:133
  642.7 19.9 %dynamic_update_slice.29 = f32[4,1024,4,64]{1,0,3,2:T(4,128)} dynamic-update-slice(f32[4,1024,4,64]{1,0,3,2:T(4,128)} %get-tuple-element.412, f32[1,1024,4,64]{1,0,3,2:T(1,128)S(1)} %copy.90, s32[]{:T(128)S(6)} %copy.109, s32[]{:T(128)} %constant.68.clone.1..sunk, s32[]{:T(128)} %constant.68.clone.1..sunk, s32[]{:T(128)} %constant.68.clone.1..sunk) | dynamic-update-slice | bytes 2097156 | tf_op jit(solution)/shard_map/while/body/jit(dynamic_update_index_in_dim)/dynamic_update_slice | solution.py:133
  662.6 19.9 %dynamic_update_slice.28 = f32[4,1024,4,64]{1,0,3,2:T(4,128)} dynamic-update-slice(f32[4,1024,4,64]{1,0,3,2:T(4,128)} %get-tuple-element.411, f32[1,1024,4,64]{1,0,3,2:T(1,128)S(1)} %copy.89, s32[]{:T(128)S(6)} %copy.109, s32[]{:T(128)} %constant.68.clone.1..sunk, s32[]{:T(128)} %constant.68.clone.1..sunk, s32[]{:T(128)} %constant.68.clone.1..sunk) | dynamic-update-slice | bytes 2097156 | tf_op jit(solution)/shard_map/while/body/jit(dynamic_update_index_in_dim)/dynamic_update_slice | solution.py:133
  722.2 19.9 %dynamic_update_slice.29 = f32[4,1024,4,64]{1,0,3,2:T(4,128)} dynamic-update-slice(f32[4,1024,4,64]{1,0,3,2:T(4,128)} %get-tuple-element.412, f32[1,1024,4,64]{1,0,3,2:T(1,128)S(1)} %copy.90, s32[]{:T(128)S(6)} %copy.109, s32[]{:T(128)} %constant.68.clone.1..sunk, s32[]{:T(128)} %constant.68.clone.1..sunk, s32[]{:T(128)} %constant.68.clone.1..sunk) | dynamic-update-slice | bytes 2097156 | tf_op jit(solution)/shard_map/while/body/jit(dynamic_update_index_in_dim)/dynamic_update_slice | solution.py:133
  742.1 19.9 %dynamic_update_slice.28 = f32[4,1024,4,64]{1,0,3,2:T(4,128)} dynamic-update-slice(f32[4,1024,4,64]{1,0,3,2:T(4,128)} %get-tuple-element.411, f32[1,1024,4,64]{1,0,3,2:T(1,128)S(1)} %copy.89, s32[]{:T(128)S(6)} %copy.109, s32[]{:T(128)} %constant.68.clone.1..sunk, s32[]{:T(128)} %constant.68.clone.1..sunk, s32[]{:T(128)} %constant.68.clone.1..sunk) | dynamic-update-slice | bytes 2097156 | tf_op jit(solution)/shard_map/while/body/jit(dynamic_update_index_in_dim)/dynamic_update_slice | solution.py:133
  777.0 31.1 %fusion.76 = f32[4096,1408]{0,1:T(8,128)} fusion(bf16[4096,2048]{1,0:T(8,128)(2,1)} %all-gather.7.cloned.1.call-done, bf16[2048,1408]{0,1:T(8,128)(2,1)} %bitcast.176), kind=kOutput, calls=%fused_computation.135 | convolution fusion | flops 23622320128 | bytes 45613056 | tf_op jit(solution)/shard_map/dot_general | solution.py:135
  808.1 28.1 %multiply_convert_fusion.2 = (bf16[4096,704]{0,1:T(8,128)(2,1)}, bf16[4096,704]{0,1:T(8,128)(2,1)}, bf16[4096,704]{0,1:T(8,128)(2,1)}) fusion(f32[4096,1408]{0,1:T(8,128)} %fusion.76, bf16[4096,2048]{1,0:T(8,128)(2,1)} %all-gather.17.cloned.1.call-done, bf16[2048,704]{0,1:T(8,128)(2,1)} %all-gather.15.cloned.1.call-done), kind=kOutput, calls=%fused_computation.70 | convolution fusion | flops 11851530240 | bytes 60030976 | tf_op jit(solution)/shard_map/dot_general | solution.py:153
  836.2 18.7 %fusion.69 = bf16[2048,704]{0,1:T(8,128)(2,1)} fusion(bf16[4096,704]{0,1:T(8,128)(2,1)} %get-tuple-element.221, bf16[4096,2048]{1,0:T(8,128)(2,1)} %all-gather.17.cloned.1.call-done), kind=kOutput, calls=%fused_computation.106 | convolution fusion | flops 11812601856 | bytes 25427968 | tf_op jit(solution)/shard_map/dot_general | solution.py:46
  873.5 19.1 %convolution_convert_fusion.3 = bf16[2048,768]{0,1:T(8,128)(2,1)S(1)} fusion(bf16[4096,768]{0,1:T(8,128)(2,1)S(1)} %constant_dynamic-update-slice_fusion, bf16[4096,2048]{1,0:T(8,128)(2,1)} %all-gather.7.cloned.1.call-done), kind=kOutput, calls=%fused_computation.102 | convolution fusion | flops 12886474752 | bytes 26214400 | tf_op jit(solution)/shard_map/dot_general | solution.py:46
  895.5 31.7 %convolution_convert_fusion.1 = bf16[2048,1408]{0,1:T(8,128)(2,1)} fusion(bf16[4096,2048]{1,0:T(8,128)(2,1)} %all-gather.7.cloned.1.call-done, bf16[4096,704]{0,1:T(8,128)(2,1)} %get-tuple-element.220, bf16[4096,704]{0,1:T(8,128)(2,1)} %get-tuple-element.219), kind=kOutput, calls=%fused_computation.74 | convolution fusion | flops 23648272384 | bytes 34078720 | tf_op jit(solution)/shard_map/dot_general | solution.py:46
  929.7 20.0 %fusion.77 = f32[4096,2048]{1,0:T(8,128)} fusion(bf16[4096,768]{0,1:T(8,128)(2,1)} %copy-done.10, bf16[2048,768]{0,1:T(8,128)(2,1)S(1)} %bitcast.179), kind=kOutput, calls=%fused_computation.136 | convolution fusion | flops 12884901888 | bytes 42991616 | tf_op jit(solution)/shard_map/dot_general | solution.py:46
  949.7 35.2 %add_convert_fusion = bf16[4096,2048]{1,0:T(8,128)(2,1)} fusion(f32[4096,2048]{1,0:T(8,128)} %fusion.77, bf16[2048,1408]{0,1:T(8,128)(2,1)} %bitcast.177, bf16[4096,704]{0,1:T(8,128)(2,1)} %get-tuple-element.220, bf16[4096,704]{0,1:T(8,128)(2,1)} %get-tuple-element.219), kind=kOutput, calls=%fused_computation.66 | convolution fusion | flops 23662166016 | bytes 67633152 | tf_op jit(solution)/shard_map/dot_general | solution.py:46
  986.7 19.0 %convolution_convert_fusion = bf16[4096,2048]{1,0:T(8,128)(2,1)} fusion(bf16[4096,704]{0,1:T(8,128)(2,1)} %get-tuple-element.221, bf16[2048,704]{0,1:T(8,128)(2,1)S(1)} %copy-done.24), kind=kOutput, calls=%fused_computation.67 | convolution fusion | flops 11819548672 | bytes 25427968 | tf_op jit(solution)/shard_map/dot_general | solution.py:46
  1007.5 13.3 fusion.75
  1027.8 59.5 %reduce-scatter.16.cloned.1.call-done = bf16[512,2,704]{0,2,1:T(8,128)(2,1)} async-done(((bf16[2048,2,704]{0,2,1:T(8,128)(2,1)}), bf16[512,2,704]{0,2,1:T(8,128)(2,1)}) %reduce-scatter.16.cloned.1.call-update) | async-done | bytes 1441808 | tf_op jit(solution)/shard_map/reduce_scatter | solution.py:189
  1090.6 117.2 %reduce-scatter.12.cloned.1.call-done = bf16[4096,256]{1,0:T(8,128)(2,1)} async-done(((bf16[4096,2048]{1,0:T(8,128)(2,1)}), bf16[4096,256]{1,0:T(8,128)(2,1)}) %reduce-scatter.12.cloned.1.call-update) | async-done | bytes 2097168 | tf_op jit(solution)/shard_map/reduce_scatter | solution.py:202
  1212.0 12.2 all-reduce.6
  1224.3 22.3 %all-reduce.7 = (bf16[4096]{0:T(1024)(128)(2,1)S(1)}, bf16[4096]{0:T(1024)(128)(2,1)S(1)}) all-reduce(bf16[4096]{0:T(1024)(128)(2,1)S(1)} %get-tuple-element.170, bf16[4096]{0:T(1024)(128)(2,1)S(1)} %get-tuple-element.171), channel_id=1, replica_groups=mesh['row'=4,'col'=8] {'col'}, use_global_device_ids=true, to_apply=%region_17.18 | all-reduce | flops 8192 | bytes 32768 | tf_op jit(solution)/shard_map/psum | solution.py:208
  1246.6 81.0 %reduce-scatter.10.cloned.1.call-done = bf16[4096,256]{1,0:T(8,128)(2,1)} async-done(((bf16[4096,2048]{1,0:T(8,128)(2,1)}), bf16[4096,256]{1,0:T(8,128)(2,1)}) %reduce-scatter.10.cloned.1.call-update) | async-done | bytes 2097168 | tf_op jit(solution)/shard_map/reduce_scatter | solution.py:143
  1327.6 209.3 %reduce-scatter.8.cloned.1.call-done = f32[4096,256]{1,0:T(8,128)} async-done(((f32[4096,2048]{1,0:T(8,128)}), f32[4096,256]{1,0:T(8,128)}) %reduce-scatter.8.cloned.1.call-update) | async-done | bytes 4194320 | tf_op jit(solution)/shard_map/reduce_scatter | solution.py:142
  (222 shorter events, 377.2 us)
Async XLA Ops:
  7.2 31.1 %copy-start = (bf16[4096,256]{1,0:T(8,128)(2,1)S(1)}, bf16[4096,256]{1,0:T(8,128)(2,1)}, u32[]{:S(2)}) copy-start(bf16[4096,256]{1,0:T(8,128)(2,1)} %param.14) | copy-start | bytes 6291460
  7.2 56.9 %copy-start.20 = (f32[256]{0:T(256)S(1)}, f32[256]{0:T(256)}, u32[]{:S(2)}) copy-start(f32[256]{0:T(256)} %param.15) | copy-start | bytes 3076
  7.2 56.9 %copy-start.22 = (f32[256]{0:T(256)S(1)}, f32[256]{0:T(256)}, u32[]{:S(2)}) copy-start(f32[256]{0:T(256)} %param.16) | copy-start | bytes 3076
  7.2 69.2 %all-gather.9.cloned.1.call-start = ((), (), s32[]{:S(2)}) async-start(), calls=%async_computation.8 | async-start | bytes 3932160 | tf_op jit(solution)/shard_map/all_gather | solution.py:113
  9.7 161.0 %all-gather.7.cloned.1.call-start = ((), (), s32[]{:S(2)}) async-start(), calls=%async_computation.7 | async-start | bytes 18874368 | tf_op jit(solution)/shard_map/all_gather | solution.py:126
  38.3 29.0 %copy-start.11 = (f32[4096]{0:T(1024)}, f32[4096]{0:T(1024)S(1)}, u32[]{:S(2)}) copy-start(f32[4096]{0:T(1024)S(1)} %broadcast_multiply_fusion) | copy-start | bytes 49156
  67.3 132.9 %all-gather.11.cloned.1.call-start = ((), (), s32[]{:S(2)}) async-start(), calls=%async_computation.9 | async-start | bytes 1310720 | tf_op jit(solution)/shard_map/all_gather | solution.py:115
  68.1 226.5 %all-gather.17.cloned.1.call-start = ((), (), s32[]{:S(2)}) async-start(), calls=%async_computation.14 | async-start | bytes 18874368 | tf_op jit(solution)/shard_map/all_gather | solution.py:147
  68.7 708.4 %all-gather.13.cloned.1.call-start = ((), (), s32[]{:S(2)}) async-start(), calls=%async_computation.11 | async-start | bytes 7208960 | tf_op jit(solution)/shard_map/all_gather | solution.py:114
  69.2 738.9 %all-gather.15.cloned.1.call-start = ((), (), s32[]{:S(2)}) async-start(), calls=%async_computation.12 | async-start | bytes 3604480 | tf_op jit(solution)/shard_map/all_gather | solution.py:116
  69.8 951.0 %reduce-scatter.18.cloned.1.call-start = ((), (), s32[]{:S(2)}) async-start(), calls=%async_computation.18 | async-start | bytes 1310720 | tf_op jit(solution)/shard_map/reduce_scatter | solution.py:192
  70.1 291.1 %copy-start.13 = (f32[1024,8]{0,1:T(8,128)}, f32[1024,8]{0,1:T(8,128)S(1)}, u32[]{:S(2)}) copy-start(f32[1024,8]{0,1:T(8,128)S(1)} %get-tuple-element.238) | copy-start | bytes 98308
  70.1 291.1 %copy-start.15 = (f32[1024,8]{0,1:T(8,128)}, f32[1024,8]{0,1:T(8,128)S(1)}, u32[]{:S(2)}) copy-start(f32[1024,8]{0,1:T(8,128)S(1)} %get-tuple-element.239) | copy-start | bytes 98308
  358.5 4.9 copy-start.5
  368.2 2.2 copy-start.19
  368.2 2.2 copy-start.25
  441.8 2.0 copy-start.4
  777.0 245.8 %reduce-scatter.20.cloned.1.call-start = ((), (), s32[]{:S(2)}) async-start(), calls=%async_computation.19 | async-start | bytes 3604480 | tf_op jit(solution)/shard_map/reduce_scatter | solution.py:195
  854.9 4.4 copy-start.6
  863.2 162.1 %reduce-scatter.14.cloned.1.call-start = ((), (), s32[]{:S(2)}) async-start(), calls=%async_computation.16 | async-start | bytes 3932160 | tf_op jit(solution)/shard_map/reduce_scatter | solution.py:186
  863.2 3.0 copy-start.7
  863.3 3.0 copy-start.8
  873.5 19.2 %copy-start.10 = (bf16[4096,768]{0,1:T(8,128)(2,1)}, bf16[4096,768]{0,1:T(8,128)(2,1)S(1)}, u32[]{:S(2)}) copy-start(bf16[4096,768]{0,1:T(8,128)(2,1)S(1)} %constant_dynamic-update-slice_fusion) | copy-start | bytes 18874372
  895.5 191.7 %reduce-scatter.16.cloned.1.call-start = ((), (), s32[]{:S(2)}) async-start(), calls=%async_computation.17 | async-start | bytes 7208960 | tf_op jit(solution)/shard_map/reduce_scatter | solution.py:189
  927.2 2.5 copy-start.23
  927.3 280.5 %reduce-scatter.12.cloned.1.call-start = ((), (), s32[]{:S(2)}) async-start(), calls=%async_computation.15 | async-start | bytes 18874368 | tf_op jit(solution)/shard_map/reduce_scatter | solution.py:202
  984.9 342.7 %reduce-scatter.10.cloned.1.call-start = ((), (), s32[]{:S(2)}) async-start(), calls=%async_computation.13 | async-start | bytes 18874368 | tf_op jit(solution)/shard_map/reduce_scatter | solution.py:143
  1005.7 531.1 %reduce-scatter.8.cloned.1.call-start = ((), (), s32[]{:S(2)}) async-start(), calls=%async_computation.10 | async-start | bytes 37748736 | tf_op jit(solution)/shard_map/reduce_scatter | solution.py:142
  1022.8 185.0 %copy-start.1 = (bf16[4096,256]{1,0:T(8,128)(2,1)S(1)}, bf16[4096,256]{1,0:T(8,128)(2,1)}, u32[]{:S(2)}) copy-start(bf16[4096,256]{1,0:T(8,128)(2,1)} %param.14) | copy-start | bytes 6291460
  1022.8 185.0 %copy-start.12 = (f32[4096]{0:T(1024)S(1)}, f32[4096]{0:T(1024)}, u32[]{:S(2)}) copy-start(f32[4096]{0:T(1024)} %copy-done.11) | copy-start | bytes 49156
  1022.8 185.0 %copy-start.18 = (f32[4096]{0:T(1024)S(1)}, f32[4096]{0:T(1024)}, u32[]{:S(2)}) copy-start(f32[4096]{0:T(1024)} %copy-done.17) | copy-start | bytes 49156
  1022.8 185.0 %copy-start.21 = (f32[256]{0:T(256)S(1)}, f32[256]{0:T(256)}, u32[]{:S(2)}) copy-start(f32[256]{0:T(256)} %param.15) | copy-start | bytes 3076
  (7 other events, 8.7 us)
Sparse Core Ops, SparseCore 0:
  10.2 66.1 all-gather.8
  78.8 91.7 all-gather.6
  172.2 27.9 all-gather.10
  201.9 92.5 all-gather.16
  296.0 106.6 all-gather.12
  404.2 57.3 all-gather.14
  777.1 27.1 reduce-scatter.17
  863.3 56.1 reduce-scatter.19
  922.5 60.1 reduce-scatter.13
  984.9 102.2 reduce-scatter.15
  1091.2 116.4 reduce-scatter.11
  1211.6 115.9 reduce-scatter.9
  1331.6 205.2 reduce-scatter.7
where the time goes:
time: 1560 us; the launch traced here: 1550 us
  waiting for transfers between devices  672 us (43%)
  matrix products  401 us (26%)
  local copies, waits for them, and re-layouts  268 us (17%)
  other arithmetic  106 us (7%)
  blocking collectives  84.8 us (5%)
    reduce_scatter x1, waiting for transfers between devices, local(): lax.psum_scatter(attn_branch, 'col', scatter_dimension=1, tiled=True)  209 us
    dynamic_update_slice x16, local copies, waits for them, and re-layouts, local(): lax.map(attend, (queries, key_rows, value_rows, image_start, doc_ids))  168 us
    dot_general x8, matrix products, contract(): lax.dot_general(left, right, (((left_dim,), (right_dim,)), ((), ())), pre...  166 us
    reduce_scatter x1, waiting for transfers between devices, local(): lax.psum_scatter(normed_partial.astype(jnp.bfloat16), 'col', scatter_dime...  117 us
    all_gather x1, waiting for transfers between devices, local(): grad_full = lax.all_gather(out_grad, 'col', axis=1, tiled=True)  94.4 us
    all_gather x1, waiting for transfers between devices, local(): normed_full = lax.all_gather(normed, 'col', axis=1, tiled=True)  94.3 us
    reduce_scatter x1, waiting for transfers between devices, local(): lax.psum_scatter(ffn_branch.astype(jnp.bfloat16), 'col', scatter_dimensio...  81 us
    reduce_scatter x1, waiting for transfers between devices, local(): lax.psum_scatter(gate_up_grad.astype(jnp.bfloat16), 'row', scatter_dimens...  59.5 us
  transfers between devices with their start and end apart: 13, of which 8 were waited for; matrix products, arithmetic and copies ran while one was open for 49% of the time, Pallas kernels for 0%

commit v1 on v0

v1 whole, which is shorter than its diff:
```python
import functools

import jax
import jax.numpy as jnp
from jax import lax
from jax.experimental import pallas as pl
from jax.experimental.pallas import tpu as pltpu
from jax.sharding import PartitionSpec as P

D = 2048
HD = 64
ROT = 16
LEN = 1024
IMG = 256
QB = 256
MB = 512


NORM_EPS = 1e-05
MESH = pl.DeviceIdType.MESH
MASKED_SCORE = -1e30
ROPE_BASE = 10000.0


def contract(left, right, left_dim, right_dim):
    return lax.dot_general(
        left, right, (((left_dim,), (right_dim,)), ((), ())), preferred_element_type=jnp.float32
    )


def rope_tables(width):
    half = ROT // 2
    places = jnp.arange(LEN).astype(jnp.float32)
    inv_freq = ROPE_BASE ** (-2.0 * jnp.arange(half).astype(jnp.float32) / ROT)
    angles = places[:, None] * inv_freq[None, :]
    cosines, sines = jnp.cos(angles), jnp.sin(angles)
    rest = HD - ROT
    c = jnp.concatenate([cosines, cosines, jnp.ones((LEN, rest), jnp.float32)], axis=1)
    a = jnp.concatenate([-sines, jnp.zeros((LEN, HD - half), jnp.float32)], axis=1)
    b = jnp.concatenate(
        [jnp.zeros((LEN, half), jnp.float32), sines, jnp.zeros((LEN, rest), jnp.float32)], axis=1
    )
    heads = width // HD
    return tuple(jnp.tile(t, (1, heads)) for t in (c, a, b))


def spans(doc_ids, image_start):
    places = jnp.arange(LEN, dtype=jnp.int32)
    first = jnp.sum(doc_ids[:, None, :] < doc_ids[:, :, None], axis=2, dtype=jnp.int32)
    last = jnp.sum(doc_ids[:, None, :] <= doc_ids[:, :, None], axis=2, dtype=jnp.int32) - 1
    start = image_start[:, None]
    inside = (places[None] >= start) & (places[None] < start + IMG)
    final = jnp.where(inside, jnp.minimum(last, start + IMG - 1), places[None])
    return first, final


def attention_kernel(
    heads,
    low_ref,
    high_ref,
    x_ref,
    g_ref,
    w_ref,
    first_ref,
    final_ref,
    c_ref,
    a_ref,
    b_ref,
    att_ref,
    gp_ref,
    ga_scr,
    q_scr,
    k_scr,
    v_scr,
    qt_scr,
    gt_scr,
    ks_scr,
    vs_scr,
    s_scr,
    d_scr,
    p_scr,
    ds_scr,
    bias_scr,
    m_scr,
    l_scr,
    e_scr,
    o_scr,
    dq_scr,
    dkt_scr,
    dvt_scr,
):
    f32, bf16 = jnp.float32, jnp.bfloat16
    width = heads * HD
    blocks = LEN // QB
    seq = pl.program_id(0)
    nt = (((1,), (1,)), ((), ()))
    lane = lax.broadcasted_iota(jnp.int32, (1, width), 1) // HD

    def turn(x, sl, sign):
        left = pltpu.roll(x, width - ROT // 2, 1)
        right = pltpu.roll(x, ROT // 2, 1)
        return x * c_ref[sl, :] + (left * a_ref[sl, :] + right * b_ref[sl, :]) * sign

    for i in range(blocks):
        sl = pl.ds(i * QB, QB)
        x = x_ref[sl, :]
        q, k, v = (
            jnp.dot(x, w_ref[:, kind * width : (kind + 1) * width], preferred_element_type=f32)
            for kind in range(3)
        )
        g = jnp.dot(g_ref[sl, :], w_ref[:, 3 * width :], preferred_element_type=f32)
        ga_scr[sl, :] = g.astype(bf16)
        g = ga_scr[sl, :]
        q = turn(q, sl, 1.0).astype(bf16).astype(f32) * (HD**-0.5)
        q_scr[sl, :] = q.astype(bf16)
        qt_scr[:, sl] = q.T.astype(bf16)
        k = turn(k, sl, 1.0).astype(bf16)
        v = v.astype(bf16)
        k_scr[sl, :] = k
        v_scr[sl, :] = v
        gt_scr[:, sl] = g.astype(f32).T.astype(bf16)
        for h in range(heads):
            keep = lane == h
            ks_scr[i, pl.ds(h * QB, QB), :] = jnp.where(keep, k, jnp.zeros_like(k))
            vs_scr[i, pl.ds(h * QB, QB), :] = jnp.where(keep, v, jnp.zeros_like(v))
    dkt_scr[...] = jnp.zeros_like(dkt_scr)
    dvt_scr[...] = jnp.zeros_like(dvt_scr)

    def query_block(i, _):
        rows = pl.ds(pl.multiple_of(i * QB, QB), QB)
        low, high = low_ref[seq, i], high_ref[seq, i]
        q = q_scr[rows, :]
        g = ga_scr[rows, :]
        zero = jnp.zeros_like(q)
        q_all = jnp.concatenate([jnp.where(lane == h, q, zero) for h in range(heads)], axis=0)
        g_all = jnp.concatenate([jnp.where(lane == h, g, zero) for h in range(heads)], axis=0)
        m_scr[...] = jnp.full_like(m_scr, MASKED_SCORE)
        first = first_ref[rows, :]
        final = final_ref[rows, :]

        def score(kb, _):
            keys = pl.ds(pl.multiple_of(kb * QB, QB), QB)
            s = lax.dot_general(q_all, k_scr[keys, :], nt, preferred_element_type=f32)
            d = lax.dot_general(g_all, v_scr[keys, :], nt, preferred_element_type=f32)
            col = lax.broadcasted_iota(jnp.int32, (QB, QB), 1) + kb * QB
            bias_scr[...] = jnp.where((col >= first) & (col <= final), 0.0, MASKED_SCORE)
            d_scr[kb] = d
            for h in range(heads):
                hs = slice(h * QB, (h + 1) * QB)
                x = s[hs] + bias_scr[...]
                s_scr[kb, hs, :] = x
                top = m_scr[hs, :]
                for j in range(QB // 128):
                    top = jnp.maximum(top, x[:, j * 128 : (j + 1) * 128])
                m_scr[hs, :] = top
            return 0

        lax.fori_loop(low, high + 1, score, 0)
        for h in range(heads):
            hs = slice(h * QB, (h + 1) * QB)
            m_scr[hs, :] = jnp.broadcast_to(jnp.max(m_scr[hs, :], axis=1, keepdims=True), (QB, 128))
        l_scr[...] = jnp.zeros_like(l_scr)
        e_scr[...] = jnp.zeros_like(e_scr)

        def expo(kb, _):
            for h in range(heads):
                hs = slice(h * QB, (h + 1) * QB)
                top, tot, dot = m_scr[hs, :], l_scr[hs, :], e_scr[hs, :]
                for j in range(QB // 128):
                    js = slice(j * 128, (j + 1) * 128)
                    e = jnp.exp(s_scr[kb, hs, js] - top)
                    s_scr[kb, hs, js] = e
                    tot = tot + e
                    dot = dot + e * d_scr[kb, hs, js]
                l_scr[hs, :] = tot
                e_scr[hs, :] = dot
            return 0

        lax.fori_loop(low, high + 1, expo, 0)
        for h in range(heads):
            hs = slice(h * QB, (h + 1) * QB)
            inv = 1.0 / jnp.sum(l_scr[hs, :], axis=1, keepdims=True)
            delta = jnp.sum(e_scr[hs, :], axis=1, keepdims=True) * inv
            l_scr[hs, :] = jnp.broadcast_to(inv, (QB, 128))
            e_scr[hs, :] = jnp.broadcast_to(delta, (QB, 128))
        o_scr[...] = jnp.zeros_like(o_scr)
        dq_scr[...] = jnp.zeros_like(dq_scr)

        def back(kb, _):
            keys = pl.ds(pl.multiple_of(kb * QB, QB), QB)
            for h in range(heads):
                hs = slice(h * QB, (h + 1) * QB)
                inv, delta = l_scr[hs, :], e_scr[hs, :]
                for j in range(QB // 128):
                    js = slice(j * 128, (j + 1) * 128)
                    out = slice(h * QB + j * 128, h * QB + (j + 1) * 128)
                    p = s_scr[kb, hs, js] * inv
                    p_scr[:, out] = p.astype(bf16)
                    ds_scr[:, out] = (p * (d_scr[kb, hs, js] - delta)).astype(bf16)
            o_scr[...] += jnp.dot(p_scr[...], vs_scr[kb], preferred_element_type=f32)
            dq_scr[...] += jnp.dot(ds_scr[...], ks_scr[kb], preferred_element_type=f32)
            for h in range(heads):
                hs = slice(h * HD, (h + 1) * HD)
                cs = slice(h * QB, (h + 1) * QB)
                dkt_scr[hs, keys] += jnp.dot(
                    qt_scr[hs, rows], ds_scr[:, cs], preferred_element_type=f32
                )
                dvt_scr[hs, keys] += jnp.dot(
                    gt_scr[hs, rows], p_scr[:, cs], preferred_element_type=f32
                )
            return 0

        lax.fori_loop(low, high + 1, back, 0)
        att_ref[rows, :] = o_scr[...].astype(bf16)
        gp_ref[rows, :width] = turn(dq_scr[...] * (HD**-0.5), rows, -1.0).astype(bf16)
        return 0

    lax.fori_loop(0, blocks, query_block, 0)
    for i in range(blocks):
        sl = pl.ds(i * QB, QB)
        gp_ref[sl, width : 2 * width] = turn(dkt_scr[:, sl].T, sl, -1.0).astype(bf16)
        gp_ref[sl, 2 * width :] = dvt_scr[:, sl].T.astype(bf16)


def attention(normed, grad, weights, doc_ids, image_start):
    rows, width = normed.shape[0], weights.shape[1] // 4
    count = rows // LEN
    heads = width // HD
    blocks = LEN // QB
    first, final = spans(doc_ids, image_start)
    low = jnp.min(first.reshape(count, blocks, QB), axis=2) // QB
    high = jnp.max(final.reshape(count, blocks, QB), axis=2) // QB
    f32, bf16 = jnp.float32, jnp.bfloat16
    seq_rows = lambda s, *_: (s, 0)
    fixed = lambda s, *_: (0, 0)
    return pl.pallas_call(
        functools.partial(attention_kernel, heads),
        out_shape=(
            jax.ShapeDtypeStruct((rows, width), bf16),
            jax.ShapeDtypeStruct((rows, 3 * width), bf16),
        ),
        grid_spec=pltpu.PrefetchScalarGridSpec(
            num_scalar_prefetch=2,
            grid=(count,),
            in_specs=[
                pl.BlockSpec((LEN, D), seq_rows),
                pl.BlockSpec((LEN, D), seq_rows),
                pl.BlockSpec((D, 4 * width), fixed, pipeline_mode=pl.Buffered(1)),
                pl.BlockSpec((LEN, 1), seq_rows),
                pl.BlockSpec((LEN, 1), seq_rows),
                pl.BlockSpec((LEN, width), fixed, pipeline_mode=pl.Buffered(1)),
                pl.BlockSpec((LEN, width), fixed, pipeline_mode=pl.Buffered(1)),
                pl.BlockSpec((LEN, width), fixed, pipeline_mode=pl.Buffered(1)),
            ],
            out_specs=[
                pl.BlockSpec((LEN, width), seq_rows),
                pl.BlockSpec((LEN, 3 * width), seq_rows),
            ],
            scratch_shapes=[
                pltpu.VMEM((LEN, width), bf16),
                pltpu.VMEM((LEN, width), bf16),
                pltpu.VMEM((LEN, width), bf16),
                pltpu.VMEM((LEN, width), bf16),
                pltpu.VMEM((width, LEN), bf16),
                pltpu.VMEM((width, LEN), bf16),
                pltpu.VMEM((blocks, heads * QB, width), bf16),
                pltpu.VMEM((blocks, heads * QB, width), bf16),
                pltpu.VMEM((blocks, heads * QB, QB), f32),
                pltpu.VMEM((blocks, heads * QB, QB), f32),
                pltpu.VMEM((QB, heads * QB), bf16),
                pltpu.VMEM((QB, heads * QB), bf16),
                pltpu.VMEM((QB, QB), f32),
                pltpu.VMEM((heads * QB, 128), f32),
                pltpu.VMEM((heads * QB, 128), f32),
                pltpu.VMEM((heads * QB, 128), f32),
                pltpu.VMEM((QB, width), f32),
                pltpu.VMEM((QB, width), f32),
                pltpu.VMEM((width, LEN), f32),
                pltpu.VMEM((width, LEN), f32),
            ],
        ),
        compiler_params=pltpu.CompilerParams(
            dimension_semantics=("arbitrary",), vmem_limit_bytes=58 << 20
        ),
        cost_estimate=pl.CostEstimate(
            flops=12 * rows * 640 * width * 3 + 8 * rows * D * width,
            bytes_accessed=rows * (width * 8 + D * 4) + 8 * D * width,
            transcendentals=rows * 640 * heads,
        ),
        name="attention",
    )(
        low,
        high,
        normed,
        grad,
        weights,
        first.reshape(rows, 1),
        final.reshape(rows, 1),
        *rope_tables(width),
    )


NT = (((1,), (1,)), ((), ()))


def ffn_kernel(x_ref, g_ref, wgu_ref, wd_ref, hidden_ref, gg_ref, gu_ref):
    f32, bf16 = jnp.float32, jnp.bfloat16
    x = x_ref[...]
    gate = lax.dot_general(x, wgu_ref[0], NT, preferred_element_type=f32)
    up = lax.dot_general(x, wgu_ref[1], NT, preferred_element_type=f32)
    grad = lax.dot_general(g_ref[...], wd_ref[...], NT, preferred_element_type=f32)
    sigma = jax.nn.sigmoid(gate)
    silu = gate * sigma
    hidden_ref[...] = (silu * up).astype(bf16)
    gg_ref[...] = (grad * up * (sigma + silu * (1.0 - sigma))).astype(bf16)
    gu_ref[...] = (grad * silu).astype(bf16)


def feed_forward(normed, grad, wgu, wd):
    rows, ffn = normed.shape[0], wd.shape[0]
    block = lambda i: (i, 0)
    return pl.pallas_call(
        ffn_kernel,
        out_shape=[jax.ShapeDtypeStruct((rows, ffn), jnp.bfloat16)] * 3,
        grid=(rows // MB,),
        in_specs=[
            pl.BlockSpec((MB, D), block),
            pl.BlockSpec((MB, D), block),
            pl.BlockSpec((2, ffn, D), lambda i: (0, 0, 0), pipeline_mode=pl.Buffered(1)),
            pl.BlockSpec((ffn, D), lambda i: (0, 0), pipeline_mode=pl.Buffered(1)),
        ],
        out_specs=[pl.BlockSpec((MB, ffn), block)] * 3,
        compiler_params=pltpu.CompilerParams(
            dimension_semantics=("arbitrary",), vmem_limit_bytes=56 << 20
        ),
        cost_estimate=pl.CostEstimate(
            flops=6 * rows * D * ffn,
            bytes_accessed=rows * (4 * D + 6 * ffn) + 6 * D * ffn,
            transcendentals=rows * ffn,
        ),
        name="feed_forward",
    )(normed, grad, wgu, wd)


def flip(index, bits):
    bit = 1
    while bit <= bits:
        if bits & bit:
            index = index + bit - 2 * bit * ((index // bit) % 2)
        bit *= 2
    return index


def chip_orders(ways):
    bits = [1 << k for k in range(1, ways.bit_length() - 1)]
    return bits, bits[::-1]


def held(bits):
    found = [0]
    for bit in bits:
        found += [o ^ bit for o in found]
    return found


def meet(peers):
    barrier = pltpu.get_barrier_semaphore()
    for peer in peers:
        pl.semaphore_signal(barrier, inc=1, device_id=peer, device_id_type=MESH)
    pl.semaphore_wait(barrier, len(peers))


def gather_kernel(
    ways,
    pairs,
    token_ref,
    grad_ref,
    vector_ref,
    normed_ref,
    full_ref,
    stat_ref,
    vectors_ref,
    both,
    ready,
    load_sem,
    store_sem,
    full_sem,
    send_sem,
    recv_sem,
    vsend_sem,
    vrecv_sem,
):
    f32, bf16 = jnp.float32, jnp.bfloat16
    me = lax.axis_index("col")
    rows, width = token_ref.shape
    part = rows // pairs
    orders = chip_orders(ways)
    phases = len(orders[0])
    loads = [
        pltpu.make_async_copy(token_ref, both.at[me, :, pl.ds(0, width)], load_sem.at[0]),
        pltpu.make_async_copy(grad_ref, both.at[me, :, pl.ds(width, width)], load_sem.at[1]),
    ]
    for load in loads:
        load.start()
    mine = pl.ds(pl.multiple_of(me * width, width), width)
    vectors_ref[:, mine] = vector_ref[...]
    peers = [flip(me, k) for k in range(1, ways)]
    meet([{"col": peer} for peer in peers])

    def vector_copy(k):
        return pltpu.make_async_remote_copy(
            src_ref=vectors_ref.at[:, mine],
            dst_ref=vectors_ref.at[:, mine],
            send_sem=vsend_sem.at[k],
            recv_sem=vrecv_sem.at[k],
            device_id={"col": peers[k]},
            device_id_type=MESH,
        )

    for k in range(ways - 1):
        vector_copy(k).start()
    for load in loads:
        load.wait()

    def copies(p, phase):
        for k, order in enumerate(orders):
            bit = order[phase] if phase < phases else 1
            place = pl.ds(p * part + k * (part // 2), part // 2)
            for o in held(order[:phase]):
                index = (p * 2 + k) * ways + (o ^ bit)
                owner = flip(me, o)
                yield pltpu.make_async_remote_copy(
                    src_ref=both.at[owner, place],
                    dst_ref=both.at[owner, place],
                    send_sem=send_sem.at[index],
                    recv_sem=recv_sem.at[index],
                    device_id={"col": flip(me, bit)},
                    device_id_type=MESH,
                )

    def start(p, phase):
        if p < pairs:
            for copy in copies(p, phase):
                copy.start()

    def arrive(p, phase):
        for copy in copies(p, phase):
            copy.wait_recv()

    def stored(p):
        return pltpu.make_async_copy(
            ready.at[p % 2], normed_ref.at[pl.ds(p * part, part)], store_sem.at[p % 2]
        )

    def full_done(p):
        rows_p = full_ref.at[pl.ds(p * part, part)]
        return pltpu.make_async_copy(rows_p, rows_p, full_sem.at[p])

    def work(p):
        place = pl.ds(p * part, part)
        for b in range(ways):
            pltpu.make_async_copy(
                both.at[b, place, pl.ds(width, width)],
                full_ref.at[place, pl.ds(b * width, width)],
                full_sem.at[p],
            ).start()
        if p >= 2:
            stored(p - 2).wait()

        def block(j, _):
            own = pl.ds(pl.multiple_of(j * QB, QB), QB)
            at = pl.ds(pl.multiple_of(p * part + j * QB, QB), QB)
            sums = sum(both[b, at, :width].astype(f32) for b in range(ways))
            mean = jnp.sum(sums, axis=1, keepdims=True) / D
            squares = jnp.zeros((QB, width), f32)
            for b in range(ways):
                x = both[b, at, :width].astype(f32) - mean
                squares += x * x
            inv = lax.rsqrt(jnp.sum(squares, axis=1, keepdims=True) / D + NORM_EPS)
            stat_ref[at, :1] = mean
            stat_ref[at, 1:] = inv
            for b in range(ways):
                cols = slice(b * width, (b + 1) * width)
                x = (both[b, at, :width].astype(f32) - mean) * inv
                ready[p % 2, own, cols] = (
                    x * vectors_ref[0:1, cols] + vectors_ref[1:2, cols]
                ).astype(bf16)
            return 0

        lax.fori_loop(0, part // QB, block, 0)
        stored(p).start()

    start(0, 0)
    start(1, 0)
    for k in range(ways - 1):
        vector_copy(k).wait_recv()
    for p in range(pairs):
        for phase in range(phases):
            arrive(p, phase)
            start(p, phase + 1)
            if phase == 0:
                start(p + 2, 0)
                if p >= 1:
                    arrive(p - 1, phases)
                    work(p - 1)
    arrive(pairs - 1, phases)
    work(pairs - 1)
    for p in range(pairs):
        full_done(p).wait()
        for phase in range(phases + 1):
            for copy in copies(p, phase):
                copy.wait_send()
    for p in range(max(pairs - 2, 0), pairs):
        stored(p).wait()
    for k in range(ways - 1):
        vector_copy(k).wait_send()


def gather(tokens, out_grad, vectors, ways):
    rows, width = tokens.shape
    pairs = rows // LEN
    bf16, f32 = jnp.bfloat16, jnp.float32
    anywhere = pl.BlockSpec(memory_space=pl.ANY)
    vmem = pl.BlockSpec(memory_space=pltpu.VMEM)
    dma = pltpu.SemaphoreType.DMA
    return pl.pallas_call(
        functools.partial(gather_kernel, ways, pairs),
        out_shape=[
            jax.ShapeDtypeStruct((rows, D), bf16),
            jax.ShapeDtypeStruct((rows, D), bf16),
            jax.ShapeDtypeStruct((rows, 2), f32),
            jax.ShapeDtypeStruct((8, D), f32),
        ],
        in_specs=[anywhere, anywhere, vmem],
        out_specs=[anywhere, anywhere, vmem, vmem],
        scratch_shapes=[
            pltpu.VMEM((ways, rows, 2 * width), bf16),
            pltpu.VMEM((2, rows // pairs, D), bf16),
            dma((2,)),
            dma((2,)),
            dma((pairs,)),
            dma((pairs * 2 * ways,)),
            dma((pairs * 2 * ways,)),
            dma((ways - 1,)),
            dma((ways - 1,)),
        ],
        compiler_params=pltpu.CompilerParams(
            collective_id=0, has_side_effects=True, vmem_limit_bytes=56 << 20
        ),
        cost_estimate=pl.CostEstimate(
            flops=200 * rows * D * D // ways, bytes_accessed=rows * D * 8, transcendentals=0
        ),
        name="gather",
    )(tokens, out_grad, vectors)


class Reducer:
    def __init__(self, ways, parts, inbox, send_sem, recv_sem):
        self.ways, self.parts, self.inbox = ways, parts, inbox
        self.send_sem, self.recv_sem = send_sem, recv_sem
        self.me = lax.axis_index("col")
        self.orders = chip_orders(ways)
        self.phases = 1 + len(self.orders[0])

    def moves(self, step, phase):
        halves = [None] if phase == 0 else [0, 1]
        for k in halves:
            order = [1] if phase == 0 else [1, *self.orders[k]]
            bit = order[phase]
            done = sum(order[:phase])
            count = MB if k is None else MB // 2
            rows = pl.ds(pl.multiple_of(step * MB + (k or 0) * count, count), count)
            for o in range(self.ways):
                if o & done or not o & bit:
                    continue
                goal = o ^ bit
                slot = slot_of(self.ways, self.orders, phase, k, goal)
                sem = 2 * slot + (k or 0)
                copy = pltpu.make_async_remote_copy(
                    src_ref=self.parts.at[o, rows],
                    dst_ref=self.inbox.at[slot, rows],
                    send_sem=self.send_sem.at[step, sem],
                    recv_sem=self.recv_sem.at[step, sem],
                    device_id={"col": flip(self.me, bit)},
                    device_id_type=MESH,
                )
                yield copy, goal, slot, rows

    def send(self, step, phase):
        for copy, *_ in self.moves(step, phase):
            copy.start()

    def absorb(self, step, phase):
        out = []
        for copy, goal, slot, rows in self.moves(step, phase):
            copy.wait_recv()
            value = self.parts[goal, rows, :].astype(jnp.float32)
            value += self.inbox[slot, rows, :].astype(jnp.float32)
            if phase == self.phases - 1:
                out.append(value)
            else:
                self.parts[goal, rows, :] = value.astype(jnp.bfloat16)
        return out

    def finish(self, step):
        for phase in range(self.phases):
            for copy, *_ in self.moves(step, phase):
                copy.wait_send()

    def advance(self, t, steps, lags):
        pl.when(t < steps)(lambda: self.send(t, 0))
        for phase in range(self.phases - 1):
            s = t - lags[phase]

            @pl.when((s >= 0) & (s < steps))
            def _():
                self.absorb(s, phase)
                self.send(s, phase + 1)


def slot_of(ways, orders, phase, half, goal):
    if phase == 0:
        return goal // 2
    order = [1, *orders[half]]
    base = ways // 2
    for p in range(1, phase):
        base += ways >> (p + 1)
    goals = [g for g in range(ways) if not g & sum(order[: phase + 1])]
    return base + goals.index(goal)


def lags_of(ways):
    return [1 + 2 * p for p in range(len(chip_orders(ways)[0]) + 1)]


def reducer_scratch(ways, rows, width):
    steps = rows // MB
    return [
        pltpu.VMEM((ways, rows, width), jnp.bfloat16),
        pltpu.VMEM((ways - 1, rows, width), jnp.bfloat16),
        pltpu.SemaphoreType.DMA((steps, 2 * ways)),
        pltpu.SemaphoreType.DMA((steps, 2 * ways)),
    ]


def branch_kernel(
    ways,
    steps,
    att_ref,
    hidden_ref,
    grad_ref,
    token_ref,
    wout_ref,
    wd_ref,
    out_ref,
    wgrad_ref,
    parts,
    inbox,
    send_sem,
    recv_sem,
    acc,
):
    f32, bf16 = jnp.float32, jnp.bfloat16
    t = pl.program_id(0)
    me, width = lax.axis_index("col"), D // ways
    lags = lags_of(ways)
    ring = Reducer(ways, parts, inbox, send_sem, recv_sem)

    @pl.when(t == 0)
    def _():
        acc[...] = jnp.zeros_like(acc)
        meet([{"col": flip(me, 1 << k)} for k in range(ways.bit_length() - 1)])

    @pl.when(t < steps)
    def _():
        rows = pl.ds(pl.multiple_of(t * MB, MB), MB)
        att, hidden = att_ref[...], hidden_ref[...]
        for o in range(ways):
            cols = pl.ds(pl.multiple_of(flip(me, o) * width, width), width)
            total = lax.dot_general(att, wout_ref[cols, :], NT, preferred_element_type=f32)
            total += jnp.dot(hidden, wd_ref[:, cols], preferred_element_type=f32)
            parts[o, rows, :] = total.astype(bf16)

    ring.advance(t, steps, lags)

    @pl.when(t < steps)
    def _():
        acc[...] += contract(hidden_ref[...], grad_ref[...], 0, 0)

    @pl.when(t == steps)
    def _():
        wgrad_ref[...] = acc[...].astype(bf16)

    s = t - lags[-1]

    @pl.when(s >= 0)
    def _():
        for k, value in enumerate(ring.absorb(s, ring.phases - 1)):
            half = slice(k * (MB // 2), (k + 1) * (MB // 2))
            out_ref[half, :] = (token_ref[half, :].astype(f32) + value).astype(bf16)
        ring.finish(s)


def branches(att, hidden, grad, tokens, weights, wd, ways):
    rows, width = tokens.shape
    ffn = wd.shape[0]
    steps = rows // MB
    lag = lags_of(ways)[-1]
    now = lambda t: (jnp.minimum(t, steps - 1), 0)
    late = lambda t: (jnp.maximum(t - lag, 0), 0)
    fixed = lambda t: (0, 0)
    once = pl.Buffered(1)
    return pl.pallas_call(
        functools.partial(branch_kernel, ways, steps),
        out_shape=[
            jax.ShapeDtypeStruct((rows, width), jnp.bfloat16),
            jax.ShapeDtypeStruct((ffn, D), jnp.bfloat16),
        ],
        grid=(steps + lag,),
        in_specs=[
            pl.BlockSpec((MB, width), now),
            pl.BlockSpec((MB, ffn), now),
            pl.BlockSpec((MB, D), now),
            pl.BlockSpec((MB, width), late),
            pl.BlockSpec((D, width), lambda t: (0, 3), pipeline_mode=once),
            pl.BlockSpec((ffn, D), fixed, pipeline_mode=once),
        ],
        out_specs=[
            pl.BlockSpec((MB, width), late),
            pl.BlockSpec((ffn, D), fixed, pipeline_mode=once),
        ],
        scratch_shapes=[*reducer_scratch(ways, rows, width), pltpu.VMEM((ffn, D), jnp.float32)],
        compiler_params=pltpu.CompilerParams(
            collective_id=1,
            has_side_effects=True,
            dimension_semantics=("arbitrary",),
            vmem_limit_bytes=60 << 20,
        ),
        cost_estimate=pl.CostEstimate(
            flops=8 * rows * D * (2 * ffn + width), bytes_accessed=4 * rows * D, transcendentals=0
        ),
        name="branches",
    )(att, hidden, grad, tokens, weights, wd)


def back_kernel(
    ways,
    lines,
    steps,
    gp_ref,
    gg_ref,
    gu_ref,
    x_ref,
    token_ref,
    cot_ref,
    stat_ref,
    w_ref,
    wgu_ref,
    vectors_ref,
    gain_ref,
    out_ref,
    vgrad_ref,
    parts,
    inbox,
    send_sem,
    recv_sem,
    sums,
    ssend_sem,
    srecv_sem,
    acc,
    vsend_sem,
    vrecv_sem,
):
    f32, bf16 = jnp.float32, jnp.bfloat16
    t = pl.program_id(0)
    me, width = lax.axis_index("col"), D // ways
    line = lax.axis_index("row")
    lags = lags_of(ways)
    ring = Reducer(ways, parts, inbox, send_sem, recv_sem)

    @pl.when(t == 0)
    def _():
        acc[...] = jnp.zeros_like(acc)
        meet(
            [{"col": flip(me, k)} for k in range(1, ways)]
            + [{"row": (line + k) % lines} for k in range(1, lines)]
        )

    def sum_copies(step):
        rows = pl.ds(pl.multiple_of(step * MB, MB), MB)
        for k in range(1, ways):
            yield pltpu.make_async_remote_copy(
                src_ref=sums.at[0, :, rows],
                dst_ref=sums.at[k, :, rows],
                send_sem=ssend_sem.at[step, k - 1],
                recv_sem=srecv_sem.at[step, k - 1],
                device_id={"col": flip(me, k)},
                device_id_type=MESH,
            )

    @pl.when(t < steps)
    def _():
        rows = pl.ds(pl.multiple_of(t * MB, MB), MB)
        gp, gg, gu = gp_ref[...], gg_ref[...], gu_ref[...]
        plain = jnp.zeros((MB, 1), f32)
        cross = jnp.zeros((MB, 1), f32)
        for o in range(ways):
            cols = pl.ds(pl.multiple_of(flip(me, o) * width, width), width)
            total = jnp.dot(gg, wgu_ref[0, :, cols], preferred_element_type=f32)
            total += jnp.dot(gu, wgu_ref[1, :, cols], preferred_element_type=f32)
            total += lax.dot_general(gp, w_ref[cols, :], NT, preferred_element_type=f32)
            parts[o, rows, :] = total.astype(bf16)
            scaled = x_ref[:, cols].astype(f32) - vectors_ref[1:2, cols]
            plain += jnp.sum(total * vectors_ref[0:1, cols], axis=1, keepdims=True)
            cross += jnp.sum(total * scaled, axis=1, keepdims=True)
        lane = lax.broadcasted_iota(jnp.int32, (MB, 128), 1)
        pair = jnp.where(lane == 0, plain, jnp.where(lane == 1, cross, 0.0))
        sums[0, :, rows] = pair.T[:8]
        for copy in sum_copies(t):
            copy.start()

    ring.advance(t, steps, lags)
    s = t - lags[-1]

    @pl.when(s >= 0)
    def _():
        rows = pl.ds(pl.multiple_of(s * MB, MB), MB)
        for copy in sum_copies(s):
            copy.wait_recv()
        both = sum(sums[k, :, rows] for k in range(ways)).T
        for k, value in enumerate(ring.absorb(s, ring.phases - 1)):
            half = slice(k * (MB // 2), (k + 1) * (MB // 2))
            inv = stat_ref[half, 1:]
            unit = (token_ref[half, :].astype(f32) - stat_ref[half, :1]) * inv
            scaled = value * gain_ref[0:1, :]
            out_ref[half, :] = cot_ref[half, :].astype(f32) + inv * (
                scaled - both[half, 0:1] / D - unit * (both[half, 1:2] / D)
            )
            acc[0, 0:1, :] += jnp.sum(value * unit, axis=0, keepdims=True)
            acc[0, 1:2, :] += jnp.sum(value, axis=0, keepdims=True)
        for copy in sum_copies(s):
            copy.wait_send()
        ring.finish(s)

    @pl.when(t == pl.num_programs(0) - 1)
    def _():
        copies = [
            pltpu.make_async_remote_copy(
                src_ref=acc.at[0],
                dst_ref=acc.at[k],
                send_sem=vsend_sem.at[k - 1],
                recv_sem=vrecv_sem.at[k - 1],
                device_id={"row": (line + k) % lines},
                device_id_type=MESH,
            )
            for k in range(1, lines)
        ]
        for copy in copies:
            copy.start()
        for copy in copies:
            copy.wait()
        vgrad_ref[...] = sum(acc[k] for k in range(lines))


def norm_back(gp, gg, gu, normed, tokens, cot, stats, weights, wgu, vectors, own, ways, lines):
    rows, width = tokens.shape
    ffn = gg.shape[1]
    steps = rows // MB
    lag = lags_of(ways)[-1]
    now = lambda t: (jnp.minimum(t, steps - 1), 0)
    late = lambda t: (jnp.maximum(t - lag, 0), 0)
    fixed = lambda t: (0, 0)
    once = pl.Buffered(1)
    dma = pltpu.SemaphoreType.DMA
    return pl.pallas_call(
        functools.partial(back_kernel, ways, lines, steps),
        out_shape=[
            jax.ShapeDtypeStruct((rows, width), jnp.float32),
            jax.ShapeDtypeStruct((8, width), jnp.float32),
        ],
        grid=(steps + lag,),
        in_specs=[
            pl.BlockSpec((MB, 3 * width), now),
            pl.BlockSpec((MB, ffn), now),
            pl.BlockSpec((MB, ffn), now),
            pl.BlockSpec((MB, D), now),
            pl.BlockSpec((MB, width), late),
            pl.BlockSpec((MB, width), late),
            pl.BlockSpec((MB, 2), late),
            pl.BlockSpec((D, 3 * width), fixed, pipeline_mode=once),
            pl.BlockSpec((2, ffn, D), lambda t: (0, 0, 0), pipeline_mode=once),
            pl.BlockSpec((8, D), fixed),
            pl.BlockSpec((8, width), fixed),
        ],
        out_specs=[pl.BlockSpec((MB, width), late), pl.BlockSpec((8, width), fixed)],
        scratch_shapes=[
            *reducer_scratch(ways, rows, width),
            pltpu.VMEM((ways, 8, rows), jnp.float32),
            dma((steps, ways - 1)),
            dma((steps, ways - 1)),
            pltpu.VMEM((lines, 8, width), jnp.float32),
            dma((lines - 1,)),
            dma((lines - 1,)),
        ],
        compiler_params=pltpu.CompilerParams(
            collective_id=2,
            has_side_effects=True,
            dimension_semantics=("arbitrary",),
            vmem_limit_bytes=61 << 20,
        ),
        cost_estimate=pl.CostEstimate(
            flops=4 * rows * D * (2 * ffn + 3 * width), bytes_accessed=6 * rows * D, transcendentals=0
        ),
        name="norm_back",
    )(gp, gg, gu, normed, tokens, cot, stats, weights, wgu, vectors, own)


def after(value, *others):
    return lax.optimization_barrier((value, others))[0]


def local(
    tokens,
    norm_gain,
    norm_bias,
    qkv_weight,
    gate_up_weight,
    out_weight,
    down_weight,
    image_start,
    doc_ids,
    out_grad,
):
    f32, bf16 = jnp.float32, jnp.bfloat16
    block_rows, width = tokens.shape
    ways = D // width
    lines = D // qkv_weight.shape[0]

    own = jnp.concatenate([qkv_weight[:, k] for k in range(3)] + [out_weight], axis=1)
    weights = lax.all_gather(own, "row", axis=0, tiled=True)
    full_gate_up = lax.all_gather(gate_up_weight, "row", axis=0, tiled=True)
    full_down = lax.all_gather(down_weight, "row", axis=0, tiled=True)
    wgu = jnp.transpose(full_gate_up, (1, 2, 0))
    wd = jnp.transpose(full_down, (1, 0))
    own_vectors = jnp.pad(jnp.stack([norm_gain, norm_bias]), ((0, 6), (0, 0)))

    normed, grad, stats, vectors = gather(tokens, out_grad, own_vectors, ways)
    attended, grad_projected = attention(normed, grad, weights, doc_ids, image_start)

    def weight_sum(grad):
        return lax.psum_scatter(grad, "row", scatter_dimension=0, tiled=True)

    def weight_grad(left, right):
        return contract(left, right, 0, 0).astype(bf16)

    grad_qkv = weight_grad(normed, grad_projected)
    grad_out = weight_grad(grad, attended)
    hidden, grad_gate, grad_up = feed_forward(after(normed, grad_qkv, grad_out), grad, wgu, wd)
    weight_gate = weight_grad(normed, grad_gate)
    weight_up = weight_grad(normed, after(grad_up, weight_gate))
    outputs, weight_down = branches(
        after(attended, weight_up), hidden, grad, tokens, weights, wd, ways
    )
    input_grad, vector_grads = norm_back(
        after(grad_projected, outputs),
        grad_gate,
        grad_up,
        normed,
        tokens,
        out_grad,
        stats,
        weights,
        wgu,
        vectors,
        own_vectors,
        ways,
        lines,
    )
    qkv_sum = weight_sum(grad_qkv.reshape(D, 3, width)).astype(f32)
    out_sum = weight_sum(grad_out).astype(f32)
    gate_sum = weight_sum(weight_gate)
    up_sum = weight_sum(weight_up)
    down_sum = weight_sum(jnp.transpose(weight_down, (1, 0))).astype(f32)
    gate_up_sum = jnp.stack([gate_sum.astype(f32), up_sum.astype(f32)], axis=1)
    return (
        outputs,
        input_grad,
        vector_grads[0],
        vector_grads[1],
        qkv_sum,
        gate_up_sum,
        out_sum,
        down_sum,
    )


def solution(mesh):
    placed = (
        P("row", "col"),
        P("col"),
        P("col"),
        P("row", None, "col"),
        P("row", None, "col"),
        P("row", "col"),
        P("row", "col"),
        P("row"),
        P("row", None),
        P("row", "col"),
    )
    return jax.shard_map(
        local,
        mesh=mesh,
        in_specs=placed,
        out_specs=(
            P("row", "col"),
            P("row", "col"),
            P("col"),
            P("col"),
            P("row", None, "col"),
            P("row", None, "col"),
            P("row", "col"),
            P("row", "col"),
        ),
        check_vma=False,
    )
```

time: 1560 us -> 634 us (0.41)
  waiting for transfers between devices: 672 us -> 1.54 us
  Pallas kernels: 0 us -> 494 us
  matrix products: 401 us -> 69.1 us
  local copies, waits for them, and re-layouts: 268 us -> 24 us
  blocking collectives: 84.8 us -> 0 us
  other arithmetic: 106 us -> 23.1 us
    pallas_call x0 -> x5, Pallas kernels: none -> 494 us  [the longest x1 158 us: gather(): pl.pallas_call(functools.partial(gather_kernel, ways, pairs), out_shape=[...]
    reduce_scatter x7 -> x5, waiting for transfers between devices: 467 us -> 0.02 us  [weight_sum(): return lax.psum_scatter(grad, 'row', scatter_dimension=0, tiled=True)]
    dot_general x32 -> x0, matrix products: 235 us -> none  [the longest x8 40.5 us: masked_scores(): jnp.einsum('qhd,khd->hqk', queries, key_rows, preferred_element_type=jnp....]
    all_gather x6 -> x3, waiting for transfers between devices: 203 us -> 0.04 us  [the longest x1 0.02 us: local(): full_down = lax.all_gather(down_weight, 'row', axis=0, tiled=True)]
    dynamic_update_slice x16 -> x0, local copies, waits for them, and re-layouts: 168 us -> none  [local(): lax.map(attend, (queries, key_rows, value_rows, image_start, doc_ids))]
    dot_general x8 -> x4, matrix products: 166 us -> 69.1 us  [contract(): lax.dot_general(left, right, (((left_dim,), (right_dim,)), ((), ())), pre...]
    psum x4 -> x0, blocking collectives: 84.8 us -> none  [the longest x1 26.3 us: local(): row_mean = lax.psum(jnp.sum(inputs, axis=1), 'col') / D]
    convert_element_type x9 -> x4, other arithmetic: 42.7 us -> 6.75 us  [the longest x1 2.56 us: local(): down_sum = weight_sum(jnp.transpose(weight_down, (1, 0))).astype(f32)]
  transfers between devices with their start and end apart: 13 -> 8, of which waited for: 8 -> 0; matrix products, arithmetic and copies ran while one was open for 49% -> 17% of each run, Pallas kernels for 0% -> 79%
where the time goes in v1:
time: 634 us; the launch traced here: 627 us
  Pallas kernels  494 us (78%)
  matrix products  69.1 us (11%)
  local copies, waits for them, and re-layouts  24 us (4%)
  other arithmetic  23.1 us (4%)
  between operations  14.8 us (2%)
    pallas_call x1, Pallas kernels, gather(): pl.pallas_call(functools.partial(gather_kernel, ways, pairs), out_shape=[...  158 us
    pallas_call x1, Pallas kernels, norm_back(): pl.pallas_call(functools.partial(back_kernel, ways, lines, steps), out_sh...  106 us
    pallas_call x1, Pallas kernels, attention(): pl.pallas_call(functools.partial(attention_kernel, heads), out_shape=(jax...  95.7 us
    pallas_call x1, Pallas kernels, branches(): pl.pallas_call(functools.partial(branch_kernel, ways, steps), out_shape=[...  85.6 us
    dot_general x4, matrix products, contract(): lax.dot_general(left, right, (((left_dim,), (right_dim,)), ((), ())), pre...  69.1 us
    pallas_call x1, Pallas kernels, feed_forward(): pl.pallas_call(ffn_kernel, out_shape=[jax.ShapeDtypeStruct((rows, ffn), j...  48.6 us
  transfers between devices with their start and end apart: 8, of which 0 were waited for; matrix products, arithmetic and copies ran while one was open for 17% of the time, Pallas kernels for 79%

profile of v1, /device:TPU:0, one launch (start us, length us, event | category | flops | bytes accessed | tf_op | source)
XLA Modules:
  0.0 627.5 jit_solution(6569822883659314825)
XLA Ops:
  7.2 1.2 slice_bitcast_fusion.2
  8.4 2.1 pad_maximum_fusion
  10.5 0.7 all-gather.8.cloned.1.call-update
  11.3 0.7 all-gather.6.cloned.1.call-update
  14.9 158.2 %gather.1 = (bf16[4096,2048]{1,0:T(8,128)(2,1)}, bf16[4096,2048]{1,0:T(8,128)(2,1)}, f32[4096,2]{1,0:T(8,128)}, f32[8,2048]{1,0:T(8,128)}) custom-call(bf16[4096,256]{1,0:T(8,128)(2,1)} %token_ref.5, bf16[4096,256]{1,0:T(8,128)(2,1)} %cot_ref.1, f32[8,256]{1,0:T(8,128)} %select_maximum_fusion.vector_ref.gain_ref), custom_call_target="tpu_custom_call" | custom-call | flops 429496729600 | bytes 67108864 | tf_op jit(solution)/shard_map/gather/pallas_call | solution.py:526
  174.1 3.9 convert_reduce_fusion
  178.4 1.5 copy.43
  179.9 0.8 maximum_maximum_fusion
  180.8 1.3 copy.47.c_ref
  182.2 1.4 copy.48.a_ref
  183.6 1.1 tile.31
  184.7 1.3 copy.49.b_ref
  186.0 2.0 copy.58
  188.0 2.0 copy.52
  189.9 2.0 copy.56
  192.9 4.0 bitcast_select_fusion.final_ref
  196.9 95.7 %attention.1 = (bf16[4096,256]{1,0:T(8,128)(2,1)}, bf16[4096,768]{1,0:T(8,128)(2,1)}) custom-call(s32[4,4]{1,0:T(4,128)} %get-tuple-element.59.low_ref, s32[4,4]{1,0:T(4,128)} %get-tuple-element.58.high_ref, bf16[4096,2048]{1,0:T(8,128)(2,1)} %get-tuple-element.29.x_ref, bf16[4096,2048]{1,0:T(8,128)(2,1)} %get-tuple-element.26.g_ref.grad_ref, ...), custom_call_target="tpu_custom_call" | custom-call | flops 41339060224 | bytes 46137344 | tf_op jit(solution)/shard_map/attention/pallas_call | solution.py:236
  292.6 12.3 %convolution_convert_fusion.3 = bf16[2048,256]{1,0:T(8,128)(2,1)} fusion(bf16[4096,2048]{1,0:T(8,128)(2,1)} %get-tuple-element.26.g_ref.grad_ref, bf16[4096,256]{1,0:T(8,128)(2,1)} %get-tuple-element.33.att_ref), kind=kOutput, calls=%fused_computation.5 | convolution fusion | flops 4295491584 | bytes 19922944 | tf_op jit(solution)/shard_map/dot_general | solution.py:26
  305.0 18.9 %convolution_convert_fusion = bf16[2048,768]{0,1:T(8,128)(2,1)S(1)} fusion(bf16[4096,2048]{1,0:T(8,128)(2,1)} %get-tuple-element.29.x_ref, bf16[4096,768]{1,0:T(8,128)(2,1)} %get-tuple-element.36.gp_ref), kind=kOutput, calls=%fused_computation.2 | convolution fusion | flops 12886474752 | bytes 26214400 | tf_op jit(solution)/shard_map/dot_general | solution.py:26
  323.9 2.8 copy.50
  327.0 48.6 %feed_forward.1 = (bf16[4096,704]{1,0:T(8,128)(2,1)}, bf16[4096,704]{1,0:T(8,128)(2,1)}, bf16[4096,704]{1,0:T(8,128)(2,1)}) custom-call(bf16[4096,2048]{1,0:T(8,128)(2,1)} %get-tuple-element.29.x_ref, bf16[4096,2048]{1,0:T(8,128)(2,1)} %get-tuple-element.26.g_ref.grad_ref, bf16[2,704,2048]{2,1,0:T(8,128)(2,1)} %bitcast.76, bf16[704,2048]{1,0:T(8,128)(2,1)} %bitcast.78), custom_call_target="tpu_custom_call" | custom-call | flops 35433480192 | bytes 59506688 | tf_op jit(solution)/shard_map/feed_forward/pallas_call | solution.py:322
  375.5 18.8 %convolution_convert_fusion.2 = bf16[2048,704]{0,1:T(8,128)(2,1)} fusion(bf16[4096,2048]{1,0:T(8,128)(2,1)} %get-tuple-element.29.x_ref, bf16[4096,704]{1,0:T(8,128)(2,1)} %get-tuple-element.31.gg_ref), kind=kOutput, calls=%fused_computation.4 | convolution fusion | flops 11812601856 | bytes 25427968 | tf_op jit(solution)/shard_map/dot_general | solution.py:26
  394.4 1.8 convert_element_type.66
  396.2 19.2 %convolution_convert_fusion.1 = bf16[2048,704]{0,1:T(8,128)(2,1)} fusion(bf16[4096,2048]{1,0:T(8,128)(2,1)} %get-tuple-element.29.x_ref, bf16[4096,704]{1,0:T(8,128)(2,1)} %get-tuple-element.32.gu_ref), kind=kOutput, calls=%fused_computation.3 | convolution fusion | flops 11812601856 | bytes 25427968 | tf_op jit(solution)/shard_map/dot_general | solution.py:26
  415.7 85.6 %branches.1 = (bf16[4096,256]{1,0:T(8,128)(2,1)}, bf16[704,2048]{1,0:T(8,128)(2,1)}) custom-call(bf16[4096,256]{1,0:T(8,128)(2,1)} %get-tuple-element.33.att_ref, bf16[4096,704]{1,0:T(8,128)(2,1)} %get-tuple-element.34.hidden_ref, bf16[4096,2048]{1,0:T(8,128)(2,1)} %get-tuple-element.26.g_ref.grad_ref, bf16[4096,256]{1,0:T(8,128)(2,1)} %token_ref.5, ...), custom_call_target="tpu_custom_call" | custom-call | flops 111669149696 | bytes 33554432 | tf_op jit(solution)/shard_map/branches/pallas_call | solution.py:713
  501.3 106.1 %norm_back.1 = (f32[4096,256]{1,0:T(8,128)}, f32[8,256]{1,0:T(8,128)}) custom-call(bf16[4096,768]{1,0:T(8,128)(2,1)} %get-tuple-element.36.gp_ref, bf16[4096,704]{1,0:T(8,128)(2,1)} %get-tuple-element.31.gg_ref, bf16[4096,704]{1,0:T(8,128)(2,1)} %get-tuple-element.32.gu_ref, bf16[4096,2048]{1,0:T(8,128)(2,1)} %get-tuple-element.29.x_ref, ...), custom_call_target="tpu_custom_call" | custom-call | flops 73014444032 | bytes 50331648 | tf_op jit(solution)/shard_map/norm_back/pallas_call | solution.py:875
  607.4 1.3 fusion.6
  608.7 2.4 convert_element_type.65
  611.1 3.2 maximum_convert_fusion
  614.4 2.6 convert_element_type.67
  616.9 1.3 copy.61
  618.3 2.0 copy.62
  (79 shorter events, 6.2 us)
Async XLA Ops:
  7.2 6.6 %copy-start.4 = (s32[4]{0:T(128)S(1)}, s32[4]{0:T(128)}, u32[]{:S(2)}) copy-start(s32[4]{0:T(128)} %param.17) | copy-start | bytes 52
  7.2 7.1 %copy-start.7 = (f32[256]{0:T(256)S(1)}, f32[256]{0:T(256)}, u32[]{:S(2)}) copy-start(f32[256]{0:T(256)} %param.12) | copy-start | bytes 3076
  7.2 7.1 %copy-start.8 = (f32[256]{0:T(256)S(1)}, f32[256]{0:T(256)}, u32[]{:S(2)}) copy-start(f32[256]{0:T(256)} %param.11) | copy-start | bytes 3076
  7.2 189.7 %all-gather.4.cloned.1.call-start = ((), (), s32[]{:S(2)}) async-start(), calls=%async_computation.5 | async-start | bytes 5242880 | tf_op jit(solution)/shard_map/all_gather | solution.py:940
  10.5 316.4 %all-gather.8.cloned.1.call-start = ((), (), s32[]{:S(2)}) async-start(), calls=%async_computation.7 | async-start | bytes 3604480 | tf_op jit(solution)/shard_map/all_gather | solution.py:942
  11.2 315.7 %all-gather.6.cloned.1.call-start = ((), (), s32[]{:S(2)}) async-start(), calls=%async_computation.6 | async-start | bytes 7208960 | tf_op jit(solution)/shard_map/all_gather | solution.py:941
  12.0 382.4 %reduce-scatter.12.cloned.1.call-start = ((), (), s32[]{:S(2)}) async-start(), calls=%async_computation.11 | async-start | bytes 1310720 | tf_op jit(solution)/shard_map/reduce_scatter | solution.py:951
  14.9 158.3 %copy-start.6 = (s32[4]{0:T(128)S(1)}, s32[4]{0:T(128)}, u32[]{:S(2)}) copy-start(s32[4]{0:T(128)} %get-tuple-element.54) | copy-start | bytes 52
  14.9 158.4 %copy-start.5 = (s32[4]{0:T(128)S(1)}, s32[4]{0:T(128)}, u32[]{:S(2)}) copy-start(s32[4]{0:T(128)} %param.17) | copy-start | bytes 52
  14.9 159.2 %copy-start.12 = (s32[4,1024]{1,0:T(4,128)S(1)}, s32[4,1024]{1,0:T(4,128)}, u32[]{:S(2)}) copy-start(s32[4,1024]{1,0:T(4,128)} %param.18) | copy-start | bytes 49156
  14.9 163.2 %copy-start.3 = (s32[4]{0:T(128)S(1)}, s32[4]{0:T(128)}, u32[]{:S(2)}) copy-start(s32[4]{0:T(128)} %get-tuple-element.55) | copy-start | bytes 52
  173.1 6.8 %copy-start.9 = (f32[64]{0:T(128)S(1)}, f32[64]{0:T(128)}, u32[]{:S(2)}) copy-start(f32[64]{0:T(128)} %pad.8.clone) | copy-start | bytes 772
  173.1 6.8 %copy-start.10 = (f32[64]{0:T(128)S(1)}, f32[64]{0:T(128)}, u32[]{:S(2)}) copy-start(f32[64]{0:T(128)} %pad.10.clone) | copy-start | bytes 772
  173.2 6.7 %copy-start.11 = (f32[64]{0:T(128)S(1)}, f32[64]{0:T(128)}, u32[]{:S(2)}) copy-start(f32[64]{0:T(128)} %pad.13.clone) | copy-start | bytes 772
  186.0 6.9 %copy-start.1 = (pred[4096,1]{1,0:T(8,128)(4,1)S(1)}, pred[4096,1]{1,0:T(8,128)(4,1)}, u32[]{:S(2)}) copy-start(pred[4096,1]{1,0:T(8,128)(4,1)} %copy.43) | copy-start | bytes 12292
  304.9 303.8 %reduce-scatter.6.cloned.1.call-start = ((), (), s32[]{:S(2)}) async-start(), calls=%async_computation.8 | async-start | bytes 3932160 | tf_op jit(solution)/shard_map/reduce_scatter | solution.py:951
  326.7 284.4 %reduce-scatter.8.cloned.1.call-start = ((), (), s32[]{:S(2)}) async-start(), calls=%async_computation.9 | async-start | bytes 3604480 | tf_op jit(solution)/shard_map/reduce_scatter | solution.py:951
  394.3 216.8 %reduce-scatter.10.cloned.1.call-start = ((), (), s32[]{:S(2)}) async-start(), calls=%async_computation.10 | async-start | bytes 3604480 | tf_op jit(solution)/shard_map/reduce_scatter | solution.py:951
  415.4 199.0 %reduce-scatter.14.cloned.1.call-start = ((), (), s32[]{:S(2)}) async-start(), calls=%async_computation.12 | async-start | bytes 3604480 | tf_op jit(solution)/shard_map/reduce_scatter | solution.py:951
  611.1 5.8 copy-start.2
  614.4 3.9 copy-start
Sparse Core Ops, SparseCore 0:
  10.6 83.4 all-gather.3
  95.7 57.6 all-gather.7
  155.0 105.4 all-gather.5
  305.0 25.1 reduce-scatter.11
  333.1 58.8 reduce-scatter.5
  394.4 55.9 reduce-scatter.7
  453.5 56.0 reduce-scatter.9
  511.9 56.0 reduce-scatter.13

commit v2 on v1

v2 whole, which is shorter than its diff:
```python
import functools

import jax
import jax.numpy as jnp
import numpy as np
from jax import lax
from jax.experimental import pallas as pl
from jax.experimental.pallas import tpu as pltpu
from jax.sharding import PartitionSpec as P

D = 2048
HD = 64
ROT = 16
LEN = 1024
IMG = 256
QB = 256
MB = 512
RB = 256
GB = 512
SUMS = 4


NORM_EPS = 1e-05
MESH = pl.DeviceIdType.MESH
MASKED_SCORE = -1e30
ROPE_BASE = 10000.0
NT = (((1,), (1,)), ((), ()))


def contract(left, right, left_dim, right_dim):
    return lax.dot_general(
        left, right, (((left_dim,), (right_dim,)), ((), ())), preferred_element_type=jnp.float32
    )


def rope_rows():
    half = ROT // 2
    inv_freq = np.float32(ROPE_BASE) ** (np.float32(-2.0 / ROT) * np.arange(half, dtype=np.float32))
    angles = np.arange(LEN, dtype=np.float32)[None, :] * inv_freq[:, None]
    wide = angles.astype(np.float64)
    return np.concatenate([np.cos(wide), np.sin(wide)]).astype(np.float32)


def fill_tables(rows_ref, tables):
    half = ROT // 2
    for i in range(LEN // QB):
        sl = pl.ds(i * QB, QB)
        cosines, sines = rows_ref[:half, sl], rows_ref[half:, sl]
        zero = jnp.zeros_like(sines)
        rest = [zero] * (HD // half - 2)
        ones = [jnp.ones_like(sines)] * (HD // half - 2)
        tables[0, sl, :] = jnp.concatenate([cosines, cosines, *ones] * (128 // HD), axis=0).T
        tables[1, sl, :] = jnp.concatenate([-sines, zero, *rest] * (128 // HD), axis=0).T
        tables[2, sl, :] = jnp.concatenate([zero, sines, *rest] * (128 // HD), axis=0).T


def turn(x, tables, sl, sign):
    width = x.shape[1]
    c, a, b = (jnp.concatenate([tables[k, sl, :]] * (width // 128), axis=1) for k in range(3))
    left = pltpu.roll(x, width - ROT // 2, 1)
    right = pltpu.roll(x, ROT // 2, 1)
    return x * c + (left * a + right * b) * sign


class Attention:
    def __init__(self, heads, scratch):
        self.heads, self.width = heads, heads * HD
        (
            self.tables,
            self.span,
            self.data,
            self.kt,
            self.vt,
            self.s,
            self.d,
            self.e,
            self.bias,
            self.m,
            self.l,
            self.x,
            self.ot,
            self.dqt,
            self.dk,
            self.dv,
        ) = scratch

    @staticmethod
    def scratch(heads):
        f32, bf16, blocks, width = jnp.float32, jnp.bfloat16, LEN // QB, heads * HD
        return [
            pltpu.VMEM((3, LEN, 128), f32),
            pltpu.VMEM((blocks, 8, QB), jnp.int32),
            pltpu.VMEM((LEN, 4 * width), bf16),
            pltpu.VMEM((blocks, width, QB), bf16),
            pltpu.VMEM((blocks, width, QB), bf16),
            pltpu.VMEM((blocks, heads, QB, QB), f32),
            pltpu.VMEM((blocks, heads, QB, QB), f32),
            pltpu.VMEM((blocks, heads, QB, QB), bf16),
            pltpu.VMEM((QB, QB), f32),
            pltpu.VMEM((heads, 8, QB), f32),
            pltpu.VMEM((heads, 8, QB), f32),
            pltpu.VMEM((heads, 8, QB), f32),
            pltpu.VMEM((width, QB), f32),
            pltpu.VMEM((width, QB), f32),
            pltpu.VMEM((LEN, width), f32),
            pltpu.VMEM((LEN, width), f32),
        ]

    def part(self, kind):
        return pl.ds(kind * self.width, self.width)

    def begin(self, doc_ref, seq, start, x_ref, g_ref, w_ref):
        f32, bf16, width = jnp.float32, jnp.bfloat16, self.width
        docs = doc_ref[pl.ds(seq, 1), :].astype(f32)
        down = jnp.broadcast_to(docs, (128, LEN)).T[:, :1]
        for i in range(LEN // QB):
            own = docs[:, i * QB : (i + 1) * QB]
            first = jnp.sum((down < own).astype(jnp.int32), axis=0, keepdims=True)
            last = jnp.sum((down <= own).astype(jnp.int32), axis=0, keepdims=True) - 1
            at = lax.broadcasted_iota(jnp.int32, (1, QB), 1) + i * QB
            inside = (at >= start) & (at < start + IMG)
            self.span[i, 0:1, :] = first
            self.span[i, 1:2, :] = jnp.where(inside, jnp.minimum(last, start + IMG - 1), at)

        def block(i, _):
            sl = pl.ds(pl.multiple_of(i * QB, QB), QB)
            x = x_ref[sl, :]
            q = jnp.dot(x, w_ref[:, :width], preferred_element_type=f32)
            k = jnp.dot(x, w_ref[:, width : 2 * width], preferred_element_type=f32)
            v = jnp.dot(x, w_ref[:, 2 * width : 3 * width], preferred_element_type=f32)
            g = jnp.dot(g_ref[sl, :], w_ref[:, 3 * width :], preferred_element_type=f32)
            q = turn(q, self.tables, sl, 1.0).astype(bf16).astype(f32) * HD**-0.5
            k = turn(k, self.tables, sl, 1.0).astype(bf16)
            self.data[sl, self.part(0)] = q.astype(bf16)
            self.data[sl, self.part(1)] = k
            self.data[sl, self.part(2)] = v.astype(bf16)
            self.data[sl, self.part(3)] = g.astype(bf16)
            self.kt[i] = k.astype(f32).T.astype(bf16)
            self.vt[i] = v.T.astype(bf16)
            return 0

        lax.fori_loop(0, LEN // QB, block, 0)
        self.dk[...] = jnp.zeros_like(self.dk)
        self.dv[...] = jnp.zeros_like(self.dv)

    def bounds(self, i):
        return jnp.min(self.span[i, 0:1, :]) // QB, jnp.max(self.span[i, 1:2, :]) // QB

    def query_block(self, i, low, high, att_ref, gp_ref):
        f32, bf16, heads, width = jnp.float32, jnp.bfloat16, self.heads, self.width
        rows = pl.ds(pl.multiple_of(i * QB, QB), QB)
        lane = lax.broadcasted_iota(jnp.int32, (1, width), 1) // HD
        first, final = self.span[i, 0:1, :], self.span[i, 1:2, :]
        q, g = self.data[rows, self.part(0)], self.data[rows, self.part(3)]
        zero = jnp.zeros_like(q)
        q_own = [jnp.where(lane == h, q, zero) for h in range(heads)]
        g_own = [jnp.where(lane == h, g, zero) for h in range(heads)]
        self.m[...] = jnp.full_like(self.m, MASKED_SCORE)

        def fold(x, op):
            out = x[:8]
            for r in range(8, QB, 8):
                out = op(out, x[r : r + 8])
            return out

        def score(kb, _):
            keys = pl.ds(pl.multiple_of(kb * QB, QB), QB)
            k, v = self.data[keys, self.part(1)], self.data[keys, self.part(2)]
            at = lax.broadcasted_iota(jnp.int32, (QB, QB), 0) + kb * QB
            self.bias[...] = jnp.where((at >= first) & (at <= final), 0.0, MASKED_SCORE)
            for h in range(heads):
                s = lax.dot_general(k, q_own[h], NT, preferred_element_type=f32) + self.bias[...]
                self.s[kb, h] = s
                self.m[h] = jnp.maximum(self.m[h], fold(s, jnp.maximum))
                self.d[kb, h] = lax.dot_general(v, g_own[h], NT, preferred_element_type=f32)
            return 0

        lax.fori_loop(low, high + 1, score, 0)
        for h in range(heads):
            self.m[h] = jnp.broadcast_to(jnp.max(self.m[h], axis=0, keepdims=True), (8, QB))
        self.l[...] = jnp.zeros_like(self.l)
        self.x[...] = jnp.zeros_like(self.x)
        self.ot[...] = jnp.zeros_like(self.ot)
        self.dqt[...] = jnp.zeros_like(self.dqt)

        def expo(kb, _):
            for h in range(heads):
                hs = slice(h * HD, (h + 1) * HD)
                e = jnp.exp(self.s[kb, h] - self.m[h, 0:1, :])
                self.l[h] += fold(e, jnp.add)
                self.x[h] += fold(e * self.d[kb, h], jnp.add)
                e = e.astype(bf16)
                self.e[kb, h] = e
                self.ot[hs, :] += jnp.dot(self.vt[kb, hs, :], e, preferred_element_type=f32)
            return 0

        lax.fori_loop(low, high + 1, expo, 0)
        for h in range(heads):
            inv = 1.0 / jnp.sum(self.l[h], axis=0, keepdims=True)
            self.l[h] = jnp.broadcast_to(inv, (8, QB))
            delta = jnp.sum(self.x[h], axis=0, keepdims=True) * inv
            self.x[h] = jnp.broadcast_to(delta, (8, QB))

        def back(kb, _):
            keys = pl.ds(pl.multiple_of(kb * QB, QB), QB)
            dk = self.dk[keys, :]
            dv = self.dv[keys, :]
            for h in range(heads):
                hs = slice(h * HD, (h + 1) * HD)
                p = self.e[kb, h].astype(f32) * self.l[h, 0:1, :]
                ds = (p * (self.d[kb, h] - self.x[h, 0:1, :])).astype(bf16)
                dv += jnp.dot(p.astype(bf16), g_own[h], preferred_element_type=f32)
                dk += jnp.dot(ds, q_own[h], preferred_element_type=f32)
                self.dqt[hs, :] += jnp.dot(self.kt[kb, hs, :], ds, preferred_element_type=f32)
            self.dk[keys, :] = dk
            self.dv[keys, :] = dv
            return 0

        lax.fori_loop(low, high + 1, back, 0)
        for h in range(heads):
            hs = slice(h * HD, (h + 1) * HD)
            self.ot[hs, :] = self.ot[hs, :] * self.l[h, 0:1, :]
        att_ref[rows, :] = self.ot[...].T.astype(bf16)
        dq = self.dqt[...].T * HD**-0.5
        gp_ref[rows, :width] = turn(dq, self.tables, rows, -1.0).astype(bf16)

    def finish(self, gp_ref):
        width = self.width

        def block(i, _):
            sl = pl.ds(pl.multiple_of(i * QB, QB), QB)
            dk = turn(self.dk[sl, :], self.tables, sl, -1.0)
            gp_ref[sl, width : 2 * width] = dk.astype(jnp.bfloat16)
            gp_ref[sl, 2 * width :] = self.dv[sl, :].astype(jnp.bfloat16)
            return 0

        lax.fori_loop(0, LEN // QB, block, 0)


def attention_kernel(
    heads, first, start_ref, x_ref, g_ref, w_ref, doc_ref, rope_ref, *refs
):
    att_ref, gp_ref = refs[2:4]
    seq = pl.program_id(0) + first
    attend = Attention(heads, refs[4:])

    @pl.when(pl.program_id(0) == 0)
    def _():
        fill_tables(rope_ref, attend.tables)

    attend.begin(doc_ref, seq, start_ref[seq], x_ref, g_ref, w_ref)

    def query_block(i, _):
        attend.query_block(i, *attend.bounds(i), att_ref, gp_ref)
        return 0

    lax.fori_loop(0, LEN // QB, query_block, 0)
    attend.finish(gp_ref)


def attention(first, normed, grad, weights, image_start, doc_ids, earlier):
    rows, width = normed.shape[0], weights.shape[1] // 4
    count, heads = rows // LEN, width // HD
    bf16 = jnp.bfloat16
    seq_rows = lambda s, *_: (s + first, 0)
    fixed = lambda s, *_: (0, 0)
    return pl.pallas_call(
        functools.partial(attention_kernel, heads, first),
        out_shape=[jax.ShapeDtypeStruct(e.shape, bf16) for e in earlier],
        grid_spec=pltpu.PrefetchScalarGridSpec(
            num_scalar_prefetch=1,
            grid=(count - first,),
            in_specs=[
                pl.BlockSpec((LEN, D), seq_rows),
                pl.BlockSpec((LEN, D), seq_rows),
                pl.BlockSpec((D, 4 * width), fixed, pipeline_mode=pl.Buffered(1)),
                pl.BlockSpec((count, LEN), fixed),
                pl.BlockSpec((ROT, LEN), fixed),
                pl.BlockSpec(memory_space=pl.ANY),
                pl.BlockSpec(memory_space=pl.ANY),
            ],
            out_specs=[
                pl.BlockSpec((LEN, width), seq_rows),
                pl.BlockSpec((LEN, 3 * width), seq_rows),
            ],
            scratch_shapes=Attention.scratch(heads),
        ),
        input_output_aliases={6: 0, 7: 1},
        compiler_params=pltpu.CompilerParams(
            dimension_semantics=("arbitrary",), vmem_limit_bytes=56 << 20
        ),
        cost_estimate=pl.CostEstimate(
            flops=(count - first) * LEN * (36 * 640 * width + 8 * D * width),
            bytes_accessed=(count - first) * LEN * (width * 8 + 4 * D) + 8 * D * width,
            transcendentals=(count - first) * LEN * 640 * heads,
        ),
        name="attention",
    )(image_start, normed, grad, weights, doc_ids, jnp.asarray(rope_rows()), *earlier)


def ffn_kernel(x_ref, g_ref, wgu_ref, wd_ref, hidden_ref, gg_ref, gu_ref):
    f32, bf16 = jnp.float32, jnp.bfloat16
    x = x_ref[...]
    gate = lax.dot_general(x, wgu_ref[0], NT, preferred_element_type=f32)
    up = lax.dot_general(x, wgu_ref[1], NT, preferred_element_type=f32)
    grad = lax.dot_general(g_ref[...], wd_ref[...], NT, preferred_element_type=f32)
    sigma = jax.nn.sigmoid(gate)
    silu = gate * sigma
    hidden_ref[...] = (silu * up).astype(bf16)
    gg_ref[...] = (grad * up * (sigma + silu * (1.0 - sigma))).astype(bf16)
    gu_ref[...] = (grad * silu).astype(bf16)


def feed_forward(normed, grad, wgu, wd):
    rows, ffn = normed.shape[0], wd.shape[0]
    block = lambda i: (i, 0)
    return pl.pallas_call(
        ffn_kernel,
        out_shape=[jax.ShapeDtypeStruct((rows, ffn), jnp.bfloat16)] * 3,
        grid=(rows // MB,),
        in_specs=[
            pl.BlockSpec((MB, D), block),
            pl.BlockSpec((MB, D), block),
            pl.BlockSpec((2, ffn, D), lambda i: (0, 0, 0), pipeline_mode=pl.Buffered(1)),
            pl.BlockSpec((ffn, D), lambda i: (0, 0), pipeline_mode=pl.Buffered(1)),
        ],
        out_specs=[pl.BlockSpec((MB, ffn), block)] * 3,
        compiler_params=pltpu.CompilerParams(
            dimension_semantics=("arbitrary",), vmem_limit_bytes=56 << 20
        ),
        cost_estimate=pl.CostEstimate(
            flops=6 * rows * D * ffn,
            bytes_accessed=rows * (4 * D + 6 * ffn) + 6 * D * ffn,
            transcendentals=rows * ffn,
        ),
        name="feed_forward",
    )(normed, grad, wgu, wd)


def flip(index, bits):
    bit = 1
    while bit <= bits:
        if bits & bit:
            index = index + bit - 2 * bit * ((index // bit) % 2)
        bit *= 2
    return index


def chip_orders(ways):
    bits = [1 << k for k in range(1, ways.bit_length() - 1)]
    return bits, bits[::-1]


def held(bits):
    found = [0]
    for bit in bits:
        found += [o ^ bit for o in found]
    return found


def meet(peers):
    barrier = pltpu.get_barrier_semaphore()
    for peer in peers:
        pl.semaphore_signal(barrier, inc=1, device_id=peer, device_id_type=MESH)
    pl.semaphore_wait(barrier, len(peers))


def gather_kernel(ways, base, attended, *refs):
    f32, bf16 = jnp.float32, jnp.bfloat16
    me = lax.axis_index("col")
    if attended:
        (token_ref, cot_ref, vectors_ref, w_ref, rope_ref, doc_ref, image_ref, old_ref) = refs[:8]
        (old_normed, old_grad, normed_ref, full_ref, stat_ref, att_ref, gp_ref) = refs[8:15]
        refs = refs[15:]
    else:
        (token_ref, cot_ref, vector_ref, normed_ref, full_ref, stat_ref, vectors_ref) = refs[:7]
        refs = refs[7:]
    (both, load_sem, store_sem, full_sem, send_sem, recv_sem) = refs[:6]
    refs = refs[6:]
    width = token_ref.shape[1]
    rows = both.shape[1]
    pairs = rows // GB
    orders = chip_orders(ways)
    phases = len(orders[0])
    mine = pl.ds(pl.multiple_of(me * width, width), width)
    source = pl.ds(base, rows)
    loads = [
        pltpu.make_async_copy(token_ref.at[source], both.at[me, :, pl.ds(0, width)], load_sem.at[0]),
        pltpu.make_async_copy(cot_ref.at[source], both.at[me, :, pl.ds(width, width)], load_sem.at[1]),
    ]
    for load in loads:
        load.start()
    peers = [flip(me, k) for k in range(1, ways)]
    if attended:
        meet([{"col": flip(me, 1 << k)} for k in range(ways.bit_length() - 1)])
    else:
        vectors_ref[:, mine] = vector_ref[...]
        meet([{"col": peer} for peer in peers])

    def vector_copy(k):
        return pltpu.make_async_remote_copy(
            src_ref=vectors_ref.at[:, mine],
            dst_ref=vectors_ref.at[:, mine],
            send_sem=refs[0].at[k],
            recv_sem=refs[1].at[k],
            device_id={"col": peers[k]},
            device_id_type=MESH,
        )

    def copies(p, phase):
        for k, order in enumerate(orders):
            bit = order[phase] if phase < phases else 1
            place = pl.ds(pl.multiple_of(p * GB + k * (GB // 2), GB // 2), GB // 2)
            for o in held(order[:phase]):
                index = k * ways + (o ^ bit)
                owner = flip(me, o)
                yield pltpu.make_async_remote_copy(
                    src_ref=both.at[owner, place],
                    dst_ref=both.at[owner, place],
                    send_sem=send_sem.at[p, index],
                    recv_sem=recv_sem.at[p, index],
                    device_id={"col": flip(me, bit)},
                    device_id_type=MESH,
                )

    def start(p, phase):
        for copy in copies(p, phase):
            copy.start()

    def arrive(p, phase):
        for copy in copies(p, phase):
            copy.wait_recv()

    def filed(p, first, out_ref, sem):
        place = pl.ds(pl.multiple_of(p * GB, GB), GB)
        goal = pl.ds(pl.multiple_of(base + p * GB, GB), GB)
        for b in range(ways):
            pltpu.make_async_copy(
                both.at[b, place, pl.ds(first, width)],
                out_ref.at[goal, pl.ds(b * width, width)],
                sem.at[p],
            ).start()

    def filed_wait(p, out_ref, sem):
        place = out_ref.at[pl.ds(base + p * GB, GB)]
        pltpu.make_async_copy(place, place, sem.at[p]).wait()

    def norm(p):
        filed(p, width, full_ref, full_sem)
        for phase in range(phases + 1):
            for copy in copies(p, phase):
                copy.wait_send()

        def block(j, _):
            at = pl.ds(pl.multiple_of(p * GB + j * QB, QB), QB)
            goal = pl.ds(pl.multiple_of(base + p * GB + j * QB, QB), QB)
            sums = sum(both[b, at, :width].astype(f32) for b in range(ways))
            mean = jnp.sum(sums, axis=1, keepdims=True) / D
            squares = jnp.zeros((QB, width), f32)
            for b in range(ways):
                x = both[b, at, :width].astype(f32) - mean
                squares += x * x
            inv = lax.rsqrt(jnp.sum(squares, axis=1, keepdims=True) / D + NORM_EPS)
            stat_ref[goal, :1] = mean
            stat_ref[goal, 1:] = inv
            for b in range(ways):
                cols = slice(b * width, (b + 1) * width)
                x = (both[b, at, :width].astype(f32) - mean) * inv
                x = x * vectors_ref[0:1, cols] + vectors_ref[1:2, cols]
                both[b, at, :width] = x.astype(bf16)
            return 0

        lax.fori_loop(0, GB // QB, block, 0)
        filed(p, 0, normed_ref, store_sem)

    if attended:
        x_scr, g_scr, att_scr, gp_scr, in_sem, out_sem = refs[:6]
        attend = Attention(width // HD, refs[6:])
        stat_ref[pl.ds(0, base), :] = old_ref[pl.ds(0, base), :]

        def fetch(seq):
            place = pl.ds(pl.multiple_of(seq * LEN, LEN), LEN)
            return [
                pltpu.make_async_copy(old_normed.at[place], x_scr, in_sem.at[seq, 0]),
                pltpu.make_async_copy(old_grad.at[place], g_scr, in_sem.at[seq, 1]),
            ]

        def give(seq):
            place = pl.ds(pl.multiple_of(seq * LEN, LEN), LEN)
            return [
                pltpu.make_async_copy(att_scr.at[seq], att_ref.at[place], out_sem.at[seq, 0]),
                pltpu.make_async_copy(gp_scr.at[seq], gp_ref.at[place], out_sem.at[seq, 1]),
            ]

        for move in fetch(0):
            move.start()

    for load in loads:
        load.wait()
    start(0, 0)
    start(1, 0)
    if attended:
        fill_tables(rope_ref, attend.tables)
    else:
        for k in range(ways - 1):
            vector_copy(k).start()
        for k in range(ways - 1):
            vector_copy(k).wait_recv()
    blocks = LEN // QB
    turns = attended * blocks // pairs if attended else 0

    def step(p, _):
        for phase in range(phases):
            arrive(p, phase)
            start(p, phase + 1)
            if phase == 0:
                pl.when(p + 2 < pairs)(lambda: start(p + 2, 0))

                @pl.when(p >= 1)
                def _():
                    arrive(p - 1, phases)
                    norm(p - 1)

                if attended:
                    seq = p * turns // blocks
                    spot = p * turns % blocks

                    @pl.when(spot == 0)
                    def _():
                        for move in fetch(seq):
                            move.wait()
                        attend.begin(doc_ref, seq, image_ref[seq], x_scr, g_scr, w_ref)

                        @pl.when(seq + 1 < attended)
                        def _():
                            for move in fetch(seq + 1):
                                move.start()

                    def query_block(i, _):
                        low = i // (blocks - 1)
                        attend.query_block(i, low, i + 1 - low, att_scr.at[seq], gp_scr.at[seq])
                        return 0

                    lax.fori_loop(spot, spot + turns, query_block, 0)

                    @pl.when(spot + turns == blocks)
                    def _():
                        attend.finish(gp_scr.at[seq])
                        for move in give(seq):
                            move.start()
        return 0

    lax.fori_loop(0, pairs, step, 0)
    arrive(pairs - 1, phases)
    norm(pairs - 1)
    for p in range(pairs):
        filed_wait(p, full_ref, full_sem)
        filed_wait(p, normed_ref, store_sem)
    if attended:
        for seq in range(attended):
            for move in give(seq):
                move.wait()
    else:
        for k in range(ways - 1):
            vector_copy(k).wait_send()


def gather_scratch(ways, rows, width):
    dma = pltpu.SemaphoreType.DMA
    pairs = rows // GB
    return [
        pltpu.VMEM((ways, rows, 2 * width), jnp.bfloat16),
        dma((2,)),
        dma((pairs,)),
        dma((pairs,)),
        dma((pairs, 2 * ways)),
        dma((pairs, 2 * ways)),
    ]


def gather_first(tokens, out_grad, vectors, count, ways):
    rows, width = tokens.shape
    bf16, f32 = jnp.bfloat16, jnp.float32
    anywhere = pl.BlockSpec(memory_space=pl.ANY)
    vmem = pl.BlockSpec(memory_space=pltpu.VMEM)
    dma = pltpu.SemaphoreType.DMA
    return pl.pallas_call(
        functools.partial(gather_kernel, ways, 0, 0),
        out_shape=[
            jax.ShapeDtypeStruct((rows, D), bf16),
            jax.ShapeDtypeStruct((rows, D), bf16),
            jax.ShapeDtypeStruct((rows, 2), f32),
            jax.ShapeDtypeStruct((8, D), f32),
        ],
        in_specs=[anywhere, anywhere, vmem],
        out_specs=[anywhere, anywhere, vmem, vmem],
        scratch_shapes=[*gather_scratch(ways, count, width), dma((ways - 1,)), dma((ways - 1,))],
        compiler_params=pltpu.CompilerParams(
            collective_id=0, has_side_effects=True, vmem_limit_bytes=40 << 20
        ),
        cost_estimate=pl.CostEstimate(
            flops=100 * count * D * D // ways, bytes_accessed=count * D * 8, transcendentals=0
        ),
        name="gather_first",
    )(tokens, out_grad, vectors)


def gather_rest(tokens, out_grad, vectors, weights, doc_ids, image_start, stats, normed, grad, ways):
    rows, width = tokens.shape
    count = rows // 2
    bf16, f32 = jnp.bfloat16, jnp.float32
    anywhere = pl.BlockSpec(memory_space=pl.ANY)
    vmem = pl.BlockSpec(memory_space=pltpu.VMEM)
    dma = pltpu.SemaphoreType.DMA
    seqs = count // LEN
    return pl.pallas_call(
        functools.partial(gather_kernel, ways, count, seqs),
        out_shape=[
            jax.ShapeDtypeStruct((rows, D), bf16),
            jax.ShapeDtypeStruct((rows, D), bf16),
            jax.ShapeDtypeStruct((rows, 2), f32),
            jax.ShapeDtypeStruct((rows, width), bf16),
            jax.ShapeDtypeStruct((rows, 3 * width), bf16),
        ],
        in_specs=[
            anywhere,
            anywhere,
            vmem,
            vmem,
            vmem,
            vmem,
            pl.BlockSpec(memory_space=pltpu.SMEM),
            vmem,
            anywhere,
            anywhere,
        ],
        out_specs=[anywhere, anywhere, vmem, anywhere, anywhere],
        input_output_aliases={8: 0, 9: 1},
        scratch_shapes=[
            *gather_scratch(ways, rows - count, width),
            pltpu.VMEM((LEN, D), bf16),
            pltpu.VMEM((LEN, D), bf16),
            pltpu.VMEM((seqs, LEN, width), bf16),
            pltpu.VMEM((seqs, LEN, 3 * width), bf16),
            dma((seqs, 2)),
            dma((seqs, 2)),
            *Attention.scratch(width // HD),
        ],
        compiler_params=pltpu.CompilerParams(
            collective_id=3, has_side_effects=True, vmem_limit_bytes=60 << 20
        ),
        cost_estimate=pl.CostEstimate(
            flops=100 * count * D * D // ways, bytes_accessed=count * D * 8, transcendentals=0
        ),
        name="gather_rest",
    )(tokens, out_grad, vectors, weights, jnp.asarray(rope_rows()), doc_ids, image_start, stats, normed, grad)


class Reducer:
    def __init__(self, ways, parts, inbox, send_sem, recv_sem):
        self.ways, self.parts, self.inbox = ways, parts, inbox
        self.send_sem, self.recv_sem = send_sem, recv_sem
        self.me = lax.axis_index("col")
        self.orders = chip_orders(ways)
        self.phases = 1 + len(self.orders[0])

    def moves(self, step, phase):
        halves = [None] if phase == 0 else [0, 1]
        for k in halves:
            order = [1] if phase == 0 else [1, *self.orders[k]]
            bit = order[phase]
            done = sum(order[:phase])
            count = RB if k is None else RB // 2
            rows = pl.ds(pl.multiple_of(step * RB + (k or 0) * count, count), count)
            for o in range(self.ways):
                if o & done or not o & bit:
                    continue
                goal = o ^ bit
                slot = slot_of(self.ways, self.orders, phase, k, goal)
                sem = 2 * slot + (k or 0)
                copy = pltpu.make_async_remote_copy(
                    src_ref=self.parts.at[o, rows],
                    dst_ref=self.inbox.at[slot, rows],
                    send_sem=self.send_sem.at[step, sem],
                    recv_sem=self.recv_sem.at[step, sem],
                    device_id={"col": flip(self.me, bit)},
                    device_id_type=MESH,
                )
                yield copy, goal, slot, rows

    def send(self, step, phase):
        for copy, *_ in self.moves(step, phase):
            copy.start()

    def absorb(self, step, phase):
        out = []
        for copy, goal, slot, rows in self.moves(step, phase):
            copy.wait_recv()
            value = self.parts[goal, rows, :].astype(jnp.float32)
            value += self.inbox[slot, rows, :].astype(jnp.float32)
            if phase == self.phases - 1:
                out.append(value)
            else:
                self.parts[goal, rows, :] = value.astype(jnp.bfloat16)
        return out

    def finish(self, step):
        for phase in range(self.phases):
            for copy, *_ in self.moves(step, phase):
                copy.wait_send()

    def advance(self, t, steps, lags):
        pl.when(t < steps)(lambda: self.send(t, 0))
        for phase in range(self.phases - 1):
            s = t - lags[phase]

            @pl.when((s >= 0) & (s < steps))
            def _():
                self.absorb(s, phase)
                self.send(s, phase + 1)


def slot_of(ways, orders, phase, half, goal):
    if phase == 0:
        return goal // 2
    order = [1, *orders[half]]
    base = ways // 2
    for p in range(1, phase):
        base += ways >> (p + 1)
    goals = [g for g in range(ways) if not g & sum(order[: phase + 1])]
    return base + goals.index(goal)


def lags_of(ways):
    return [1 + 2 * p for p in range(len(chip_orders(ways)[0]) + 1)]


def reducer_scratch(ways, rows, width):
    steps = rows // RB
    return [
        pltpu.VMEM((ways, rows, width), jnp.bfloat16),
        pltpu.VMEM((ways - 1, rows, width), jnp.bfloat16),
        pltpu.SemaphoreType.DMA((steps, 2 * ways)),
        pltpu.SemaphoreType.DMA((steps, 2 * ways)),
    ]


def branch_kernel(
    ways,
    steps,
    att_ref,
    hidden_ref,
    grad_ref,
    token_ref,
    wout_ref,
    wd_ref,
    out_ref,
    wgrad_ref,
    parts,
    inbox,
    send_sem,
    recv_sem,
    acc,
):
    f32, bf16 = jnp.float32, jnp.bfloat16
    t = pl.program_id(0)
    me, width = lax.axis_index("col"), D // ways
    lags = lags_of(ways)
    ring = Reducer(ways, parts, inbox, send_sem, recv_sem)

    @pl.when(t == 0)
    def _():
        acc[...] = jnp.zeros_like(acc)
        meet([{"col": flip(me, 1 << k)} for k in range(ways.bit_length() - 1)])

    @pl.when(t < steps)
    def _():
        rows = pl.ds(pl.multiple_of(t * RB, RB), RB)
        att, hidden = att_ref[...], hidden_ref[...]
        for o in range(ways):
            cols = pl.ds(pl.multiple_of(flip(me, o) * width, width), width)
            total = lax.dot_general(att, wout_ref[cols, :], NT, preferred_element_type=f32)
            total += jnp.dot(hidden, wd_ref[:, cols], preferred_element_type=f32)
            parts[o, rows, :] = total.astype(bf16)

    ring.advance(t, steps, lags)

    @pl.when(t < steps)
    def _():
        acc[...] += contract(hidden_ref[...], grad_ref[...], 0, 0)

    @pl.when(t == steps)
    def _():
        wgrad_ref[...] = acc[...].astype(bf16)

    s = t - lags[-1]

    @pl.when(s >= 0)
    def _():
        for k, value in enumerate(ring.absorb(s, ring.phases - 1)):
            half = slice(k * (RB // 2), (k + 1) * (RB // 2))
            out_ref[half, :] = (token_ref[half, :].astype(f32) + value).astype(bf16)
        ring.finish(s)


def branches(att, hidden, grad, tokens, weights, wd, ways):
    rows, width = tokens.shape
    ffn = wd.shape[0]
    steps = rows // RB
    lag = lags_of(ways)[-1]
    now = lambda t: (jnp.minimum(t, steps - 1), 0)
    late = lambda t: (jnp.maximum(t - lag, 0), 0)
    fixed = lambda t: (0, 0)
    once = pl.Buffered(1)
    return pl.pallas_call(
        functools.partial(branch_kernel, ways, steps),
        out_shape=[
            jax.ShapeDtypeStruct((rows, width), jnp.bfloat16),
            jax.ShapeDtypeStruct((ffn, D), jnp.bfloat16),
        ],
        grid=(steps + lag,),
        in_specs=[
            pl.BlockSpec((RB, width), now),
            pl.BlockSpec((RB, ffn), now),
            pl.BlockSpec((RB, D), now),
            pl.BlockSpec((RB, width), late),
            pl.BlockSpec((D, width), lambda t: (0, 3), pipeline_mode=once),
            pl.BlockSpec((ffn, D), fixed, pipeline_mode=once),
        ],
        out_specs=[
            pl.BlockSpec((RB, width), late),
            pl.BlockSpec((ffn, D), fixed, pipeline_mode=once),
        ],
        scratch_shapes=[*reducer_scratch(ways, rows, width), pltpu.VMEM((ffn, D), jnp.float32)],
        compiler_params=pltpu.CompilerParams(
            collective_id=1,
            has_side_effects=True,
            dimension_semantics=("arbitrary",),
            vmem_limit_bytes=60 << 20,
        ),
        cost_estimate=pl.CostEstimate(
            flops=8 * rows * D * (2 * ffn + width), bytes_accessed=4 * rows * D, transcendentals=0
        ),
        name="branches",
    )(att, hidden, grad, tokens, weights, wd)


def back_kernel(
    ways,
    lines,
    steps,
    gp_ref,
    gg_ref,
    gu_ref,
    x_ref,
    token_ref,
    cot_ref,
    stat_ref,
    w_ref,
    wgu_ref,
    vectors_ref,
    gain_ref,
    out_ref,
    vgrad_ref,
    parts,
    inbox,
    send_sem,
    recv_sem,
    sums,
    ssend_sem,
    srecv_sem,
    acc,
    vsend_sem,
    vrecv_sem,
):
    f32, bf16 = jnp.float32, jnp.bfloat16
    t = pl.program_id(0)
    me, width = lax.axis_index("col"), D // ways
    line = lax.axis_index("row")
    lags = lags_of(ways)
    ring = Reducer(ways, parts, inbox, send_sem, recv_sem)

    @pl.when(t == 0)
    def _():
        acc[...] = jnp.zeros_like(acc)
        meet(
            [{"col": flip(me, k)} for k in range(1, ways)]
            + [{"row": (line + k) % lines} for k in range(1, lines)]
        )

    def sum_copies(group):
        rows = pl.ds(pl.multiple_of(group * (SUMS * RB), SUMS * RB), SUMS * RB)
        for k in range(1, ways):
            yield pltpu.make_async_remote_copy(
                src_ref=sums.at[0, :, rows],
                dst_ref=sums.at[k, :, rows],
                send_sem=ssend_sem.at[group, k - 1],
                recv_sem=srecv_sem.at[group, k - 1],
                device_id={"col": flip(me, k)},
                device_id_type=MESH,
            )

    @pl.when(t < steps)
    def _():
        rows = pl.ds(pl.multiple_of(t * RB, RB), RB)
        gp, gg, gu = gp_ref[...], gg_ref[...], gu_ref[...]
        plain = jnp.zeros((RB, 1), f32)
        cross = jnp.zeros((RB, 1), f32)
        for o in range(ways):
            cols = pl.ds(pl.multiple_of(flip(me, o) * width, width), width)
            total = jnp.dot(gg, wgu_ref[0, :, cols], preferred_element_type=f32)
            total += jnp.dot(gu, wgu_ref[1, :, cols], preferred_element_type=f32)
            total += lax.dot_general(gp, w_ref[cols, :], NT, preferred_element_type=f32)
            parts[o, rows, :] = total.astype(bf16)
            scaled = x_ref[:, cols].astype(f32) - vectors_ref[1:2, cols]
            plain += jnp.sum(total * vectors_ref[0:1, cols], axis=1, keepdims=True)
            cross += jnp.sum(total * scaled, axis=1, keepdims=True)
        lane = lax.broadcasted_iota(jnp.int32, (RB, 128), 1)
        pair = jnp.where(lane == 0, plain, jnp.where(lane == 1, cross, 0.0))
        sums[0, :, rows] = pair.T[:8]

        @pl.when(t % SUMS == SUMS - 1)
        def _():
            for copy in sum_copies(t // SUMS):
                copy.start()

    ring.advance(t, steps, lags)
    s = t - lags[-1]

    @pl.when(s >= 0)
    def _():
        rows = pl.ds(pl.multiple_of(s * RB, RB), RB)

        @pl.when(s % SUMS == 0)
        def _():
            for copy in sum_copies(s // SUMS):
                copy.wait_recv()

        both = sum(sums[k, :, rows] for k in range(ways)).T
        for k, value in enumerate(ring.absorb(s, ring.phases - 1)):
            half = slice(k * (RB // 2), (k + 1) * (RB // 2))
            inv = stat_ref[half, 1:]
            unit = (token_ref[half, :].astype(f32) - stat_ref[half, :1]) * inv
            scaled = value * gain_ref[0:1, :]
            out_ref[half, :] = cot_ref[half, :].astype(f32) + inv * (
                scaled - both[half, 0:1] / D - unit * (both[half, 1:2] / D)
            )
            acc[0, 0:1, :] += jnp.sum(value * unit, axis=0, keepdims=True)
            acc[0, 1:2, :] += jnp.sum(value, axis=0, keepdims=True)

        @pl.when(s % SUMS == 0)
        def _():
            for copy in sum_copies(s // SUMS):
                copy.wait_send()

        ring.finish(s)

    @pl.when(t == pl.num_programs(0) - 1)
    def _():
        copies = [
            pltpu.make_async_remote_copy(
                src_ref=acc.at[0],
                dst_ref=acc.at[k],
                send_sem=vsend_sem.at[k - 1],
                recv_sem=vrecv_sem.at[k - 1],
                device_id={"row": (line + k) % lines},
                device_id_type=MESH,
            )
            for k in range(1, lines)
        ]
        for copy in copies:
            copy.start()
        for copy in copies:
            copy.wait()
        vgrad_ref[...] = sum(acc[k] for k in range(lines))


def norm_back(gp, gg, gu, normed, tokens, cot, stats, weights, wgu, vectors, own, ways, lines):
    rows, width = tokens.shape
    ffn = gg.shape[1]
    steps = rows // RB
    lag = lags_of(ways)[-1]
    now = lambda t: (jnp.minimum(t, steps - 1), 0)
    late = lambda t: (jnp.maximum(t - lag, 0), 0)
    fixed = lambda t: (0, 0)
    once = pl.Buffered(1)
    dma = pltpu.SemaphoreType.DMA
    return pl.pallas_call(
        functools.partial(back_kernel, ways, lines, steps),
        out_shape=[
            jax.ShapeDtypeStruct((rows, width), jnp.float32),
            jax.ShapeDtypeStruct((8, width), jnp.float32),
        ],
        grid=(steps + lag,),
        in_specs=[
            pl.BlockSpec((RB, 3 * width), now),
            pl.BlockSpec((RB, ffn), now),
            pl.BlockSpec((RB, ffn), now),
            pl.BlockSpec((RB, D), now),
            pl.BlockSpec((RB, width), late),
            pl.BlockSpec((RB, width), late),
            pl.BlockSpec((RB, 2), late),
            pl.BlockSpec((D, 3 * width), fixed, pipeline_mode=once),
            pl.BlockSpec((2, ffn, D), lambda t: (0, 0, 0), pipeline_mode=once),
            pl.BlockSpec((8, D), fixed),
            pl.BlockSpec((8, width), fixed),
        ],
        out_specs=[pl.BlockSpec((RB, width), late), pl.BlockSpec((8, width), fixed)],
        scratch_shapes=[
            *reducer_scratch(ways, rows, width),
            pltpu.VMEM((ways, 8, rows), jnp.float32),
            dma((steps // SUMS, ways - 1)),
            dma((steps // SUMS, ways - 1)),
            pltpu.VMEM((lines, 8, width), jnp.float32),
            dma((lines - 1,)),
            dma((lines - 1,)),
        ],
        compiler_params=pltpu.CompilerParams(
            collective_id=2,
            has_side_effects=True,
            dimension_semantics=("arbitrary",),
            vmem_limit_bytes=61 << 20,
        ),
        cost_estimate=pl.CostEstimate(
            flops=4 * rows * D * (2 * ffn + 3 * width), bytes_accessed=6 * rows * D, transcendentals=0
        ),
        name="norm_back",
    )(gp, gg, gu, normed, tokens, cot, stats, weights, wgu, vectors, own)


def after(value, *others):
    return lax.optimization_barrier((value, others))[0]


def local(
    tokens,
    norm_gain,
    norm_bias,
    qkv_weight,
    gate_up_weight,
    out_weight,
    down_weight,
    image_start,
    doc_ids,
    out_grad,
):
    f32, bf16 = jnp.float32, jnp.bfloat16
    block_rows, width = tokens.shape
    ways = D // width
    lines = D // qkv_weight.shape[0]

    own = jnp.concatenate([qkv_weight[:, k] for k in range(3)] + [out_weight], axis=1)
    weights = lax.all_gather(own, "row", axis=0, tiled=True)
    full_gate_up = lax.all_gather(gate_up_weight, "row", axis=0, tiled=True)
    full_down = lax.all_gather(down_weight, "row", axis=0, tiled=True)
    wgu = jnp.transpose(full_gate_up, (1, 2, 0))
    wd = jnp.transpose(full_down, (1, 0))
    own_vectors = jnp.pad(jnp.stack([norm_gain, norm_bias]), ((0, 6), (0, 0)))

    half = block_rows // 2
    normed, grad, stats, vectors = gather_first(tokens, out_grad, own_vectors, half, ways)
    normed, grad, stats, *earlier = gather_rest(
        tokens, out_grad, vectors, weights, doc_ids, image_start, stats, normed, grad, ways
    )
    attended, grad_projected = attention(
        half // LEN, normed, grad, weights, image_start, doc_ids, earlier
    )

    def weight_sum(grad):
        return lax.psum_scatter(grad, "row", scatter_dimension=0, tiled=True)

    def weight_grad(left, right):
        return contract(left, right, 0, 0).astype(bf16)

    grad_qkv = weight_grad(normed, grad_projected)
    grad_out = weight_grad(grad, attended)
    hidden, grad_gate, grad_up = feed_forward(after(normed, grad_qkv, grad_out), grad, wgu, wd)
    weight_gate = weight_grad(normed, grad_gate)
    weight_up = weight_grad(normed, after(grad_up, weight_gate))
    outputs, weight_down = branches(
        after(attended, weight_up), hidden, grad, tokens, weights, wd, ways
    )
    input_grad, vector_grads = norm_back(
        after(grad_projected, outputs),
        grad_gate,
        grad_up,
        normed,
        tokens,
        out_grad,
        stats,
        weights,
        wgu,
        vectors,
        own_vectors,
        ways,
        lines,
    )
    qkv_sum = after(weight_sum(grad_qkv.reshape(D, 3, width)), input_grad).astype(f32)
    out_sum = after(weight_sum(grad_out), input_grad).astype(f32)
    gate_sum = after(weight_sum(weight_gate), input_grad)
    up_sum = weight_sum(weight_up)
    down_sum = weight_sum(jnp.transpose(weight_down, (1, 0))).astype(f32)
    gate_up_sum = jnp.stack([gate_sum.astype(f32), up_sum.astype(f32)], axis=1)
    return (
        outputs,
        input_grad,
        vector_grads[0],
        vector_grads[1],
        qkv_sum,
        gate_up_sum,
        out_sum,
        down_sum,
    )


def solution(mesh):
    placed = (
        P("row", "col"),
        P("col"),
        P("col"),
        P("row", None, "col"),
        P("row", None, "col"),
        P("row", "col"),
        P("row", "col"),
        P("row"),
        P("row", None),
        P("row", "col"),
    )
    return jax.shard_map(
        local,
        mesh=mesh,
        in_specs=placed,
        out_specs=(
            P("row", "col"),
            P("row", "col"),
            P("col"),
            P("col"),
            P("row", None, "col"),
            P("row", None, "col"),
            P("row", "col"),
            P("row", "col"),
        ),
        check_vma=False,
    )
```

time: 634 us -> 589 us (0.929)
  Pallas kernels: 494 us -> 470 us
  local copies, waits for them, and re-layouts: 24 us -> 12.9 us
  other arithmetic: 23.1 us -> 12.1 us
    pallas_call x2 -> x3, Pallas kernels: 254 us -> 231 us  [the longest x1 94.5 us: gather_rest(): pl.pallas_call(functools.partial(gather_kernel, ways, count, seqs), out_s...]
  transfers between devices with their start and end apart: 8 -> 8, of which waited for: 0 -> 0; matrix products, arithmetic and copies ran while one was open for 17% -> 14% of each run, Pallas kernels for 79% -> 81%
where the time goes in v2:
time: 589 us; the launch traced here: 581 us
  Pallas kernels  470 us (80%)
  matrix products  69.2 us (12%)
  between operations  14.6 us (2%)
  local copies, waits for them, and re-layouts  12.9 us (2%)
  other arithmetic  12.1 us (2%)
    pallas_call x1, Pallas kernels, norm_back(): pl.pallas_call(functools.partial(back_kernel, ways, lines, steps), out_sh...  107 us
    pallas_call x1, Pallas kernels, gather_rest(): pl.pallas_call(functools.partial(gather_kernel, ways, count, seqs), out_s...  94.5 us
    pallas_call x1, Pallas kernels, gather_first(): pl.pallas_call(functools.partial(gather_kernel, ways, 0, 0), out_shape=[j...  86.9 us
    pallas_call x1, Pallas kernels, branches(): pl.pallas_call(functools.partial(branch_kernel, ways, steps), out_shape=[...  83.9 us
    dot_general x4, matrix products, contract(): lax.dot_general(left, right, (((left_dim,), (right_dim,)), ((), ())), pre...  69.2 us
    pallas_call x1, Pallas kernels, attention(): pl.pallas_call(functools.partial(attention_kernel, heads, first), out_sha...  49.4 us
    pallas_call x1, Pallas kernels, feed_forward(): pl.pallas_call(ffn_kernel, out_shape=[jax.ShapeDtypeStruct((rows, ffn), j...  48.7 us
  transfers between devices with their start and end apart: 8, of which 0 were waited for; matrix products, arithmetic and copies ran while one was open for 14% of the time, Pallas kernels for 81%

profile of v2, /device:TPU:0, one launch (start us, length us, event | category | flops | bytes accessed | tf_op | source)
XLA Modules:
  0.0 580.5 jit_solution(9501048835223850127)
XLA Ops:
  7.2 1.3 slice_bitcast_fusion.2
  8.6 2.1 pad_maximum_fusion
  10.6 0.0 all-gather.8.cloned.1.call-start
  10.7 0.7 all-gather.8.cloned.1.call-update
  11.4 0.7 all-gather.6.cloned.1.call-update
  12.1 0.0 reduce-scatter.12.cloned.1.call-start
  12.2 1.6 copy-done.2
  13.8 86.9 %gather_first.1 = (bf16[4096,2048]{1,0:T(8,128)(2,1)}, bf16[4096,2048]{1,0:T(8,128)(2,1)}, f32[4096,2]{1,0:T(8,128)S(1)}, f32[8,2048]{1,0:T(8,128)S(1)}) custom-call(bf16[4096,256]{1,0:T(8,128)(2,1)S(1)} %copy-done.1, bf16[4096,256]{1,0:T(8,128)(2,1)S(1)} %copy-done.2, f32[8,256]{1,0:T(8,128)S(1)} %select_maximum_fusion.refs_2_.gain_ref), custom_call_target="tpu_custom_call" | custom-call | flops 107374182400 | bytes 33554432 | tf_op jit(solution)/shard_map/gather_first/pallas_call | solution.py:587
  100.8 0.6 copy-done
  101.4 1.3 copy-done.3
  102.7 0.6 copy-done.4
  103.3 94.5 %gather_rest.1 = (bf16[4096,2048]{1,0:T(8,128)(2,1)}, bf16[4096,2048]{1,0:T(8,128)(2,1)}, f32[4096,2]{1,0:T(8,128)}, bf16[4096,256]{1,0:T(8,128)(2,1)}, bf16[4096,768]{1,0:T(8,128)(2,1)}) custom-call(bf16[4096,256]{1,0:T(8,128)(2,1)} %token_ref.3, bf16[4096,256]{1,0:T(8,128)(2,1)} %cot_ref.1, ...), custom_call_target="tpu_custom_call", output_to_operand_aliasing={{0}: (8, {}), {1}: (9, {})} | custom-call | flops 107374182400 | bytes 33554432 | tf_op jit(solution)/shard_map/gather_rest/pallas_call | solution.py:616
  197.8 49.4 %attention.1 = (bf16[4096,256]{1,0:T(8,128)(2,1)}, bf16[4096,768]{1,0:T(8,128)(2,1)}) custom-call(s32[4]{0:T(128)} %start_ref.1, bf16[4096,2048]{1,0:T(8,128)(2,1)} %get-tuple-element.43.x_ref, bf16[4096,2048]{1,0:T(8,128)(2,1)} %get-tuple-element.38.g_ref.grad_ref, ...), custom_call_target="tpu_custom_call", output_to_operand_aliasing={{0}: (6, {}), {1}: (7, {})} | custom-call | flops 20669530112 | bytes 25165824 | tf_op jit(solution)/shard_map/attention/pallas_call | solution.py:267
  247.2 12.3 %convolution_convert_fusion.3 = bf16[2048,256]{1,0:T(8,128)(2,1)} fusion(bf16[4096,2048]{1,0:T(8,128)(2,1)} %get-tuple-element.38.g_ref.grad_ref, bf16[4096,256]{1,0:T(8,128)(2,1)} %get-tuple-element.47.att_ref), kind=kOutput, calls=%fused_computation.3 | convolution fusion | flops 4295491584 | bytes 19922944 | tf_op jit(solution)/shard_map/dot_general | solution.py:31
  259.5 0.0 reduce-scatter.6.cloned.1.call-start
  259.5 19.2 %convolution_convert_fusion = bf16[2048,768]{0,1:T(8,128)(2,1)S(1)} fusion(bf16[4096,2048]{1,0:T(8,128)(2,1)} %get-tuple-element.43.x_ref, bf16[4096,768]{1,0:T(8,128)(2,1)} %get-tuple-element.50.gp_ref), kind=kOutput, calls=%fused_computation | convolution fusion | flops 12886474752 | bytes 26214400 | tf_op jit(solution)/shard_map/dot_general | solution.py:31
  278.8 2.8 copy.24
  281.6 0.0 reduce-scatter.8.cloned.1.call-start
  281.7 48.7 %feed_forward.1 = (bf16[4096,704]{1,0:T(8,128)(2,1)}, bf16[4096,704]{1,0:T(8,128)(2,1)}, bf16[4096,704]{1,0:T(8,128)(2,1)}) custom-call(bf16[4096,2048]{1,0:T(8,128)(2,1)} %get-tuple-element.43.x_ref, bf16[4096,2048]{1,0:T(8,128)(2,1)} %get-tuple-element.38.g_ref.grad_ref, bf16[2,704,2048]{2,1,0:T(8,128)(2,1)} %bitcast.32, bf16[704,2048]{1,0:T(8,128)(2,1)} %bitcast.34), custom_call_target="tpu_custom_call" | custom-call | flops 35433480192 | bytes 59506688 | tf_op jit(solution)/shard_map/feed_forward/pallas_call | solution.py:317
  330.4 18.8 %convolution_convert_fusion.2 = bf16[2048,704]{0,1:T(8,128)(2,1)} fusion(bf16[4096,2048]{1,0:T(8,128)(2,1)} %get-tuple-element.43.x_ref, bf16[4096,704]{1,0:T(8,128)(2,1)} %get-tuple-element.45.gg_ref), kind=kOutput, calls=%fused_computation.2 | convolution fusion | flops 11812601856 | bytes 25427968 | tf_op jit(solution)/shard_map/dot_general | solution.py:31
  349.2 0.0 reduce-scatter.10.cloned.1.call-start
  349.3 18.9 %convolution_convert_fusion.1 = bf16[2048,704]{0,1:T(8,128)(2,1)} fusion(bf16[4096,2048]{1,0:T(8,128)(2,1)} %get-tuple-element.43.x_ref, bf16[4096,704]{1,0:T(8,128)(2,1)} %get-tuple-element.46.gu_ref), kind=kOutput, calls=%fused_computation.1 | convolution fusion | flops 11812601856 | bytes 25427968 | tf_op jit(solution)/shard_map/dot_general | solution.py:31
  368.2 0.0 reduce-scatter.14.cloned.1.call-start
  368.3 83.9 %branches.1 = (bf16[4096,256]{1,0:T(8,128)(2,1)}, bf16[704,2048]{1,0:T(8,128)(2,1)}) custom-call(bf16[4096,256]{1,0:T(8,128)(2,1)} %get-tuple-element.47.att_ref, bf16[4096,704]{1,0:T(8,128)(2,1)} %get-tuple-element.48.hidden_ref, bf16[4096,2048]{1,0:T(8,128)(2,1)} %get-tuple-element.38.g_ref.grad_ref, bf16[4096,256]{1,0:T(8,128)(2,1)} %token_ref.3, ...), custom_call_target="tpu_custom_call" | custom-call | flops 111669149696 | bytes 33554432 | tf_op jit(solution)/shard_map/branches/pallas_call | solution.py:815
  452.2 106.5 %norm_back.1 = (f32[4096,256]{1,0:T(8,128)}, f32[8,256]{1,0:T(8,128)}) custom-call(bf16[4096,768]{1,0:T(8,128)(2,1)} %get-tuple-element.50.gp_ref, bf16[4096,704]{1,0:T(8,128)(2,1)} %get-tuple-element.45.gg_ref, bf16[4096,704]{1,0:T(8,128)(2,1)} %get-tuple-element.46.gu_ref, bf16[4096,2048]{1,0:T(8,128)(2,1)} %get-tuple-element.43.x_ref, ...), custom_call_target="tpu_custom_call" | custom-call | flops 73014444032 | bytes 50331648 | tf_op jit(solution)/shard_map/norm_back/pallas_call | solution.py:988
  558.7 1.8 convert_element_type.30
  560.5 1.3 fusion
  561.9 2.6 convert_element_type.29
  564.4 3.1 maximum_convert_fusion
  567.5 2.6 convert_element_type.31
  570.1 1.3 copy.31
  571.4 2.0 copy.32
  (31 shorter events, 0.3 us)
Async XLA Ops:
  7.2 5.0 copy-start.8
  7.2 5.0 copy-start.7
  7.2 5.0 copy-start.1
  7.2 96.1 %all-gather.4.cloned.1.call-start = ((), (), s32[]{:S(2)}) async-start(), calls=%async_computation.5 | async-start | bytes 5242880 | tf_op jit(solution)/shard_map/all_gather | solution.py:1053
  10.6 271.0 %all-gather.8.cloned.1.call-start = ((), (), s32[]{:S(2)}) async-start(), calls=%async_computation.7 | async-start | bytes 3604480 | tf_op jit(solution)/shard_map/all_gather | solution.py:1055
  11.4 270.3 %all-gather.6.cloned.1.call-start = ((), (), s32[]{:S(2)}) async-start(), calls=%async_computation.6 | async-start | bytes 7208960 | tf_op jit(solution)/shard_map/all_gather | solution.py:1054
  12.1 546.6 %reduce-scatter.12.cloned.1.call-start = ((), (), s32[]{:S(2)}) async-start(), calls=%async_computation.11 | async-start | bytes 1310720 | tf_op jit(solution)/shard_map/reduce_scatter | solution.py:1070
  12.2 1.6 copy-start.2
  100.8 0.6 copy-start
  101.4 1.3 copy-start.3
  102.7 0.6 copy-start.4
  259.5 302.4 %reduce-scatter.6.cloned.1.call-start = ((), (), s32[]{:S(2)}) async-start(), calls=%async_computation.8 | async-start | bytes 3932160 | tf_op jit(solution)/shard_map/reduce_scatter | solution.py:1070
  281.6 282.8 %reduce-scatter.8.cloned.1.call-start = ((), (), s32[]{:S(2)}) async-start(), calls=%async_computation.9 | async-start | bytes 3604480 | tf_op jit(solution)/shard_map/reduce_scatter | solution.py:1070
  349.2 215.2 %reduce-scatter.10.cloned.1.call-start = ((), (), s32[]{:S(2)}) async-start(), calls=%async_computation.10 | async-start | bytes 3604480 | tf_op jit(solution)/shard_map/reduce_scatter | solution.py:1070
  368.2 199.3 %reduce-scatter.14.cloned.1.call-start = ((), (), s32[]{:S(2)}) async-start(), calls=%async_computation.12 | async-start | bytes 3604480 | tf_op jit(solution)/shard_map/reduce_scatter | solution.py:1070
  561.9 8.2 %copy-start.6 = (bf16[4096,256]{1,0:T(8,128)(2,1)S(1)}, bf16[4096,256]{1,0:T(8,128)(2,1)}, u32[]{:S(2)}) copy-start(bf16[4096,256]{1,0:T(8,128)(2,1)} %get-tuple-element.71) | copy-start | bytes 6291460
  567.5 3.9 copy-start.5
Sparse Core Ops, SparseCore 0:
  10.8 83.4 all-gather.3
  95.8 57.6 all-gather.7
  155.1 105.4 all-gather.5
  263.3 25.3 reduce-scatter.11
  291.6 58.8 reduce-scatter.5
  352.8 56.2 reduce-scatter.7
  412.0 56.0 reduce-scatter.9
  470.5 56.0 reduce-scatter.13

commit v3 on v2

--- a/solution.py
+++ b/solution.py
@@ -511,10 +511,20 @@
 
     def step(p, _):
         for phase in range(phases):
-            arrive(p, phase)
-            start(p, phase + 1)
+            if phase or attended:
+                arrive(p, phase)
+                start(p, phase + 1)
             if phase == 0:
-                pl.when(p + 2 < pairs)(lambda: start(p + 2, 0))
+                if attended:
+                    pl.when(p + 2 < pairs)(lambda: start(p + 2, 0))
+                else:
+
+                    @pl.when(p + 1 < pairs)
+                    def _():
+                        arrive(p + 1, 0)
+                        start(p + 1, 1)
+
+                    pl.when(p + 3 < pairs)(lambda: start(p + 3, 0))
 
                 @pl.when(p >= 1)
                 def _():
@@ -550,6 +560,10 @@
                             move.start()
         return 0
 
+    if not attended:
+        arrive(0, 0)
+        start(0, 1)
+        start(2, 0)
     lax.fori_loop(0, pairs, step, 0)
     arrive(pairs - 1, phases)
     norm(pairs - 1)
@@ -756,11 +770,13 @@
     wd_ref,
     out_ref,
     wgrad_ref,
+    wout_grad_ref,
     parts,
     inbox,
     send_sem,
     recv_sem,
     acc,
+    acc_out,
 ):
     f32, bf16 = jnp.float32, jnp.bfloat16
     t = pl.program_id(0)
@@ -771,6 +787,7 @@
     @pl.when(t == 0)
     def _():
         acc[...] = jnp.zeros_like(acc)
+        acc_out[...] = jnp.zeros_like(acc_out)
         meet([{"col": flip(me, 1 << k)} for k in range(ways.bit_length() - 1)])
 
     @pl.when(t < steps)
@@ -788,10 +805,12 @@
     @pl.when(t < steps)
     def _():
         acc[...] += contract(hidden_ref[...], grad_ref[...], 0, 0)
+        acc_out[...] += contract(att_ref[...], grad_ref[...], 0, 0)
 
     @pl.when(t == steps)
     def _():
         wgrad_ref[...] = acc[...].astype(bf16)
+        wout_grad_ref[...] = acc_out[...].astype(bf16)
 
     s = t - lags[-1]
 
@@ -817,6 +836,7 @@
         out_shape=[
             jax.ShapeDtypeStruct((rows, width), jnp.bfloat16),
             jax.ShapeDtypeStruct((ffn, D), jnp.bfloat16),
+            jax.ShapeDtypeStruct((width, D), jnp.bfloat16),
         ],
         grid=(steps + lag,),
         in_specs=[
@@ -830,8 +850,13 @@
         out_specs=[
             pl.BlockSpec((RB, width), late),
             pl.BlockSpec((ffn, D), fixed, pipeline_mode=once),
-        ],
-        scratch_shapes=[*reducer_scratch(ways, rows, width), pltpu.VMEM((ffn, D), jnp.float32)],
+            pl.BlockSpec((width, D), fixed, pipeline_mode=once),
+        ],
+        scratch_shapes=[
+            *reducer_scratch(ways, rows, width),
+            pltpu.VMEM((ffn, D), jnp.float32),
+            pltpu.VMEM((width, D), jnp.float32),
+        ],
         compiler_params=pltpu.CompilerParams(
             collective_id=1,
             has_side_effects=True,
@@ -860,8 +885,10 @@
     wgu_ref,
     vectors_ref,
     gain_ref,
+    wqkv_ref,
     out_ref,
     vgrad_ref,
+    qkv_ref,
     parts,
     inbox,
     send_sem,
@@ -889,7 +916,7 @@
         )
 
     def sum_copies(group):
-        rows = pl.ds(pl.multiple_of(group * (SUMS * RB), SUMS * RB), SUMS * RB)
+        rows = pl.ds(pl.multiple_of(group * RB, RB), RB)
         for k in range(1, ways):
             yield pltpu.make_async_remote_copy(
                 src_ref=sums.at[0, :, rows],
@@ -916,8 +943,13 @@
             plain += jnp.sum(total * vectors_ref[0:1, cols], axis=1, keepdims=True)
             cross += jnp.sum(total * scaled, axis=1, keepdims=True)
         lane = lax.broadcasted_iota(jnp.int32, (RB, 128), 1)
-        pair = jnp.where(lane == 0, plain, jnp.where(lane == 1, cross, 0.0))
-        sums[0, :, rows] = pair.T[:8]
+        spot = 2 * (t % SUMS)
+        pair = jnp.where(lane == spot, plain, jnp.where(lane == spot + 1, cross, 0.0))
+        group = pl.ds(pl.multiple_of(t // SUMS * RB, RB), RB)
+        before = jnp.where(jnp.broadcast_to(spot == 0, (8, RB)), 0.0, sums[0, :, group])
+        sums[0, :, group] = before + pair.T[:8]
+        for kind in range(3):
+            qkv_ref[kind] = wqkv_ref[:, kind * width : (kind + 1) * width].astype(f32)
 
         @pl.when(t % SUMS == SUMS - 1)
         def _():
@@ -929,21 +961,24 @@
 
     @pl.when(s >= 0)
     def _():
-        rows = pl.ds(pl.multiple_of(s * RB, RB), RB)
-
         @pl.when(s % SUMS == 0)
         def _():
             for copy in sum_copies(s // SUMS):
                 copy.wait_recv()
 
-        both = sum(sums[k, :, rows] for k in range(ways)).T
+        group = pl.ds(pl.multiple_of(s // SUMS * RB, RB), RB)
+        both = sum(sums[k, :, group] for k in range(ways)).T
+        lane = lax.broadcasted_iota(jnp.int32, (RB, 8), 1)
+        spot = 2 * (s % SUMS)
+        plain = jnp.sum(jnp.where(lane == spot, both, 0.0), axis=1, keepdims=True) / D
+        cross = jnp.sum(jnp.where(lane == spot + 1, both, 0.0), axis=1, keepdims=True) / D
         for k, value in enumerate(ring.absorb(s, ring.phases - 1)):
             half = slice(k * (RB // 2), (k + 1) * (RB // 2))
             inv = stat_ref[half, 1:]
             unit = (token_ref[half, :].astype(f32) - stat_ref[half, :1]) * inv
             scaled = value * gain_ref[0:1, :]
             out_ref[half, :] = cot_ref[half, :].astype(f32) + inv * (
-                scaled - both[half, 0:1] / D - unit * (both[half, 1:2] / D)
+                scaled - plain[half] - unit * cross[half]
             )
             acc[0, 0:1, :] += jnp.sum(value * unit, axis=0, keepdims=True)
             acc[0, 1:2, :] += jnp.sum(value, axis=0, keepdims=True)
@@ -975,11 +1010,15 @@
         vgrad_ref[...] = sum(acc[k] for k in range(lines))
 
 
-def norm_back(gp, gg, gu, normed, tokens, cot, stats, weights, wgu, vectors, own, ways, lines):
+def norm_back(
+    gp, gg, gu, normed, tokens, cot, stats, weights, wgu, vectors, own, qkv, ways, lines
+):
     rows, width = tokens.shape
     ffn = gg.shape[1]
     steps = rows // RB
     lag = lags_of(ways)[-1]
+    deep = qkv.shape[0]
+    slab = deep // steps
     now = lambda t: (jnp.minimum(t, steps - 1), 0)
     late = lambda t: (jnp.maximum(t - lag, 0), 0)
     fixed = lambda t: (0, 0)
@@ -990,6 +1029,7 @@
         out_shape=[
             jax.ShapeDtypeStruct((rows, width), jnp.float32),
             jax.ShapeDtypeStruct((8, width), jnp.float32),
+            jax.ShapeDtypeStruct((3, deep, width), jnp.float32),
         ],
         grid=(steps + lag,),
         in_specs=[
@@ -1004,11 +1044,16 @@
             pl.BlockSpec((2, ffn, D), lambda t: (0, 0, 0), pipeline_mode=once),
             pl.BlockSpec((8, D), fixed),
             pl.BlockSpec((8, width), fixed),
-        ],
-        out_specs=[pl.BlockSpec((RB, width), late), pl.BlockSpec((8, width), fixed)],
+            pl.BlockSpec((slab, 3 * width), now),
+        ],
+        out_specs=[
+            pl.BlockSpec((RB, width), late),
+            pl.BlockSpec((8, width), fixed),
+            pl.BlockSpec((3, slab, width), lambda t: (0, jnp.minimum(t, steps - 1), 0)),
+        ],
         scratch_shapes=[
             *reducer_scratch(ways, rows, width),
-            pltpu.VMEM((ways, 8, rows), jnp.float32),
+            pltpu.VMEM((ways, 8, rows // SUMS), jnp.float32),
             dma((steps // SUMS, ways - 1)),
             dma((steps // SUMS, ways - 1)),
             pltpu.VMEM((lines, 8, width), jnp.float32),
@@ -1025,7 +1070,7 @@
             flops=4 * rows * D * (2 * ffn + 3 * width), bytes_accessed=6 * rows * D, transcendentals=0
         ),
         name="norm_back",
-    )(gp, gg, gu, normed, tokens, cot, stats, weights, wgu, vectors, own)
+    )(gp, gg, gu, normed, tokens, cot, stats, weights, wgu, vectors, own, qkv)
 
 
 def after(value, *others):
@@ -1073,15 +1118,16 @@
         return contract(left, right, 0, 0).astype(bf16)
 
     grad_qkv = weight_grad(normed, grad_projected)
-    grad_out = weight_grad(grad, attended)
-    hidden, grad_gate, grad_up = feed_forward(after(normed, grad_qkv, grad_out), grad, wgu, wd)
+    hidden, grad_gate, grad_up = feed_forward(after(normed, grad_qkv), grad, wgu, wd)
     weight_gate = weight_grad(normed, grad_gate)
     weight_up = weight_grad(normed, after(grad_up, weight_gate))
-    outputs, weight_down = branches(
-        after(attended, weight_up), hidden, grad, tokens, weights, wd, ways
+    qkv_sum = weight_sum(grad_qkv)
+    gate_sum = weight_sum(weight_gate)
+    outputs, weight_down, weight_out = branches(
+        after(attended, weight_up, qkv_sum), hidden, grad, tokens, weights, wd, ways
     )
-    input_grad, vector_grads = norm_back(
-        after(grad_projected, outputs),
+    input_grad, vector_grads, qkv_sum = norm_back(
+        after(grad_projected, outputs, gate_sum),
         grad_gate,
         grad_up,
         normed,
@@ -1092,14 +1138,14 @@
         wgu,
         vectors,
         own_vectors,
+        qkv_sum,
         ways,
         lines,
     )
-    qkv_sum = after(weight_sum(grad_qkv.reshape(D, 3, width)), input_grad).astype(f32)
-    out_sum = after(weight_sum(grad_out), input_grad).astype(f32)
-    gate_sum = after(weight_sum(weight_gate), input_grad)
-    up_sum = weight_sum(weight_up)
+    qkv_sum = jnp.transpose(qkv_sum, (1, 0, 2))
+    up_sum = after(weight_sum(weight_up), input_grad)
     down_sum = weight_sum(jnp.transpose(weight_down, (1, 0))).astype(f32)
+    out_sum = weight_sum(jnp.transpose(weight_out, (1, 0))).astype(f32)
     gate_up_sum = jnp.stack([gate_sum.astype(f32), up_sum.astype(f32)], axis=1)
     return (
         outputs,

time: 589 us -> 567 us (0.963)
  matrix products: 69.2 us -> 57.8 us
  Pallas kernels: 470 us -> 461 us
    dot_general x4 -> x3, matrix products: 69.2 us -> 57.8 us  [contract(): lax.dot_general(left, right, (((left_dim,), (right_dim,)), ((), ())), pre...]
    pallas_call x1, Pallas kernels: 107 us -> 99.9 us  [norm_back(): pl.pallas_call(functools.partial(back_kernel, ways, lines, steps), out_sh...]
  transfers between devices with their start and end apart: 8 -> 8, of which waited for: 0 -> 0; matrix products, arithmetic and copies ran while one was open for 14% -> 11% of each run, Pallas kernels for 81% -> 83%
where the time goes in v3:
time: 567 us; the launch traced here: 558 us
  Pallas kernels  461 us (81%)
  matrix products  57.8 us (10%)
  between operations  14.8 us (3%)
  local copies, waits for them, and re-layouts  13.7 us (2%)
  other arithmetic  7.65 us (1%)
    pallas_call x1, Pallas kernels, norm_back(): pl.pallas_call(functools.partial(back_kernel, ways, lines, steps), out_sh...  99.9 us
    pallas_call x1, Pallas kernels, gather_rest(): pl.pallas_call(functools.partial(gather_kernel, ways, count, seqs), out_s...  95.6 us
    pallas_call x1, Pallas kernels, gather_first(): pl.pallas_call(functools.partial(gather_kernel, ways, 0, 0), out_shape=[j...  84.7 us
    pallas_call x1, Pallas kernels, branches(): pl.pallas_call(functools.partial(branch_kernel, ways, steps), out_shape=[...  84.3 us
    dot_general x3, matrix products, contract(): lax.dot_general(left, right, (((left_dim,), (right_dim,)), ((), ())), pre...  57.8 us
    pallas_call x1, Pallas kernels, feed_forward(): pl.pallas_call(ffn_kernel, out_shape=[jax.ShapeDtypeStruct((rows, ffn), j...  48.7 us
    pallas_call x1, Pallas kernels, attention(): pl.pallas_call(functools.partial(attention_kernel, heads, first), out_sha...  48.1 us
  transfers between devices with their start and end apart: 8, of which 0 were waited for; matrix products, arithmetic and copies ran while one was open for 11% of the time, Pallas kernels for 83%

profile of v3, /device:TPU:0, one launch (start us, length us, event | category | flops | bytes accessed | tf_op | source)
XLA Modules:
  0.0 557.7 jit_solution(9554948027622998324)
XLA Ops:
  7.2 1.3 slice_bitcast_fusion.2
  8.6 2.1 pad_maximum_fusion
  10.6 0.0 all-gather.8.cloned.1.call-start
  10.7 0.7 all-gather.8.cloned.1.call-update
  11.4 0.7 all-gather.6.cloned.1.call-update
  12.1 0.0 reduce-scatter.6.cloned.1.call-start
  12.2 1.6 copy-done.2
  13.8 84.7 %gather_first.1 = (bf16[4096,2048]{1,0:T(8,128)(2,1)}, bf16[4096,2048]{1,0:T(8,128)(2,1)}, f32[4096,2]{1,0:T(8,128)S(1)}, f32[8,2048]{1,0:T(8,128)S(1)}) custom-call(bf16[4096,256]{1,0:T(8,128)(2,1)S(1)} %copy-done.1, bf16[4096,256]{1,0:T(8,128)(2,1)S(1)} %copy-done.2, f32[8,256]{1,0:T(8,128)S(1)} %select_maximum_fusion.refs_2_.gain_ref), custom_call_target="tpu_custom_call" | custom-call | flops 107374182400 | bytes 33554432 | tf_op jit(solution)/shard_map/gather_first/pallas_call | solution.py:601
  98.5 0.6 copy-done
  99.1 1.3 copy-done.3
  100.5 0.6 copy-done.4
  101.1 95.6 %gather_rest.1 = (bf16[4096,2048]{1,0:T(8,128)(2,1)}, bf16[4096,2048]{1,0:T(8,128)(2,1)}, f32[4096,2]{1,0:T(8,128)}, bf16[4096,256]{1,0:T(8,128)(2,1)}, bf16[4096,768]{1,0:T(8,128)(2,1)}) custom-call(bf16[4096,256]{1,0:T(8,128)(2,1)} %token_ref.3, bf16[4096,256]{1,0:T(8,128)(2,1)} %cot_ref.1, ...), custom_call_target="tpu_custom_call", output_to_operand_aliasing={{0}: (8, {}), {1}: (9, {})} | custom-call | flops 107374182400 | bytes 33554432 | tf_op jit(solution)/shard_map/gather_rest/pallas_call | solution.py:630
  196.7 48.1 %attention.1 = (bf16[4096,256]{1,0:T(8,128)(2,1)}, bf16[4096,768]{1,0:T(8,128)(2,1)}) custom-call(s32[4]{0:T(128)} %start_ref.1, bf16[4096,2048]{1,0:T(8,128)(2,1)} %get-tuple-element.43.x_ref, bf16[4096,2048]{1,0:T(8,128)(2,1)} %get-tuple-element.38.g_ref.grad_ref, ...), custom_call_target="tpu_custom_call", output_to_operand_aliasing={{0}: (6, {}), {1}: (7, {})} | custom-call | flops 20669530112 | bytes 25165824 | tf_op jit(solution)/shard_map/attention/pallas_call | solution.py:267
  244.8 20.1 %convolution_convert_fusion = bf16[2048,768]{1,0:T(8,128)(2,1)} fusion(bf16[4096,2048]{1,0:T(8,128)(2,1)} %get-tuple-element.43.x_ref, bf16[4096,768]{1,0:T(8,128)(2,1)} %get-tuple-element.50.gp_ref), kind=kOutput, calls=%fused_computation | convolution fusion | flops 12886474752 | bytes 26214400 | tf_op jit(solution)/shard_map/dot_general | solution.py:31
  264.9 0.0 reduce-scatter.8.cloned.1.call-start
  265.0 48.7 %feed_forward.1 = (bf16[4096,704]{1,0:T(8,128)(2,1)}, bf16[4096,704]{1,0:T(8,128)(2,1)}, bf16[4096,704]{1,0:T(8,128)(2,1)}) custom-call(bf16[4096,2048]{1,0:T(8,128)(2,1)} %get-tuple-element.43.x_ref, bf16[4096,2048]{1,0:T(8,128)(2,1)} %get-tuple-element.38.g_ref.grad_ref, bf16[2,704,2048]{2,1,0:T(8,128)(2,1)} %bitcast.32, bf16[704,2048]{1,0:T(8,128)(2,1)} %bitcast.34), custom_call_target="tpu_custom_call" | custom-call | flops 35433480192 | bytes 59506688 | tf_op jit(solution)/shard_map/feed_forward/pallas_call | solution.py:317
  313.7 18.8 %convolution_convert_fusion.2 = bf16[2048,704]{0,1:T(8,128)(2,1)} fusion(bf16[4096,2048]{1,0:T(8,128)(2,1)} %get-tuple-element.43.x_ref, bf16[4096,704]{1,0:T(8,128)(2,1)} %get-tuple-element.45.gg_ref), kind=kOutput, calls=%fused_computation.2 | convolution fusion | flops 11812601856 | bytes 25427968 | tf_op jit(solution)/shard_map/dot_general | solution.py:31
  332.5 0.0 reduce-scatter.10.cloned.1.call-start
  332.6 18.9 %convolution_convert_fusion.1 = bf16[2048,704]{0,1:T(8,128)(2,1)} fusion(bf16[4096,2048]{1,0:T(8,128)(2,1)} %get-tuple-element.43.x_ref, bf16[4096,704]{1,0:T(8,128)(2,1)} %get-tuple-element.46.gu_ref), kind=kOutput, calls=%fused_computation.1 | convolution fusion | flops 11812601856 | bytes 25427968 | tf_op jit(solution)/shard_map/dot_general | solution.py:31
  351.5 0.0 reduce-scatter.12.cloned.1.call-start
  351.5 84.3 %branches.1 = (bf16[4096,256]{1,0:T(8,128)(2,1)}, bf16[704,2048]{1,0:T(8,128)(2,1)}, bf16[256,2048]{1,0:T(8,128)(2,1)}) custom-call(bf16[4096,256]{1,0:T(8,128)(2,1)} %get-tuple-element.47.att_ref, bf16[4096,704]{1,0:T(8,128)(2,1)} %get-tuple-element.48.hidden_ref, bf16[4096,2048]{1,0:T(8,128)(2,1)} %get-tuple-element.38.g_ref.grad_ref, ...), custom_call_target="tpu_custom_call" | custom-call | flops 111669149696 | bytes 33554432 | tf_op jit(solution)/shard_map/branches/pallas_call | solution.py:834
  435.9 0.0 reduce-scatter.14.cloned.1.call-start
  435.9 0.7 reduce-scatter.14.cloned.1.call-update
  436.7 99.9 %norm_back.1 = (f32[4096,256]{1,0:T(8,128)}, f32[8,256]{1,0:T(8,128)}, f32[3,512,256]{2,1,0:T(8,128)}) custom-call(bf16[4096,768]{1,0:T(8,128)(2,1)} %get-tuple-element.50.gp_ref, bf16[4096,704]{1,0:T(8,128)(2,1)} %get-tuple-element.45.gg_ref, bf16[4096,704]{1,0:T(8,128)(2,1)} %get-tuple-element.46.gu_ref, bf16[4096,2048]{1,0:T(8,128)(2,1)} %get-tuple-element.43.x_ref, ...), custom_call_target="tpu_custom_call" | custom-call | flops 73014444032 | bytes 50331648 | tf_op jit(solution)/shard_map/norm_back/pallas_call | solution.py:1027
  536.6 3.0 maximum_convert_fusion
  539.6 1.3 fusion
  541.0 1.9 copy.24
  542.8 2.6 convert_element_type.23
  545.4 1.3 copy.32
  546.7 2.0 copy.33
  548.7 0.5 copy-done.7
  549.3 1.1 copy.34
  (33 shorter events, 0.3 us)
Async XLA Ops:
  7.2 5.0 copy-start.10
  7.2 5.0 copy-start.9
  7.2 5.0 copy-start.1
  7.2 93.9 %all-gather.4.cloned.1.call-start = ((), (), s32[]{:S(2)}) async-start(), calls=%async_computation.5 | async-start | bytes 5242880 | tf_op jit(solution)/shard_map/all_gather | solution.py:1098
  10.6 254.3 %all-gather.8.cloned.1.call-start = ((), (), s32[]{:S(2)}) async-start(), calls=%async_computation.7 | async-start | bytes 3604480 | tf_op jit(solution)/shard_map/all_gather | solution.py:1100
  11.4 253.6 %all-gather.6.cloned.1.call-start = ((), (), s32[]{:S(2)}) async-start(), calls=%async_computation.6 | async-start | bytes 7208960 | tf_op jit(solution)/shard_map/all_gather | solution.py:1099
  12.1 339.4 %reduce-scatter.6.cloned.1.call-start = ((), (), s32[]{:S(2)}) async-start(), calls=%async_computation.8 | async-start | bytes 3932160 | tf_op jit(solution)/shard_map/reduce_scatter | solution.py:1115
  12.2 1.6 copy-start.2
  98.5 0.6 copy-start
  99.1 1.3 copy-start.3
  100.5 0.6 copy-start.4
  264.9 171.8 %reduce-scatter.8.cloned.1.call-start = ((), (), s32[]{:S(2)}) async-start(), calls=%async_computation.9 | async-start | bytes 3604480 | tf_op jit(solution)/shard_map/reduce_scatter | solution.py:1115
  332.5 204.1 %reduce-scatter.10.cloned.1.call-start = ((), (), s32[]{:S(2)}) async-start(), calls=%async_computation.10 | async-start | bytes 3604480 | tf_op jit(solution)/shard_map/reduce_scatter | solution.py:1115
  351.5 189.5 %reduce-scatter.12.cloned.1.call-start = ((), (), s32[]{:S(2)}) async-start(), calls=%async_computation.11 | async-start | bytes 1310720 | tf_op jit(solution)/shard_map/reduce_scatter | solution.py:1115
  435.9 107.0 %reduce-scatter.14.cloned.1.call-start = ((), (), s32[]{:S(2)}) async-start(), calls=%async_computation.12 | async-start | bytes 3604480 | tf_op jit(solution)/shard_map/reduce_scatter | solution.py:1115
  436.7 99.9 %copy-start.8 = (bf16[512,704]{0,1:T(8,128)(2,1)S(1)}, bf16[512,704]{0,1:T(8,128)(2,1)}, u32[]{:S(2)}) copy-start(bf16[512,704]{0,1:T(8,128)(2,1)} %reduce-scatter.8.cloned.1.call-done) | copy-start | bytes 2162692
  536.5 8.9 %copy-start.6 = (bf16[4096,256]{1,0:T(8,128)(2,1)S(1)}, bf16[4096,256]{1,0:T(8,128)(2,1)}, u32[]{:S(2)}) copy-start(bf16[4096,256]{1,0:T(8,128)(2,1)} %get-tuple-element.79) | copy-start | bytes 6291460
  542.8 3.9 copy-start.5
  546.7 2.5 copy-start.7
Sparse Core Ops, SparseCore 0:
  10.8 83.4 all-gather.3
  95.8 57.6 all-gather.7
  155.1 105.4 all-gather.5
  265.0 63.3 reduce-scatter.5
  332.6 59.2 reduce-scatter.7
  394.7 56.0 reduce-scatter.9
  453.0 26.9 reduce-scatter.11
  482.5 55.2 reduce-scatter.13

commit v4 on v3

--- a/solution.py
+++ b/solution.py
@@ -14,9 +14,10 @@
 LEN = 1024
 IMG = 256
 QB = 256
-MB = 512
+MB = 256
 RB = 256
-GB = 512
+GB = 256
+GA = 256
 SUMS = 4
 
 
@@ -77,7 +78,6 @@
             self.bias,
             self.m,
             self.l,
-            self.x,
             self.ot,
             self.dqt,
             self.dk,
@@ -96,8 +96,7 @@
             pltpu.VMEM((blocks, heads, QB, QB), f32),
             pltpu.VMEM((blocks, heads, QB, QB), f32),
             pltpu.VMEM((blocks, heads, QB, QB), bf16),
-            pltpu.VMEM((QB, QB), f32),
-            pltpu.VMEM((heads, 8, QB), f32),
+            pltpu.VMEM((2, QB, QB), f32),
             pltpu.VMEM((heads, 8, QB), f32),
             pltpu.VMEM((heads, 8, QB), f32),
             pltpu.VMEM((width, QB), f32),
@@ -146,6 +145,17 @@
     def bounds(self, i):
         return jnp.min(self.span[i, 0:1, :]) // QB, jnp.max(self.span[i, 1:2, :]) // QB
 
+    @staticmethod
+    def sweep(low, high, body):
+        def two(j, _):
+            body(low + 2 * j)
+            body(low + 2 * j + 1)
+            return 0
+
+        count = high + 1 - low
+        lax.fori_loop(0, count // 2, two, 0)
+        pl.when(count % 2 == 1)(lambda: body(high))
+
     def query_block(self, i, low, high, att_ref, gp_ref):
         f32, bf16, heads, width = jnp.float32, jnp.bfloat16, self.heads, self.width
         rows = pl.ds(pl.multiple_of(i * QB, QB), QB)
@@ -158,68 +168,68 @@
         self.m[...] = jnp.full_like(self.m, MASKED_SCORE)
 
         def fold(x, op):
-            out = x[:8]
-            for r in range(8, QB, 8):
-                out = op(out, x[r : r + 8])
-            return out
-
-        def score(kb, _):
+            runs = [x[r : r + 8] for r in range(0, QB, 8)]
+            lanes = runs[:8]
+            for r, run in enumerate(runs[8:]):
+                lanes[r % 8] = op(lanes[r % 8], run)
+            while len(lanes) > 1:
+                lanes = [op(a, b) for a, b in zip(lanes[::2], lanes[1::2])]
+            return lanes[0]
+
+        def score(kb):
             keys = pl.ds(pl.multiple_of(kb * QB, QB), QB)
             k, v = self.data[keys, self.part(1)], self.data[keys, self.part(2)]
             at = lax.broadcasted_iota(jnp.int32, (QB, QB), 0) + kb * QB
-            self.bias[...] = jnp.where((at >= first) & (at <= final), 0.0, MASKED_SCORE)
+            bias = jnp.where((at >= first) & (at <= final), 0.0, MASKED_SCORE)
+            self.bias[kb % 2] = bias
             for h in range(heads):
-                s = lax.dot_general(k, q_own[h], NT, preferred_element_type=f32) + self.bias[...]
+                s = lax.dot_general(k, q_own[h], NT, preferred_element_type=f32) + self.bias[kb % 2]
                 self.s[kb, h] = s
                 self.m[h] = jnp.maximum(self.m[h], fold(s, jnp.maximum))
                 self.d[kb, h] = lax.dot_general(v, g_own[h], NT, preferred_element_type=f32)
-            return 0
-
-        lax.fori_loop(low, high + 1, score, 0)
+
+        self.sweep(low, high, score)
         for h in range(heads):
             self.m[h] = jnp.broadcast_to(jnp.max(self.m[h], axis=0, keepdims=True), (8, QB))
         self.l[...] = jnp.zeros_like(self.l)
-        self.x[...] = jnp.zeros_like(self.x)
         self.ot[...] = jnp.zeros_like(self.ot)
         self.dqt[...] = jnp.zeros_like(self.dqt)
 
-        def expo(kb, _):
+        def expo(kb):
             for h in range(heads):
                 hs = slice(h * HD, (h + 1) * HD)
                 e = jnp.exp(self.s[kb, h] - self.m[h, 0:1, :])
                 self.l[h] += fold(e, jnp.add)
-                self.x[h] += fold(e * self.d[kb, h], jnp.add)
                 e = e.astype(bf16)
                 self.e[kb, h] = e
                 self.ot[hs, :] += jnp.dot(self.vt[kb, hs, :], e, preferred_element_type=f32)
-            return 0
-
-        lax.fori_loop(low, high + 1, expo, 0)
+
+        self.sweep(low, high, expo)
+        gt = g.astype(f32).T
         for h in range(heads):
+            hs = slice(h * HD, (h + 1) * HD)
             inv = 1.0 / jnp.sum(self.l[h], axis=0, keepdims=True)
             self.l[h] = jnp.broadcast_to(inv, (8, QB))
-            delta = jnp.sum(self.x[h], axis=0, keepdims=True) * inv
-            self.x[h] = jnp.broadcast_to(delta, (8, QB))
-
-        def back(kb, _):
+            out = self.ot[hs, :] * inv
+            self.ot[hs, :] = out
+            delta = jnp.sum(out * gt[hs], axis=0, keepdims=True)
+            self.m[h] = jnp.broadcast_to(delta, (8, QB))
+
+        def back(kb):
             keys = pl.ds(pl.multiple_of(kb * QB, QB), QB)
             dk = self.dk[keys, :]
             dv = self.dv[keys, :]
             for h in range(heads):
                 hs = slice(h * HD, (h + 1) * HD)
                 p = self.e[kb, h].astype(f32) * self.l[h, 0:1, :]
-                ds = (p * (self.d[kb, h] - self.x[h, 0:1, :])).astype(bf16)
+                ds = (p * (self.d[kb, h] - self.m[h, 0:1, :])).astype(bf16)
                 dv += jnp.dot(p.astype(bf16), g_own[h], preferred_element_type=f32)
                 dk += jnp.dot(ds, q_own[h], preferred_element_type=f32)
                 self.dqt[hs, :] += jnp.dot(self.kt[kb, hs, :], ds, preferred_element_type=f32)
             self.dk[keys, :] = dk
             self.dv[keys, :] = dv
-            return 0
-
-        lax.fori_loop(low, high + 1, back, 0)
-        for h in range(heads):
-            hs = slice(h * HD, (h + 1) * HD)
-            self.ot[hs, :] = self.ot[hs, :] * self.l[h, 0:1, :]
+
+        self.sweep(low, high, back)
         att_ref[rows, :] = self.ot[...].T.astype(bf16)
         dq = self.dqt[...].T * HD**-0.5
         gp_ref[rows, :width] = turn(dq, self.tables, rows, -1.0).astype(bf16)
@@ -365,7 +375,7 @@
     pl.semaphore_wait(barrier, len(peers))
 
 
-def gather_kernel(ways, base, attended, *refs):
+def gather_kernel(ways, base, attended, count, *refs):
     f32, bf16 = jnp.float32, jnp.bfloat16
     me = lax.axis_index("col")
     if attended:
@@ -379,7 +389,7 @@
     refs = refs[6:]
     width = token_ref.shape[1]
     rows = both.shape[1]
-    pairs = rows // GB
+    pairs = rows // count
     orders = chip_orders(ways)
     phases = len(orders[0])
     mine = pl.ds(pl.multiple_of(me * width, width), width)
@@ -410,7 +420,7 @@
     def copies(p, phase):
         for k, order in enumerate(orders):
             bit = order[phase] if phase < phases else 1
-            place = pl.ds(pl.multiple_of(p * GB + k * (GB // 2), GB // 2), GB // 2)
+            place = pl.ds(pl.multiple_of(p * count + k * (count // 2), count // 2), count // 2)
             for o in held(order[:phase]):
                 index = k * ways + (o ^ bit)
                 owner = flip(me, o)
@@ -432,8 +442,8 @@
             copy.wait_recv()
 
     def filed(p, first, out_ref, sem):
-        place = pl.ds(pl.multiple_of(p * GB, GB), GB)
-        goal = pl.ds(pl.multiple_of(base + p * GB, GB), GB)
+        place = pl.ds(pl.multiple_of(p * count, count), count)
+        goal = pl.ds(pl.multiple_of(base + p * count, count), count)
         for b in range(ways):
             pltpu.make_async_copy(
                 both.at[b, place, pl.ds(first, width)],
@@ -442,7 +452,7 @@
             ).start()
 
     def filed_wait(p, out_ref, sem):
-        place = out_ref.at[pl.ds(base + p * GB, GB)]
+        place = out_ref.at[pl.ds(base + p * count, count)]
         pltpu.make_async_copy(place, place, sem.at[p]).wait()
 
     def norm(p):
@@ -452,8 +462,8 @@
                 copy.wait_send()
 
         def block(j, _):
-            at = pl.ds(pl.multiple_of(p * GB + j * QB, QB), QB)
-            goal = pl.ds(pl.multiple_of(base + p * GB + j * QB, QB), QB)
+            at = pl.ds(pl.multiple_of(p * count + j * QB, QB), QB)
+            goal = pl.ds(pl.multiple_of(base + p * count + j * QB, QB), QB)
             sums = sum(both[b, at, :width].astype(f32) for b in range(ways))
             mean = jnp.sum(sums, axis=1, keepdims=True) / D
             squares = jnp.zeros((QB, width), f32)
@@ -470,7 +480,7 @@
                 both[b, at, :width] = x.astype(bf16)
             return 0
 
-        lax.fori_loop(0, GB // QB, block, 0)
+        lax.fori_loop(0, count // QB, block, 0)
         filed(p, 0, normed_ref, store_sem)
 
     if attended:
@@ -579,9 +589,9 @@
             vector_copy(k).wait_send()
 
 
-def gather_scratch(ways, rows, width):
+def gather_scratch(ways, rows, width, count):
     dma = pltpu.SemaphoreType.DMA
-    pairs = rows // GB
+    pairs = rows // count
     return [
         pltpu.VMEM((ways, rows, 2 * width), jnp.bfloat16),
         dma((2,)),
@@ -599,7 +609,7 @@
     vmem = pl.BlockSpec(memory_space=pltpu.VMEM)
     dma = pltpu.SemaphoreType.DMA
     return pl.pallas_call(
-        functools.partial(gather_kernel, ways, 0, 0),
+        functools.partial(gather_kernel, ways, 0, 0, GB),
         out_shape=[
             jax.ShapeDtypeStruct((rows, D), bf16),
             jax.ShapeDtypeStruct((rows, D), bf16),
@@ -608,9 +618,9 @@
         ],
         in_specs=[anywhere, anywhere, vmem],
         out_specs=[anywhere, anywhere, vmem, vmem],
-        scratch_shapes=[*gather_scratch(ways, count, width), dma((ways - 1,)), dma((ways - 1,))],
+        scratch_shapes=[*gather_scratch(ways, count, width, GB), dma((ways - 1,)), dma((ways - 1,))],
         compiler_params=pltpu.CompilerParams(
-            collective_id=0, has_side_effects=True, vmem_limit_bytes=40 << 20
+            collective_id=0, has_side_effects=True, vmem_limit_bytes=63 << 20
         ),
         cost_estimate=pl.CostEstimate(
             flops=100 * count * D * D // ways, bytes_accessed=count * D * 8, transcendentals=0
@@ -628,7 +638,7 @@
     dma = pltpu.SemaphoreType.DMA
     seqs = count // LEN
     return pl.pallas_call(
-        functools.partial(gather_kernel, ways, count, seqs),
+        functools.partial(gather_kernel, ways, count, seqs, GA),
         out_shape=[
             jax.ShapeDtypeStruct((rows, D), bf16),
             jax.ShapeDtypeStruct((rows, D), bf16),
@@ -651,7 +661,7 @@
         out_specs=[anywhere, anywhere, vmem, anywhere, anywhere],
         input_output_aliases={8: 0, 9: 1},
         scratch_shapes=[
-            *gather_scratch(ways, rows - count, width),
+            *gather_scratch(ways, rows - count, width, GA),
             pltpu.VMEM((LEN, D), bf16),
             pltpu.VMEM((LEN, D), bf16),
             pltpu.VMEM((seqs, LEN, width), bf16),
@@ -661,7 +671,7 @@
             *Attention.scratch(width // HD),
         ],
         compiler_params=pltpu.CompilerParams(
-            collective_id=3, has_side_effects=True, vmem_limit_bytes=60 << 20
+            collective_id=3, has_side_effects=True, vmem_limit_bytes=63 << 20
         ),
         cost_estimate=pl.CostEstimate(
             flops=100 * count * D * D // ways, bytes_accessed=count * D * 8, transcendentals=0
@@ -770,7 +780,6 @@
     wd_ref,
     out_ref,
     wgrad_ref,
-    wout_grad_ref,
     parts,
     inbox,
     send_sem,
@@ -809,8 +818,9 @@
 
     @pl.when(t == steps)
     def _():
-        wgrad_ref[...] = acc[...].astype(bf16)
-        wout_grad_ref[...] = acc_out[...].astype(bf16)
+        ffn = acc.shape[0]
+        wgrad_ref[:ffn, :] = acc[...].astype(bf16)
+        wgrad_ref[ffn:, :] = acc_out[...].astype(bf16)
 
     s = t - lags[-1]
 
@@ -835,8 +845,7 @@
         functools.partial(branch_kernel, ways, steps),
         out_shape=[
             jax.ShapeDtypeStruct((rows, width), jnp.bfloat16),
-            jax.ShapeDtypeStruct((ffn, D), jnp.bfloat16),
-            jax.ShapeDtypeStruct((width, D), jnp.bfloat16),
+            jax.ShapeDtypeStruct((ffn + width, D), jnp.bfloat16),
         ],
         grid=(steps + lag,),
         in_specs=[
@@ -849,8 +858,7 @@
         ],
         out_specs=[
             pl.BlockSpec((RB, width), late),
-            pl.BlockSpec((ffn, D), fixed, pipeline_mode=once),
-            pl.BlockSpec((width, D), fixed, pipeline_mode=once),
+            pl.BlockSpec((ffn + width, D), fixed, pipeline_mode=once),
         ],
         scratch_shapes=[
             *reducer_scratch(ways, rows, width),
@@ -1123,7 +1131,7 @@
     weight_up = weight_grad(normed, after(grad_up, weight_gate))
     qkv_sum = weight_sum(grad_qkv)
     gate_sum = weight_sum(weight_gate)
-    outputs, weight_down, weight_out = branches(
+    outputs, weight_rest = branches(
         after(attended, weight_up, qkv_sum), hidden, grad, tokens, weights, wd, ways
     )
     input_grad, vector_grads, qkv_sum = norm_back(
@@ -1144,8 +1152,8 @@
     )
     qkv_sum = jnp.transpose(qkv_sum, (1, 0, 2))
     up_sum = after(weight_sum(weight_up), input_grad)
-    down_sum = weight_sum(jnp.transpose(weight_down, (1, 0))).astype(f32)
-    out_sum = weight_sum(jnp.transpose(weight_out, (1, 0))).astype(f32)
+    rest = weight_sum(jnp.transpose(weight_rest, (1, 0))).astype(f32)
+    down_sum, out_sum = rest[:, :-width], rest[:, -width:]
     gate_up_sum = jnp.stack([gate_sum.astype(f32), up_sum.astype(f32)], axis=1)
     return (
         outputs,

time: 567 us -> 559 us (0.986)
  Pallas kernels: 461 us -> 452 us
    all_gather x1, waiting for transfers between devices: 0.02 us -> 5.79 us  [local(): full_gate_up = lax.all_gather(gate_up_weight, 'row', axis=0, tiled=True)]
  transfers between devices with their start and end apart: 8 -> 7, of which waited for: 0 -> 1; matrix products, arithmetic and copies ran while one was open for 11% -> 11% of each run, Pallas kernels for 83% -> 82%
where the time goes in v4:
time: 559 us; the launch traced here: 550 us
  Pallas kernels  452 us (81%)
  matrix products  58.2 us (10%)
  between operations  14.7 us (3%)
  local copies, waits for them, and re-layouts  12.1 us (2%)
  waiting for transfers between devices  7.35 us (1%)
  other arithmetic  5.69 us (1%)
    pallas_call x1, Pallas kernels, norm_back(): pl.pallas_call(functools.partial(back_kernel, ways, lines, steps), out_sh...  95.1 us
    pallas_call x1, Pallas kernels, gather_rest(): pl.pallas_call(functools.partial(gather_kernel, ways, count, seqs, GA), o...  91.1 us
    pallas_call x1, Pallas kernels, branches(): pl.pallas_call(functools.partial(branch_kernel, ways, steps), out_shape=[...  85.2 us
    pallas_call x1, Pallas kernels, gather_first(): pl.pallas_call(functools.partial(gather_kernel, ways, 0, 0, GB), out_shap...  84.8 us
    dot_general x3, matrix products, contract(): lax.dot_general(left, right, (((left_dim,), (right_dim,)), ((), ())), pre...  58.2 us
    pallas_call x1, Pallas kernels, feed_forward(): pl.pallas_call(ffn_kernel, out_shape=[jax.ShapeDtypeStruct((rows, ffn), j...  49.5 us
    pallas_call x1, Pallas kernels, attention(): pl.pallas_call(functools.partial(attention_kernel, heads, first), out_sha...  45.8 us
  transfers between devices with their start and end apart: 7, of which 1 were waited for; matrix products, arithmetic and copies ran while one was open for 11% of the time, Pallas kernels for 82%

profile of v4, /device:TPU:0, one launch (start us, length us, event | category | flops | bytes accessed | tf_op | source)
XLA Modules:
  0.0 549.9 jit_solution(9801800864522603990)
XLA Ops:
  7.2 0.0 all-gather.4.cloned.1.call-start
  7.2 1.2 slice_bitcast_fusion.2
  8.4 2.1 pad_maximum_fusion
  10.5 0.0 all-gather.8.cloned.1.call-start
  10.5 0.7 all-gather.8.cloned.1.call-update
  11.2 0.0 all-gather.6.cloned.1.call-start
  11.3 0.7 all-gather.6.cloned.1.call-update
  12.0 0.0 reduce-scatter.5.cloned.1.call-start
  12.0 0.6 select_maximum_fusion.refs_2_.gain_ref
  12.6 84.8 %gather_first.1 = (bf16[4096,2048]{1,0:T(8,128)(2,1)}, bf16[4096,2048]{1,0:T(8,128)(2,1)}, f32[4096,2]{1,0:T(8,128)}, f32[8,2048]{1,0:T(8,128)}) custom-call(bf16[4096,256]{1,0:T(8,128)(2,1)} %token_ref.3, bf16[4096,256]{1,0:T(8,128)(2,1)} %cot_ref.1, f32[8,256]{1,0:T(8,128)} %select_maximum_fusion.refs_2_.gain_ref), custom_call_target="tpu_custom_call" | custom-call | flops 107374182400 | bytes 33554432 | tf_op jit(solution)/shard_map/gather_first/pallas_call | solution.py:611
  97.5 0.0 all-gather.4.cloned.1.call-done.refs_3_.w_ref.wout_ref
  97.5 91.1 %gather_rest.1 = (bf16[4096,2048]{1,0:T(8,128)(2,1)}, bf16[4096,2048]{1,0:T(8,128)(2,1)}, f32[4096,2]{1,0:T(8,128)}, bf16[4096,256]{1,0:T(8,128)(2,1)}, bf16[4096,768]{1,0:T(8,128)(2,1)}) custom-call(bf16[4096,256]{1,0:T(8,128)(2,1)} %token_ref.3, bf16[4096,256]{1,0:T(8,128)(2,1)} %cot_ref.1, ...), custom_call_target="tpu_custom_call", output_to_operand_aliasing={{0}: (8, {}), {1}: (9, {})} | custom-call | flops 107374182400 | bytes 33554432 | tf_op jit(solution)/shard_map/gather_rest/pallas_call | solution.py:640
  188.7 45.8 %attention.1 = (bf16[4096,256]{1,0:T(8,128)(2,1)}, bf16[4096,768]{1,0:T(8,128)(2,1)}) custom-call(s32[4]{0:T(128)} %start_ref.1, bf16[4096,2048]{1,0:T(8,128)(2,1)} %get-tuple-element.42.x_ref, bf16[4096,2048]{1,0:T(8,128)(2,1)} %get-tuple-element.37.g_ref.grad_ref, ...), custom_call_target="tpu_custom_call", output_to_operand_aliasing={{0}: (6, {}), {1}: (7, {})} | custom-call | flops 20669530112 | bytes 25165824 | tf_op jit(solution)/shard_map/attention/pallas_call | solution.py:277
  234.4 20.1 %convolution_convert_fusion = bf16[2048,768]{1,0:T(8,128)(2,1)} fusion(bf16[4096,2048]{1,0:T(8,128)(2,1)} %get-tuple-element.42.x_ref, bf16[4096,768]{1,0:T(8,128)(2,1)} %get-tuple-element.49.gp_ref), kind=kOutput, calls=%fused_computation | convolution fusion | flops 12886474752 | bytes 26214400 | tf_op jit(solution)/shard_map/dot_general | solution.py:32
  254.6 0.0 reduce-scatter.7.cloned.1.call-start
  254.6 5.8 %all-gather.6.cloned.1.call-done = bf16[2048,2,704]{0,2,1:T(8,128)(2,1)} async-done(((bf16[512,2,704]{0,2,1:T(8,128)(2,1)}), bf16[2048,2,704]{0,2,1:T(8,128)(2,1)}) %all-gather.6.cloned.1.call-update) | async-done | bytes 5767184 | tf_op jit(solution)/shard_map/all_gather | solution.py:1107
  260.4 49.5 %feed_forward.1 = (bf16[4096,704]{1,0:T(8,128)(2,1)}, bf16[4096,704]{1,0:T(8,128)(2,1)}, bf16[4096,704]{1,0:T(8,128)(2,1)}) custom-call(bf16[4096,2048]{1,0:T(8,128)(2,1)} %get-tuple-element.42.x_ref, bf16[4096,2048]{1,0:T(8,128)(2,1)} %get-tuple-element.37.g_ref.grad_ref, bf16[2,704,2048]{2,1,0:T(8,128)(2,1)} %bitcast.30, bf16[704,2048]{1,0:T(8,128)(2,1)} %bitcast.32), custom_call_target="tpu_custom_call" | custom-call | flops 35433480192 | bytes 59506688 | tf_op jit(solution)/shard_map/feed_forward/pallas_call | solution.py:327
  309.9 18.7 %convolution_convert_fusion.2 = bf16[2048,704]{0,1:T(8,128)(2,1)} fusion(bf16[4096,2048]{1,0:T(8,128)(2,1)} %get-tuple-element.42.x_ref, bf16[4096,704]{1,0:T(8,128)(2,1)} %get-tuple-element.44.gg_ref), kind=kOutput, calls=%fused_computation.2 | convolution fusion | flops 11812601856 | bytes 25427968 | tf_op jit(solution)/shard_map/dot_general | solution.py:32
  328.6 0.0 reduce-scatter.9.cloned.1.call-start
  328.7 19.4 %convolution_convert_fusion.1 = bf16[2048,704]{0,1:T(8,128)(2,1)} fusion(bf16[4096,2048]{1,0:T(8,128)(2,1)} %get-tuple-element.42.x_ref, bf16[4096,704]{1,0:T(8,128)(2,1)} %get-tuple-element.45.gu_ref), kind=kOutput, calls=%fused_computation.1 | convolution fusion | flops 11812601856 | bytes 25427968 | tf_op jit(solution)/shard_map/dot_general | solution.py:32
  348.1 0.0 reduce-scatter.11.cloned.1.call-start
  348.2 85.2 %branches.1 = (bf16[4096,256]{1,0:T(8,128)(2,1)}, bf16[960,2048]{1,0:T(8,128)(2,1)}) custom-call(bf16[4096,256]{1,0:T(8,128)(2,1)} %get-tuple-element.46.att_ref, bf16[4096,704]{1,0:T(8,128)(2,1)} %get-tuple-element.47.hidden_ref, bf16[4096,2048]{1,0:T(8,128)(2,1)} %get-tuple-element.37.g_ref.grad_ref, bf16[4096,256]{1,0:T(8,128)(2,1)} %token_ref.3, ...), custom_call_target="tpu_custom_call" | custom-call | flops 111669149696 | bytes 33554432 | tf_op jit(solution)/shard_map/branches/pallas_call | solution.py:844
  433.4 95.1 %norm_back.1 = (f32[4096,256]{1,0:T(8,128)}, f32[8,256]{1,0:T(8,128)}, f32[3,512,256]{2,1,0:T(8,128)}) custom-call(bf16[4096,768]{1,0:T(8,128)(2,1)} %get-tuple-element.49.gp_ref, bf16[4096,704]{1,0:T(8,128)(2,1)} %get-tuple-element.44.gg_ref, bf16[4096,704]{1,0:T(8,128)(2,1)} %get-tuple-element.45.gu_ref, bf16[4096,2048]{1,0:T(8,128)(2,1)} %get-tuple-element.42.x_ref, ...), custom_call_target="tpu_custom_call" | custom-call | flops 73014444032 | bytes 50331648 | tf_op jit(solution)/shard_map/norm_back/pallas_call | solution.py:1035
  528.6 3.0 maximum_convert_fusion
  531.6 1.3 fusion
  533.0 1.0 slice.28
  534.0 1.0 copy.24
  535.0 2.6 slice.29
  537.6 1.3 copy.32
  538.9 2.0 copy.33
  540.9 0.5 copy-done.2
  541.4 1.1 copy.34
  (21 shorter events, 0.2 us)
Async XLA Ops:
  7.2 4.9 copy-start.5
  7.2 4.9 copy-start.4
  7.2 90.3 %all-gather.4.cloned.1.call-start = ((), (), s32[]{:S(2)}) async-start(), calls=%async_computation.4 | async-start | bytes 5242880 | tf_op jit(solution)/shard_map/all_gather | solution.py:1106
  10.5 244.1 %all-gather.8.cloned.1.call-start = ((), (), s32[]{:S(2)}) async-start(), calls=%async_computation.6 | async-start | bytes 3604480 | tf_op jit(solution)/shard_map/all_gather | solution.py:1108
  11.2 249.2 %all-gather.6.cloned.1.call-start = ((), (), s32[]{:S(2)}) async-start(), calls=%async_computation.5 | async-start | bytes 7208960 | tf_op jit(solution)/shard_map/all_gather | solution.py:1107
  12.0 336.2 %reduce-scatter.5.cloned.1.call-start = ((), (), s32[]{:S(2)}) async-start(), calls=%async_computation.7 | async-start | bytes 3932160 | tf_op jit(solution)/shard_map/reduce_scatter | solution.py:1123
  254.6 178.9 %reduce-scatter.7.cloned.1.call-start = ((), (), s32[]{:S(2)}) async-start(), calls=%async_computation.8 | async-start | bytes 3604480 | tf_op jit(solution)/shard_map/reduce_scatter | solution.py:1123
  328.6 200.0 %reduce-scatter.9.cloned.1.call-start = ((), (), s32[]{:S(2)}) async-start(), calls=%async_computation.9 | async-start | bytes 3604480 | tf_op jit(solution)/shard_map/reduce_scatter | solution.py:1123
  348.1 184.9 %reduce-scatter.11.cloned.1.call-start = ((), (), s32[]{:S(2)}) async-start(), calls=%async_computation.10 | async-start | bytes 4915200 | tf_op jit(solution)/shard_map/reduce_scatter | solution.py:1123
  433.4 95.2 %copy-start.3 = (bf16[512,704]{0,1:T(8,128)(2,1)S(1)}, bf16[512,704]{0,1:T(8,128)(2,1)}, u32[]{:S(2)}) copy-start(bf16[512,704]{0,1:T(8,128)(2,1)} %reduce-scatter.7.cloned.1.call-done) | copy-start | bytes 2162692
  528.6 8.9 %copy-start.1 = (bf16[4096,256]{1,0:T(8,128)(2,1)S(1)}, bf16[4096,256]{1,0:T(8,128)(2,1)}, u32[]{:S(2)}) copy-start(bf16[4096,256]{1,0:T(8,128)(2,1)} %get-tuple-element.77) | copy-start | bytes 6291460
  535.0 3.9 copy-start
  538.9 2.5 copy-start.2
Sparse Core Ops, SparseCore 0:
  10.6 83.4 all-gather.3
  95.7 57.6 all-gather.7
  155.0 105.4 all-gather.5
  263.1 58.5 reduce-scatter.4
  328.8 54.4 reduce-scatter.6
  386.0 56.0 reduce-scatter.8
  444.3 72.5 reduce-scatter.10

commit v5 on v4

--- a/solution.py
+++ b/solution.py
@@ -108,7 +108,7 @@
     def part(self, kind):
         return pl.ds(kind * self.width, self.width)
 
-    def begin(self, doc_ref, seq, start, x_ref, g_ref, w_ref):
+    def begin(self, doc_ref, seq, start, x_ref, g_ref, w_ref, arrive=None):
         f32, bf16, width = jnp.float32, jnp.bfloat16, self.width
         docs = doc_ref[pl.ds(seq, 1), :].astype(f32)
         down = jnp.broadcast_to(docs, (128, LEN)).T[:, :1]
@@ -123,6 +123,8 @@
 
         def block(i, _):
             sl = pl.ds(pl.multiple_of(i * QB, QB), QB)
+            if arrive:
+                arrive(i)
             x = x_ref[sl, :]
             q = jnp.dot(x, w_ref[:, :width], preferred_element_type=f32)
             k = jnp.dot(x, w_ref[:, width : 2 * width], preferred_element_type=f32)
@@ -250,15 +252,34 @@
 def attention_kernel(
     heads, first, start_ref, x_ref, g_ref, w_ref, doc_ref, rope_ref, *refs
 ):
-    att_ref, gp_ref = refs[2:4]
+    att_ref, gp_ref, x_scr, g_scr, sem = refs[2:7]
     seq = pl.program_id(0) + first
-    attend = Attention(heads, refs[4:])
+    attend = Attention(heads, refs[7:])
+
+    def fetch(seq, i):
+        here = pl.ds(pl.multiple_of(i * QB, QB), QB)
+        there = pl.ds(pl.multiple_of(seq * LEN + i * QB, QB), QB)
+        return [
+            pltpu.make_async_copy(x_ref.at[there], x_scr.at[here], sem.at[0, i]),
+            pltpu.make_async_copy(g_ref.at[there], g_scr.at[here], sem.at[1, i]),
+        ]
+
+    def fetch_all(seq):
+        for i in range(LEN // QB):
+            for move in fetch(seq, i):
+                move.start()
+
+    def arrive(i):
+        for move in fetch(seq, i):
+            move.wait()
 
     @pl.when(pl.program_id(0) == 0)
     def _():
+        fetch_all(seq)
         fill_tables(rope_ref, attend.tables)
 
-    attend.begin(doc_ref, seq, start_ref[seq], x_ref, g_ref, w_ref)
+    attend.begin(doc_ref, seq, start_ref[seq], x_scr, g_scr, w_ref, arrive)
+    pl.when(pl.program_id(0) + 1 < pl.num_programs(0))(lambda: fetch_all(seq + 1))
 
     def query_block(i, _):
         attend.query_block(i, *attend.bounds(i), att_ref, gp_ref)
@@ -281,8 +302,8 @@
             num_scalar_prefetch=1,
             grid=(count - first,),
             in_specs=[
-                pl.BlockSpec((LEN, D), seq_rows),
-                pl.BlockSpec((LEN, D), seq_rows),
+                pl.BlockSpec(memory_space=pl.ANY),
+                pl.BlockSpec(memory_space=pl.ANY),
                 pl.BlockSpec((D, 4 * width), fixed, pipeline_mode=pl.Buffered(1)),
                 pl.BlockSpec((count, LEN), fixed),
                 pl.BlockSpec((ROT, LEN), fixed),
@@ -293,7 +314,12 @@
                 pl.BlockSpec((LEN, width), seq_rows),
                 pl.BlockSpec((LEN, 3 * width), seq_rows),
             ],
-            scratch_shapes=Attention.scratch(heads),
+            scratch_shapes=[
+                pltpu.VMEM((LEN, D), bf16),
+                pltpu.VMEM((LEN, D), bf16),
+                pltpu.SemaphoreType.DMA((2, LEN // QB)),
+                *Attention.scratch(heads),
+            ],
         ),
         input_output_aliases={6: 0, 7: 1},
         compiler_params=pltpu.CompilerParams(
@@ -311,8 +337,9 @@
 def ffn_kernel(x_ref, g_ref, wgu_ref, wd_ref, hidden_ref, gg_ref, gu_ref):
     f32, bf16 = jnp.float32, jnp.bfloat16
     x = x_ref[...]
-    gate = lax.dot_general(x, wgu_ref[0], NT, preferred_element_type=f32)
-    up = lax.dot_general(x, wgu_ref[1], NT, preferred_element_type=f32)
+    ffn = wd_ref.shape[0]
+    gate = lax.dot_general(x, wgu_ref[:ffn], NT, preferred_element_type=f32)
+    up = lax.dot_general(x, wgu_ref[ffn:], NT, preferred_element_type=f32)
     grad = lax.dot_general(g_ref[...], wd_ref[...], NT, preferred_element_type=f32)
     sigma = jax.nn.sigmoid(gate)
     silu = gate * sigma
@@ -321,8 +348,8 @@
     gu_ref[...] = (grad * silu).astype(bf16)
 
 
-def feed_forward(normed, grad, wgu, wd):
-    rows, ffn = normed.shape[0], wd.shape[0]
+def feed_forward(normed, grad, wffn):
+    rows, ffn = normed.shape[0], wffn.shape[0] // 3
     block = lambda i: (i, 0)
     return pl.pallas_call(
         ffn_kernel,
@@ -331,8 +358,8 @@
         in_specs=[
             pl.BlockSpec((MB, D), block),
             pl.BlockSpec((MB, D), block),
-            pl.BlockSpec((2, ffn, D), lambda i: (0, 0, 0), pipeline_mode=pl.Buffered(1)),
-            pl.BlockSpec((ffn, D), lambda i: (0, 0), pipeline_mode=pl.Buffered(1)),
+            pl.BlockSpec((2 * ffn, D), lambda i: (0, 0), pipeline_mode=pl.Buffered(1)),
+            pl.BlockSpec((ffn, D), lambda i: (2, 0), pipeline_mode=pl.Buffered(1)),
         ],
         out_specs=[pl.BlockSpec((MB, ffn), block)] * 3,
         compiler_params=pltpu.CompilerParams(
@@ -344,7 +371,7 @@
             transcendentals=rows * ffn,
         ),
         name="feed_forward",
-    )(normed, grad, wgu, wd)
+    )(normed, grad, wffn, wffn)
 
 
 def flip(index, bits):
@@ -383,8 +410,9 @@
         (old_normed, old_grad, normed_ref, full_ref, stat_ref, att_ref, gp_ref) = refs[8:15]
         refs = refs[15:]
     else:
-        (token_ref, cot_ref, vector_ref, normed_ref, full_ref, stat_ref, vectors_ref) = refs[:7]
-        refs = refs[7:]
+        (token_ref, cot_ref, vector_ref, gate_ref, down_ref) = refs[:5]
+        (normed_ref, full_ref, stat_ref, vectors_ref, ffn_ref) = refs[5:10]
+        refs = refs[10:]
     (both, load_sem, store_sem, full_sem, send_sem, recv_sem) = refs[:6]
     refs = refs[6:]
     width = token_ref.shape[1]
@@ -512,6 +540,18 @@
     if attended:
         fill_tables(rope_ref, attend.tables)
     else:
+        ffn_scr, ffn_sem = refs[2:4]
+        split = gate_ref.shape[0]
+        moves = [
+            pltpu.make_async_copy(gate_ref, ffn_scr.at[pl.ds(0, split)], ffn_sem.at[0]),
+            pltpu.make_async_copy(down_ref, ffn_scr.at[pl.ds(split, split // 2)], ffn_sem.at[1]),
+        ]
+        for move in moves:
+            move.start()
+        for move in moves:
+            move.wait()
+        laid = pltpu.make_async_copy(ffn_scr, ffn_ref, ffn_sem.at[2])
+        laid.start()
         for k in range(ways - 1):
             vector_copy(k).start()
         for k in range(ways - 1):
@@ -585,6 +625,7 @@
             for move in give(seq):
                 move.wait()
     else:
+        laid.wait()
         for k in range(ways - 1):
             vector_copy(k).wait_send()
 
@@ -602,7 +643,7 @@
     ]
 
 
-def gather_first(tokens, out_grad, vectors, count, ways):
+def gather_first(tokens, out_grad, vectors, gate_up, down, count, ways):
     rows, width = tokens.shape
     bf16, f32 = jnp.bfloat16, jnp.float32
     anywhere = pl.BlockSpec(memory_space=pl.ANY)
@@ -615,10 +656,17 @@
             jax.ShapeDtypeStruct((rows, D), bf16),
             jax.ShapeDtypeStruct((rows, 2), f32),
             jax.ShapeDtypeStruct((8, D), f32),
-        ],
-        in_specs=[anywhere, anywhere, vmem],
-        out_specs=[anywhere, anywhere, vmem, vmem],
-        scratch_shapes=[*gather_scratch(ways, count, width, GB), dma((ways - 1,)), dma((ways - 1,))],
+            jax.ShapeDtypeStruct((3 * down.shape[0], down.shape[1]), bf16),
+        ],
+        in_specs=[anywhere, anywhere, vmem, anywhere, anywhere],
+        out_specs=[anywhere, anywhere, vmem, vmem, anywhere],
+        scratch_shapes=[
+            *gather_scratch(ways, count, width, GB),
+            dma((ways - 1,)),
+            dma((ways - 1,)),
+            pltpu.VMEM((3 * down.shape[0], down.shape[1]), bf16),
+            dma((3,)),
+        ],
         compiler_params=pltpu.CompilerParams(
             collective_id=0, has_side_effects=True, vmem_limit_bytes=63 << 20
         ),
@@ -626,7 +674,7 @@
             flops=100 * count * D * D // ways, bytes_accessed=count * D * 8, transcendentals=0
         ),
         name="gather_first",
-    )(tokens, out_grad, vectors)
+    )(tokens, out_grad, vectors, gate_up, down)
 
 
 def gather_rest(tokens, out_grad, vectors, weights, doc_ids, image_start, stats, normed, grad, ways):
@@ -803,11 +851,10 @@
     def _():
         rows = pl.ds(pl.multiple_of(t * RB, RB), RB)
         att, hidden = att_ref[...], hidden_ref[...]
-        for o in range(ways):
-            cols = pl.ds(pl.multiple_of(flip(me, o) * width, width), width)
-            total = lax.dot_general(att, wout_ref[cols, :], NT, preferred_element_type=f32)
-            total += jnp.dot(hidden, wd_ref[:, cols], preferred_element_type=f32)
-            parts[o, rows, :] = total.astype(bf16)
+        total = jnp.dot(hidden, wd_ref[...], preferred_element_type=f32)
+        total += lax.dot_general(att, wout_ref[...], NT, preferred_element_type=f32)
+        for b in range(ways):
+            parts[flip(me, b), rows, :] = total[:, b * width : (b + 1) * width].astype(bf16)
 
     ring.advance(t, steps, lags)
 
@@ -832,9 +879,9 @@
         ring.finish(s)
 
 
-def branches(att, hidden, grad, tokens, weights, wd, ways):
+def branches(att, hidden, grad, tokens, weights, wffn, ways):
     rows, width = tokens.shape
-    ffn = wd.shape[0]
+    ffn = wffn.shape[0] // 3
     steps = rows // RB
     lag = lags_of(ways)[-1]
     now = lambda t: (jnp.minimum(t, steps - 1), 0)
@@ -854,7 +901,7 @@
             pl.BlockSpec((RB, D), now),
             pl.BlockSpec((RB, width), late),
             pl.BlockSpec((D, width), lambda t: (0, 3), pipeline_mode=once),
-            pl.BlockSpec((ffn, D), fixed, pipeline_mode=once),
+            pl.BlockSpec((ffn, D), lambda t: (2, 0), pipeline_mode=once),
         ],
         out_specs=[
             pl.BlockSpec((RB, width), late),
@@ -875,7 +922,7 @@
             flops=8 * rows * D * (2 * ffn + width), bytes_accessed=4 * rows * D, transcendentals=0
         ),
         name="branches",
-    )(att, hidden, grad, tokens, weights, wd)
+    )(att, hidden, grad, tokens, weights, wffn)
 
 
 def back_kernel(
@@ -939,17 +986,14 @@
     def _():
         rows = pl.ds(pl.multiple_of(t * RB, RB), RB)
         gp, gg, gu = gp_ref[...], gg_ref[...], gu_ref[...]
-        plain = jnp.zeros((RB, 1), f32)
-        cross = jnp.zeros((RB, 1), f32)
-        for o in range(ways):
-            cols = pl.ds(pl.multiple_of(flip(me, o) * width, width), width)
-            total = jnp.dot(gg, wgu_ref[0, :, cols], preferred_element_type=f32)
-            total += jnp.dot(gu, wgu_ref[1, :, cols], preferred_element_type=f32)
-            total += lax.dot_general(gp, w_ref[cols, :], NT, preferred_element_type=f32)
-            parts[o, rows, :] = total.astype(bf16)
-            scaled = x_ref[:, cols].astype(f32) - vectors_ref[1:2, cols]
-            plain += jnp.sum(total * vectors_ref[0:1, cols], axis=1, keepdims=True)
-            cross += jnp.sum(total * scaled, axis=1, keepdims=True)
+        total = jnp.dot(gg, wgu_ref[: gg.shape[1]], preferred_element_type=f32)
+        total += jnp.dot(gu, wgu_ref[gg.shape[1] :], preferred_element_type=f32)
+        total += lax.dot_general(gp, w_ref[...], NT, preferred_element_type=f32)
+        for b in range(ways):
+            parts[flip(me, b), rows, :] = total[:, b * width : (b + 1) * width].astype(bf16)
+        scaled = x_ref[...].astype(f32) - vectors_ref[1:2, :]
+        plain = jnp.sum(total * vectors_ref[0:1, :], axis=1, keepdims=True)
+        cross = jnp.sum(total * scaled, axis=1, keepdims=True)
         lane = lax.broadcasted_iota(jnp.int32, (RB, 128), 1)
         spot = 2 * (t % SUMS)
         pair = jnp.where(lane == spot, plain, jnp.where(lane == spot + 1, cross, 0.0))
@@ -1019,7 +1063,7 @@
 
 
 def norm_back(
-    gp, gg, gu, normed, tokens, cot, stats, weights, wgu, vectors, own, qkv, ways, lines
+    gp, gg, gu, normed, tokens, cot, stats, weights, wffn, vectors, own, qkv, ways, lines
 ):
     rows, width = tokens.shape
     ffn = gg.shape[1]
@@ -1049,7 +1093,7 @@
             pl.BlockSpec((RB, width), late),
             pl.BlockSpec((RB, 2), late),
             pl.BlockSpec((D, 3 * width), fixed, pipeline_mode=once),
-            pl.BlockSpec((2, ffn, D), lambda t: (0, 0, 0), pipeline_mode=once),
+            pl.BlockSpec((2 * ffn, D), fixed, pipeline_mode=once),
             pl.BlockSpec((8, D), fixed),
             pl.BlockSpec((8, width), fixed),
             pl.BlockSpec((slab, 3 * width), now),
@@ -1078,7 +1122,7 @@
             flops=4 * rows * D * (2 * ffn + 3 * width), bytes_accessed=6 * rows * D, transcendentals=0
         ),
         name="norm_back",
-    )(gp, gg, gu, normed, tokens, cot, stats, weights, wgu, vectors, own, qkv)
+    )(gp, gg, gu, normed, tokens, cot, stats, weights, wffn, vectors, own, qkv)
 
 
 def after(value, *others):
@@ -1104,14 +1148,19 @@
 
     own = jnp.concatenate([qkv_weight[:, k] for k in range(3)] + [out_weight], axis=1)
     weights = lax.all_gather(own, "row", axis=0, tiled=True)
-    full_gate_up = lax.all_gather(gate_up_weight, "row", axis=0, tiled=True)
-    full_down = lax.all_gather(down_weight, "row", axis=0, tiled=True)
-    wgu = jnp.transpose(full_gate_up, (1, 2, 0))
-    wd = jnp.transpose(full_down, (1, 0))
     own_vectors = jnp.pad(jnp.stack([norm_gain, norm_bias]), ((0, 6), (0, 0)))
 
     half = block_rows // 2
-    normed, grad, stats, vectors = gather_first(tokens, out_grad, own_vectors, half, ways)
+    normed, grad, stats, vectors, own_ffn = gather_first(
+        tokens,
+        out_grad,
+        own_vectors,
+        jnp.transpose(gate_up_weight, (1, 2, 0)).reshape(-1, D // lines),
+        jnp.transpose(down_weight, (1, 0)),
+        half,
+        ways,
+    )
+    wffn = lax.all_gather(own_ffn, "row", axis=1, tiled=True)
     normed, grad, stats, *earlier = gather_rest(
         tokens, out_grad, vectors, weights, doc_ids, image_start, stats, normed, grad, ways
     )
@@ -1126,13 +1175,13 @@
         return contract(left, right, 0, 0).astype(bf16)
 
     grad_qkv = weight_grad(normed, grad_projected)
-    hidden, grad_gate, grad_up = feed_forward(after(normed, grad_qkv), grad, wgu, wd)
+    hidden, grad_gate, grad_up = feed_forward(after(normed, grad_qkv), grad, wffn)
     weight_gate = weight_grad(normed, grad_gate)
     weight_up = weight_grad(normed, after(grad_up, weight_gate))
     qkv_sum = weight_sum(grad_qkv)
     gate_sum = weight_sum(weight_gate)
     outputs, weight_rest = branches(
-        after(attended, weight_up, qkv_sum), hidden, grad, tokens, weights, wd, ways
+        after(attended, weight_up, qkv_sum), hidden, grad, tokens, weights, wffn, ways
     )
     input_grad, vector_grads, qkv_sum = norm_back(
         after(grad_projected, outputs, gate_sum),
@@ -1143,7 +1192,7 @@
         out_grad,
         stats,
         weights,
-        wgu,
+        wffn,
         vectors,
         own_vectors,
         qkv_sum,
@@ -1152,8 +1201,8 @@
     )
     qkv_sum = jnp.transpose(qkv_sum, (1, 0, 2))
     up_sum = after(weight_sum(weight_up), input_grad)
-    rest = weight_sum(jnp.transpose(weight_rest, (1, 0))).astype(f32)
-    down_sum, out_sum = rest[:, :-width], rest[:, -width:]
+    rest = weight_sum(jnp.transpose(weight_rest, (1, 0)))
+    down_sum, out_sum = rest[:, :-width].astype(f32), rest[:, -width:].astype(f32)
     gate_up_sum = jnp.stack([gate_sum.astype(f32), up_sum.astype(f32)], axis=1)
     return (
         outputs,

time: 559 us -> 549 us (0.982)
  waiting for transfers between devices: 7.35 us -> 1.64 us
    pallas_call x1, Pallas kernels: 95.1 us -> 101 us  [norm_back(): pl.pallas_call(functools.partial(back_kernel, ways, lines, steps), out_sh...]
  transfers between devices with their start and end apart: 7 -> 6, of which waited for: 1 -> 1; matrix products, arithmetic and copies ran while one was open for 11% -> 12% of each run, Pallas kernels for 82% -> 83%
where the time goes in v5:
time: 549 us; the launch traced here: 545 us
  Pallas kernels  453 us (83%)
  matrix products  57.9 us (11%)
  between operations  14.5 us (3%)
  other arithmetic  9.24 us (2%)
  local copies, waits for them, and re-layouts  8.53 us (2%)
    pallas_call x1, Pallas kernels, norm_back(): pl.pallas_call(functools.partial(back_kernel, ways, lines, steps), out_sh...  101 us
    pallas_call x1, Pallas kernels, gather_rest(): pl.pallas_call(functools.partial(gather_kernel, ways, count, seqs, GA), o...  91 us
    pallas_call x1, Pallas kernels, branches(): pl.pallas_call(functools.partial(branch_kernel, ways, steps), out_shape=[...  85.2 us
    pallas_call x1, Pallas kernels, gather_first(): pl.pallas_call(functools.partial(gather_kernel, ways, 0, 0, GB), out_shap...  84.8 us
    dot_general x3, matrix products, contract(): lax.dot_general(left, right, (((left_dim,), (right_dim,)), ((), ())), pre...  57.9 us
    pallas_call x1, Pallas kernels, feed_forward(): pl.pallas_call(ffn_kernel, out_shape=[jax.ShapeDtypeStruct((rows, ffn), j...  49.8 us
    pallas_call x1, Pallas kernels, attention(): pl.pallas_call(functools.partial(attention_kernel, heads, first), out_sha...  41.2 us
  transfers between devices with their start and end apart: 6, of which 1 were waited for; matrix products, arithmetic and copies ran while one was open for 12% of the time, Pallas kernels for 83%

profile of v5, /device:TPU:0, one launch (start us, length us, event | category | flops | bytes accessed | tf_op | source)
XLA Modules:
  0.0 545.3 jit_solution(13081718307448136931)
XLA Ops:
  7.2 0.0 all-gather.3.cloned.1.call-start
  7.2 1.2 slice_bitcast_fusion.2
  8.4 2.1 pad_maximum_fusion
  10.5 0.0 all-gather.5.cloned.1.call-start
  10.6 0.6 select_maximum_fusion.refs_2_.gain_ref
  11.2 84.8 %gather_first.1 = (bf16[4096,2048]{1,0:T(8,128)(2,1)}, bf16[4096,2048]{1,0:T(8,128)(2,1)}, f32[4096,2]{1,0:T(8,128)}, f32[8,2048]{1,0:T(8,128)}, bf16[2112,512]{1,0:T(8,128)(2,1)}) custom-call(bf16[4096,256]{1,0:T(8,128)(2,1)} %token_ref.3, bf16[4096,256]{1,0:T(8,128)(2,1)} %cot_ref.1, f32[8,256]{1,0:T(8,128)} %select_maximum_fusion.refs_2_.gain_ref, ...), custom_call_target="tpu_custom_call" | custom-call | flops 107374182400 | bytes 33554432 | tf_op jit(solution)/shard_map/gather_first/pallas_call | solution.py:652
  96.0 0.0 all-gather.5.cloned.1.call-update
  96.0 0.2 reduce-scatter.5.cloned.1.call-start
  96.2 0.0 all-gather.3.cloned.1.call-done.refs_3_.w_ref.wout_ref
  96.3 91.0 %gather_rest.1 = (bf16[4096,2048]{1,0:T(8,128)(2,1)}, bf16[4096,2048]{1,0:T(8,128)(2,1)}, f32[4096,2]{1,0:T(8,128)}, bf16[4096,256]{1,0:T(8,128)(2,1)}, bf16[4096,768]{1,0:T(8,128)(2,1)}) custom-call(bf16[4096,256]{1,0:T(8,128)(2,1)} %token_ref.3, bf16[4096,256]{1,0:T(8,128)(2,1)} %cot_ref.1, ...), custom_call_target="tpu_custom_call", output_to_operand_aliasing={{0}: (8, {}), {1}: (9, {})} | custom-call | flops 107374182400 | bytes 33554432 | tf_op jit(solution)/shard_map/gather_rest/pallas_call | solution.py:688
  187.3 41.2 %attention.1 = (bf16[4096,256]{1,0:T(8,128)(2,1)}, bf16[4096,768]{1,0:T(8,128)(2,1)}) custom-call(s32[4]{0:T(128)} %start_ref.1, bf16[4096,2048]{1,0:T(8,128)(2,1)} %get-tuple-element.43.x_ref, bf16[4096,2048]{1,0:T(8,128)(2,1)} %get-tuple-element.38.g_ref.grad_ref, ...), custom_call_target="tpu_custom_call", output_to_operand_aliasing={{0}: (6, {}), {1}: (7, {})} | custom-call | flops 20669530112 | bytes 25165824 | tf_op jit(solution)/shard_map/attention/pallas_call | solution.py:298
  228.5 20.4 %convolution_convert_fusion = bf16[2048,768]{1,0:T(8,128)(2,1)} fusion(bf16[4096,2048]{1,0:T(8,128)(2,1)} %get-tuple-element.43.x_ref, bf16[4096,768]{1,0:T(8,128)(2,1)} %get-tuple-element.51.gp_ref), kind=kOutput, calls=%fused_computation | convolution fusion | flops 12886474752 | bytes 26214400 | tf_op jit(solution)/shard_map/dot_general | solution.py:32
  248.9 0.0 reduce-scatter.7.cloned.1.call-start
  248.9 1.5 all-gather.5.cloned.1.call-done.wgu_ref.wd_ref
  250.4 49.8 %feed_forward.1 = (bf16[4096,704]{1,0:T(8,128)(2,1)}, bf16[4096,704]{1,0:T(8,128)(2,1)}, bf16[4096,704]{1,0:T(8,128)(2,1)}) custom-call(bf16[4096,2048]{1,0:T(8,128)(2,1)} %get-tuple-element.43.x_ref, bf16[4096,2048]{1,0:T(8,128)(2,1)} %get-tuple-element.38.g_ref.grad_ref, bf16[2112,2048]{1,0:T(8,128)(2,1)} %all-gather.5.cloned.1.call-done.wgu_ref.wd_ref, ...), custom_call_target="tpu_custom_call" | custom-call | flops 35433480192 | bytes 59506688 | tf_op jit(solution)/shard_map/feed_forward/pallas_call | solution.py:354
  300.2 18.7 %convolution_convert_fusion.2 = bf16[2048,704]{0,1:T(8,128)(2,1)} fusion(bf16[4096,2048]{1,0:T(8,128)(2,1)} %get-tuple-element.43.x_ref, bf16[4096,704]{1,0:T(8,128)(2,1)} %get-tuple-element.46.gg_ref), kind=kOutput, calls=%fused_computation.2 | convolution fusion | flops 11812601856 | bytes 25427968 | tf_op jit(solution)/shard_map/dot_general | solution.py:32
  318.9 0.0 reduce-scatter.9.cloned.1.call-start
  319.0 18.8 %convolution_convert_fusion.1 = bf16[2048,704]{0,1:T(8,128)(2,1)} fusion(bf16[4096,2048]{1,0:T(8,128)(2,1)} %get-tuple-element.43.x_ref, bf16[4096,704]{1,0:T(8,128)(2,1)} %get-tuple-element.47.gu_ref), kind=kOutput, calls=%fused_computation.1 | convolution fusion | flops 11812601856 | bytes 25427968 | tf_op jit(solution)/shard_map/dot_general | solution.py:32
  337.8 0.0 reduce-scatter.11.cloned.1.call-start
  337.9 85.2 %branches.1 = (bf16[4096,256]{1,0:T(8,128)(2,1)}, bf16[960,2048]{1,0:T(8,128)(2,1)}) custom-call(bf16[4096,256]{1,0:T(8,128)(2,1)} %get-tuple-element.48.att_ref, bf16[4096,704]{1,0:T(8,128)(2,1)} %get-tuple-element.49.hidden_ref, bf16[4096,2048]{1,0:T(8,128)(2,1)} %get-tuple-element.38.g_ref.grad_ref, bf16[4096,256]{1,0:T(8,128)(2,1)} %token_ref.3, ...), custom_call_target="tpu_custom_call" | custom-call | flops 111669149696 | bytes 33554432 | tf_op jit(solution)/shard_map/branches/pallas_call | solution.py:891
  423.1 0.0 reduce-scatter.7.cloned.1.call-done
  423.1 101.1 %norm_back.1 = (f32[4096,256]{1,0:T(8,128)}, f32[8,256]{1,0:T(8,128)}, f32[3,512,256]{2,1,0:T(8,128)}) custom-call(bf16[4096,768]{1,0:T(8,128)(2,1)} %get-tuple-element.51.gp_ref, bf16[4096,704]{1,0:T(8,128)(2,1)} %get-tuple-element.46.gg_ref, bf16[4096,704]{1,0:T(8,128)(2,1)} %get-tuple-element.47.gu_ref, bf16[4096,2048]{1,0:T(8,128)(2,1)} %get-tuple-element.43.x_ref, ...), custom_call_target="tpu_custom_call" | custom-call | flops 73014444032 | bytes 50331648 | tf_op jit(solution)/shard_map/norm_back/pallas_call | solution.py:1079
  524.3 0.0 reduce-scatter.9.cloned.1.call-done
  524.3 3.0 maximum_convert_fusion
  527.3 1.3 fusion
  528.7 1.0 slice_convert_fusion.1
  529.7 1.0 copy.24
  530.7 2.6 slice_convert_fusion
  533.2 1.3 copy.32
  534.6 2.0 copy.33
  536.6 0.5 copy-done.2
  537.1 1.1 copy.34
  (18 shorter events, 0.1 us)
Async XLA Ops:
  7.2 3.4 copy-start.5
  7.2 3.4 copy-start.4
  7.2 89.1 %all-gather.3.cloned.1.call-start = ((), (), s32[]{:S(2)}) async-start(), calls=%async_computation.4 | async-start | bytes 5242880 | tf_op jit(solution)/shard_map/all_gather | solution.py:1150
  10.5 239.9 %all-gather.5.cloned.1.call-start = ((), (), s32[]{:S(2)}) async-start(), calls=%async_computation.5 | async-start | bytes 10813440 | tf_op jit(solution)/shard_map/all_gather | solution.py:1163
  96.0 241.8 %reduce-scatter.5.cloned.1.call-start = ((), (), s32[]{:S(2)}) async-start(), calls=%async_computation.6 | async-start | bytes 3932160 | tf_op jit(solution)/shard_map/reduce_scatter | solution.py:1172
  248.9 174.2 %reduce-scatter.7.cloned.1.call-start = ((), (), s32[]{:S(2)}) async-start(), calls=%async_computation.7 | async-start | bytes 3604480 | tf_op jit(solution)/shard_map/reduce_scatter | solution.py:1172
  318.9 205.3 %reduce-scatter.9.cloned.1.call-start = ((), (), s32[]{:S(2)}) async-start(), calls=%async_computation.8 | async-start | bytes 3604480 | tf_op jit(solution)/shard_map/reduce_scatter | solution.py:1172
  337.8 190.8 %reduce-scatter.11.cloned.1.call-start = ((), (), s32[]{:S(2)}) async-start(), calls=%async_computation.9 | async-start | bytes 4915200 | tf_op jit(solution)/shard_map/reduce_scatter | solution.py:1172
  423.1 101.2 %copy-start.3 = (bf16[512,704]{0,1:T(8,128)(2,1)S(1)}, bf16[512,704]{0,1:T(8,128)(2,1)}, u32[]{:S(2)}) copy-start(bf16[512,704]{0,1:T(8,128)(2,1)} %reduce-scatter.7.cloned.1.call-done) | copy-start | bytes 2162692
  524.3 9.0 %copy-start.1 = (bf16[4096,256]{1,0:T(8,128)(2,1)S(1)}, bf16[4096,256]{1,0:T(8,128)(2,1)}, u32[]{:S(2)}) copy-start(bf16[4096,256]{1,0:T(8,128)(2,1)} %get-tuple-element.79) | copy-start | bytes 6291460
  530.7 3.9 copy-start
  534.5 2.5 copy-start.2
Sparse Core Ops, SparseCore 0:
  10.6 83.4 all-gather.2
  96.1 154.2 all-gather.4
  253.3 63.2 reduce-scatter.4
  319.1 61.9 reduce-scatter.6
  383.8 56.0 reduce-scatter.8
  442.1 72.5 reduce-scatter.10

commit v6 on v5

--- a/solution.py
+++ b/solution.py
@@ -126,10 +126,10 @@
             if arrive:
                 arrive(i)
             x = x_ref[sl, :]
-            q = jnp.dot(x, w_ref[:, :width], preferred_element_type=f32)
-            k = jnp.dot(x, w_ref[:, width : 2 * width], preferred_element_type=f32)
-            v = jnp.dot(x, w_ref[:, 2 * width : 3 * width], preferred_element_type=f32)
-            g = jnp.dot(g_ref[sl, :], w_ref[:, 3 * width :], preferred_element_type=f32)
+            q = jnp.dot(x, w_ref[0], preferred_element_type=f32)
+            k = jnp.dot(x, w_ref[1], preferred_element_type=f32)
+            v = jnp.dot(x, w_ref[2], preferred_element_type=f32)
+            g = jnp.dot(g_ref[sl, :], w_ref[3], preferred_element_type=f32)
             q = turn(q, self.tables, sl, 1.0).astype(bf16).astype(f32) * HD**-0.5
             k = turn(k, self.tables, sl, 1.0).astype(bf16)
             self.data[sl, self.part(0)] = q.astype(bf16)
@@ -290,7 +290,7 @@
 
 
 def attention(first, normed, grad, weights, image_start, doc_ids, earlier):
-    rows, width = normed.shape[0], weights.shape[1] // 4
+    rows, width = normed.shape[0], weights.shape[2]
     count, heads = rows // LEN, width // HD
     bf16 = jnp.bfloat16
     seq_rows = lambda s, *_: (s + first, 0)
@@ -304,7 +304,7 @@
             in_specs=[
                 pl.BlockSpec(memory_space=pl.ANY),
                 pl.BlockSpec(memory_space=pl.ANY),
-                pl.BlockSpec((D, 4 * width), fixed, pipeline_mode=pl.Buffered(1)),
+                pl.BlockSpec((4, D, width), lambda s, *_: (0, 0, 0), pipeline_mode=pl.Buffered(1)),
                 pl.BlockSpec((count, LEN), fixed),
                 pl.BlockSpec((ROT, LEN), fixed),
                 pl.BlockSpec(memory_space=pl.ANY),
@@ -900,7 +900,7 @@
             pl.BlockSpec((RB, ffn), now),
             pl.BlockSpec((RB, D), now),
             pl.BlockSpec((RB, width), late),
-            pl.BlockSpec((D, width), lambda t: (0, 3), pipeline_mode=once),
+            pl.BlockSpec((None, D, width), lambda t: (3, 0, 0), pipeline_mode=once),
             pl.BlockSpec((ffn, D), lambda t: (2, 0), pipeline_mode=once),
         ],
         out_specs=[
@@ -988,7 +988,9 @@
         gp, gg, gu = gp_ref[...], gg_ref[...], gu_ref[...]
         total = jnp.dot(gg, wgu_ref[: gg.shape[1]], preferred_element_type=f32)
         total += jnp.dot(gu, wgu_ref[gg.shape[1] :], preferred_element_type=f32)
-        total += lax.dot_general(gp, w_ref[...], NT, preferred_element_type=f32)
+        for kind in range(3):
+            part = gp[:, kind * width : (kind + 1) * width]
+            total += lax.dot_general(part, w_ref[kind], NT, preferred_element_type=f32)
         for b in range(ways):
             parts[flip(me, b), rows, :] = total[:, b * width : (b + 1) * width].astype(bf16)
         scaled = x_ref[...].astype(f32) - vectors_ref[1:2, :]
@@ -1092,7 +1094,7 @@
             pl.BlockSpec((RB, width), late),
             pl.BlockSpec((RB, width), late),
             pl.BlockSpec((RB, 2), late),
-            pl.BlockSpec((D, 3 * width), fixed, pipeline_mode=once),
+            pl.BlockSpec((3, D, width), lambda t: (0, 0, 0), pipeline_mode=once),
             pl.BlockSpec((2 * ffn, D), fixed, pipeline_mode=once),
             pl.BlockSpec((8, D), fixed),
             pl.BlockSpec((8, width), fixed),
@@ -1146,8 +1148,8 @@
     ways = D // width
     lines = D // qkv_weight.shape[0]
 
-    own = jnp.concatenate([qkv_weight[:, k] for k in range(3)] + [out_weight], axis=1)
-    weights = lax.all_gather(own, "row", axis=0, tiled=True)
+    own = jnp.concatenate([jnp.transpose(qkv_weight, (1, 0, 2)), out_weight[None]], axis=0)
+    weights = lax.all_gather(own, "row", axis=1, tiled=True)
     own_vectors = jnp.pad(jnp.stack([norm_gain, norm_bias]), ((0, 6), (0, 0)))
 
     half = block_rows // 2

time: 549 us -> 548 us (level)
  no operation moved by 1% of the time
where the time goes in v6:
time: 548 us; the launch traced here: 544 us
  Pallas kernels  453 us (83%)
  matrix products  57.9 us (11%)
  between operations  14.4 us (3%)
  other arithmetic  10.2 us (2%)
  local copies, waits for them, and re-layouts  6.83 us (1%)
    pallas_call x1, Pallas kernels, norm_back(): pl.pallas_call(functools.partial(back_kernel, ways, lines, steps), out_sh...  101 us
    pallas_call x1, Pallas kernels, gather_rest(): pl.pallas_call(functools.partial(gather_kernel, ways, count, seqs, GA), o...  91 us
    pallas_call x1, Pallas kernels, branches(): pl.pallas_call(functools.partial(branch_kernel, ways, steps), out_shape=[...  85.2 us
    pallas_call x1, Pallas kernels, gather_first(): pl.pallas_call(functools.partial(gather_kernel, ways, 0, 0, GB), out_shap...  84.8 us
    dot_general x3, matrix products, contract(): lax.dot_general(left, right, (((left_dim,), (right_dim,)), ((), ())), pre...  57.9 us
    pallas_call x1, Pallas kernels, feed_forward(): pl.pallas_call(ffn_kernel, out_shape=[jax.ShapeDtypeStruct((rows, ffn), j...  49.8 us
    pallas_call x1, Pallas kernels, attention(): pl.pallas_call(functools.partial(attention_kernel, heads, first), out_sha...  42 us
  transfers between devices with their start and end apart: 6, of which 1 were waited for; matrix products, arithmetic and copies ran while one was open for 12% of the time, Pallas kernels for 83%

profile of v6, /device:TPU:0, one launch (start us, length us, event | category | flops | bytes accessed | tf_op | source)
XLA Modules:
  0.0 543.9 jit_solution(530654514892269665)
XLA Ops:
  7.2 0.0 all-gather.3.cloned.1.call-start
  7.2 2.3 pad_maximum_fusion
  9.5 0.0 all-gather.5.cloned.1.call-start
  9.6 1.3 select_maximum_fusion.refs_2_.gain_ref
  10.9 84.8 %gather_first.1 = (bf16[4096,2048]{1,0:T(8,128)(2,1)}, bf16[4096,2048]{1,0:T(8,128)(2,1)}, f32[4096,2]{1,0:T(8,128)}, f32[8,2048]{1,0:T(8,128)}, bf16[2112,512]{1,0:T(8,128)(2,1)}) custom-call(bf16[4096,256]{1,0:T(8,128)(2,1)} %token_ref.3, bf16[4096,256]{1,0:T(8,128)(2,1)} %cot_ref.1, f32[8,256]{1,0:T(8,128)} %select_maximum_fusion.refs_2_.gain_ref, ...), custom_call_target="tpu_custom_call" | custom-call | flops 107374182400 | bytes 33554432 | tf_op jit(solution)/shard_map/gather_first/pallas_call | solution.py:652
  95.7 0.0 all-gather.5.cloned.1.call-update
  95.7 0.2 reduce-scatter.5.cloned.1.call-start
  95.9 0.0 all-gather.3.cloned.1.call-done.refs_3_.w_ref.wout_ref
  96.0 91.0 %gather_rest.1 = (bf16[4096,2048]{1,0:T(8,128)(2,1)}, bf16[4096,2048]{1,0:T(8,128)(2,1)}, f32[4096,2]{1,0:T(8,128)}, bf16[4096,256]{1,0:T(8,128)(2,1)}, bf16[4096,768]{1,0:T(8,128)(2,1)}) custom-call(bf16[4096,256]{1,0:T(8,128)(2,1)} %token_ref.3, bf16[4096,256]{1,0:T(8,128)(2,1)} %cot_ref.1, ...), custom_call_target="tpu_custom_call", output_to_operand_aliasing={{0}: (8, {}), {1}: (9, {})} | custom-call | flops 107374182400 | bytes 33554432 | tf_op jit(solution)/shard_map/gather_rest/pallas_call | solution.py:688
  187.0 42.0 %attention.1 = (bf16[4096,256]{1,0:T(8,128)(2,1)}, bf16[4096,768]{1,0:T(8,128)(2,1)}) custom-call(s32[4]{0:T(128)} %start_ref.1, bf16[4096,2048]{1,0:T(8,128)(2,1)} %get-tuple-element.43.x_ref, bf16[4096,2048]{1,0:T(8,128)(2,1)} %get-tuple-element.38.g_ref.grad_ref, ...), custom_call_target="tpu_custom_call", output_to_operand_aliasing={{0}: (6, {}), {1}: (7, {})} | custom-call | flops 20669530112 | bytes 25165824 | tf_op jit(solution)/shard_map/attention/pallas_call | solution.py:298
  229.0 20.4 %convolution_convert_fusion = bf16[2048,768]{1,0:T(8,128)(2,1)} fusion(bf16[4096,2048]{1,0:T(8,128)(2,1)} %get-tuple-element.43.x_ref, bf16[4096,768]{1,0:T(8,128)(2,1)} %get-tuple-element.51.gp_ref), kind=kOutput, calls=%fused_computation | convolution fusion | flops 12886474752 | bytes 26214400 | tf_op jit(solution)/shard_map/dot_general | solution.py:32
  249.3 0.0 reduce-scatter.7.cloned.1.call-start
  249.4 0.7 all-gather.5.cloned.1.call-done.wgu_ref.wd_ref
  250.1 49.8 %feed_forward.1 = (bf16[4096,704]{1,0:T(8,128)(2,1)}, bf16[4096,704]{1,0:T(8,128)(2,1)}, bf16[4096,704]{1,0:T(8,128)(2,1)}) custom-call(bf16[4096,2048]{1,0:T(8,128)(2,1)} %get-tuple-element.43.x_ref, bf16[4096,2048]{1,0:T(8,128)(2,1)} %get-tuple-element.38.g_ref.grad_ref, bf16[2112,2048]{1,0:T(8,128)(2,1)} %all-gather.5.cloned.1.call-done.wgu_ref.wd_ref, ...), custom_call_target="tpu_custom_call" | custom-call | flops 35433480192 | bytes 59506688 | tf_op jit(solution)/shard_map/feed_forward/pallas_call | solution.py:354
  299.9 18.7 %convolution_convert_fusion.2 = bf16[2048,704]{0,1:T(8,128)(2,1)} fusion(bf16[4096,2048]{1,0:T(8,128)(2,1)} %get-tuple-element.43.x_ref, bf16[4096,704]{1,0:T(8,128)(2,1)} %get-tuple-element.46.gg_ref), kind=kOutput, calls=%fused_computation.2 | convolution fusion | flops 11812601856 | bytes 25427968 | tf_op jit(solution)/shard_map/dot_general | solution.py:32
  318.6 0.0 reduce-scatter.9.cloned.1.call-start
  318.7 18.8 %convolution_convert_fusion.1 = bf16[2048,704]{0,1:T(8,128)(2,1)} fusion(bf16[4096,2048]{1,0:T(8,128)(2,1)} %get-tuple-element.43.x_ref, bf16[4096,704]{1,0:T(8,128)(2,1)} %get-tuple-element.47.gu_ref), kind=kOutput, calls=%fused_computation.1 | convolution fusion | flops 11812601856 | bytes 25427968 | tf_op jit(solution)/shard_map/dot_general | solution.py:32
  337.5 0.0 reduce-scatter.9.cloned.1.call-update
  337.6 0.0 reduce-scatter.11.cloned.1.call-start
  337.6 85.2 %branches.1 = (bf16[4096,256]{1,0:T(8,128)(2,1)}, bf16[960,2048]{1,0:T(8,128)(2,1)}) custom-call(bf16[4096,256]{1,0:T(8,128)(2,1)} %get-tuple-element.48.att_ref, bf16[4096,704]{1,0:T(8,128)(2,1)} %get-tuple-element.49.hidden_ref, bf16[4096,2048]{1,0:T(8,128)(2,1)} %get-tuple-element.38.g_ref.grad_ref, bf16[4096,256]{1,0:T(8,128)(2,1)} %token_ref.3, ...), custom_call_target="tpu_custom_call" | custom-call | flops 111669149696 | bytes 33554432 | tf_op jit(solution)/shard_map/branches/pallas_call | solution.py:891
  422.8 0.0 reduce-scatter.11.cloned.1.call-update
  422.8 0.0 reduce-scatter.7.cloned.1.call-done
  422.9 100.5 %norm_back.1 = (f32[4096,256]{1,0:T(8,128)}, f32[8,256]{1,0:T(8,128)}, f32[3,512,256]{2,1,0:T(8,128)}) custom-call(bf16[4096,768]{1,0:T(8,128)(2,1)} %get-tuple-element.51.gp_ref, bf16[4096,704]{1,0:T(8,128)(2,1)} %get-tuple-element.46.gg_ref, bf16[4096,704]{1,0:T(8,128)(2,1)} %get-tuple-element.47.gu_ref, bf16[4096,2048]{1,0:T(8,128)(2,1)} %get-tuple-element.43.x_ref, ...), custom_call_target="tpu_custom_call" | custom-call | flops 73014444032 | bytes 50331648 | tf_op jit(solution)/shard_map/norm_back/pallas_call | solution.py:1081
  523.4 0.0 reduce-scatter.9.cloned.1.call-done
  523.4 3.0 maximum_convert_fusion
  526.5 1.3 fusion
  527.8 1.0 slice_convert_fusion.1
  528.8 1.0 copy.24
  529.8 2.6 slice_convert_fusion
  532.4 1.3 copy.32
  533.7 2.0 copy.33
  535.7 1.1 copy.34
  (13 shorter events, 0.1 us)
Async XLA Ops:
  7.2 88.8 %all-gather.3.cloned.1.call-start = ((), (), s32[]{:S(2)}) async-start(), calls=%async_computation.4 | async-start | bytes 5242880 | tf_op jit(solution)/shard_map/all_gather | solution.py:1152
  9.5 240.6 %all-gather.5.cloned.1.call-start = ((), (), s32[]{:S(2)}) async-start(), calls=%async_computation.5 | async-start | bytes 10813440 | tf_op jit(solution)/shard_map/all_gather | solution.py:1165
  95.7 241.8 %reduce-scatter.5.cloned.1.call-start = ((), (), s32[]{:S(2)}) async-start(), calls=%async_computation.6 | async-start | bytes 3932160 | tf_op jit(solution)/shard_map/reduce_scatter | solution.py:1174
  249.3 173.5 %reduce-scatter.7.cloned.1.call-start = ((), (), s32[]{:S(2)}) async-start(), calls=%async_computation.7 | async-start | bytes 3604480 | tf_op jit(solution)/shard_map/reduce_scatter | solution.py:1174
  318.6 204.8 %reduce-scatter.9.cloned.1.call-start = ((), (), s32[]{:S(2)}) async-start(), calls=%async_computation.8 | async-start | bytes 3604480 | tf_op jit(solution)/shard_map/reduce_scatter | solution.py:1174
  337.6 190.2 %reduce-scatter.11.cloned.1.call-start = ((), (), s32[]{:S(2)}) async-start(), calls=%async_computation.9 | async-start | bytes 4915200 | tf_op jit(solution)/shard_map/reduce_scatter | solution.py:1174
  422.8 100.6 %copy-start.3 = (bf16[512,704]{0,1:T(8,128)(2,1)S(1)}, bf16[512,704]{0,1:T(8,128)(2,1)}, u32[]{:S(2)}) copy-start(bf16[512,704]{0,1:T(8,128)(2,1)} %reduce-scatter.7.cloned.1.call-done) | copy-start | bytes 2162692
  523.4 9.0 %copy-start.1 = (bf16[4096,256]{1,0:T(8,128)(2,1)S(1)}, bf16[4096,256]{1,0:T(8,128)(2,1)}, u32[]{:S(2)}) copy-start(bf16[4096,256]{1,0:T(8,128)(2,1)} %get-tuple-element.76) | copy-start | bytes 6291460
  529.8 3.9 copy-start
  532.4 3.3 copy-start.2
Sparse Core Ops, SparseCore 0:
  10.1 83.4 all-gather.2
  95.8 154.2 all-gather.4
  253.0 62.2 reduce-scatter.4
  318.8 60.9 reduce-scatter.6
  382.5 56.0 reduce-scatter.8
  440.8 72.5 reduce-scatter.10
